TPU v7x, 512 devices: a whole 4x4x16 slice. The times are simulated.
512 devices in a mesh: date: 16 (over x, y), col: 32 (over z, core).
Axes of the slice: x: 4, y: 4, z: 16, core: 2. Of those that a mesh axis runs over, the one named last changes fastest.
Arguments:
- slc_stack: bfloat16 [2, 192, 40, 20480], P(None, 'date', None, 'col'), may hold values from -60 to 60
- offsets: int32 [192, 2], replicated, may hold values from -4 to 4
- kernels: float32 [192, 2, 8], replicated, may hold values from -2.5 to 2.5
- partner: int32 [576], P('date'), may hold values from 1 to 191, as said below
- inverse: bfloat16 [191, 576], replicated, may hold values from -3.5 to 3.5
- rate_weights: float32 [191], replicated, may hold values from -0.4375 to 0.4375
- owners: int32 [32, 256, 1], P('col', 'date'), may hold values from 0 to 31; in each aligned block of 16 rows (0 to 15, 16 to 31, ..., all dimensions but the last counted through in order) at most 2 rows name the same one
- map_cell: int32 [32, 256], P('col', 'date'), may hold values from 0 to 127
Outputs:
- geocoded: float32 [32, 128, 192], P('col', 'date')
Inputs may be any that keep to these rules, and one draw needn't show every extreme that they name: partner[k] differs from k // 3 by 1 to 6 dates; it is the later date where that lies in the stack, else the earlier one; the 3 partners of one date are distinct, and one of them is 1 date away. `owners`: within the rows of one device, no tile is named more than 2 times.
All inputs are finite; a program needn't handle non-finite values.
Results may differ from a plain program's by a relative error of at most 0.0075.
Values may be sent and summed in bfloat16 or wider, within the bound.
No kernel may reach another device: no remote copies, remote signals or barrier semaphores. Data moves between devices by JAX's collectives and lax.ppermute only.
A program may use at most 64 MiB of HBM per device.

v0:
```python
import jax
import jax.numpy as jnp
from jax import lax
from jax.sharding import PartitionSpec as P

PER_DATE = 3
SPAN = 6
ROW_BLOCK = 20
TAPS = 8
LOOK_AZ = 5
LOOK_RG = 20
TILE_DEV = 8
HALO = 8


def extended(cells, sides, width):
    for axis, dim in sides:
        count = lax.axis_size(axis)
        ends = count - 1
        head = lax.slice_in_dim(cells, 0, width, axis=dim)
        tail = lax.slice_in_dim(cells, cells.shape[dim] - width, cells.shape[dim], axis=dim)
        cells = jnp.concatenate(
            [
                lax.ppermute(tail, axis, [(i, (i + 1) % count) for i in range(ends)]),
                cells,
                lax.ppermute(head, axis, [((i + 1) % count, i) for i in range(ends)]),
            ],
            axis=dim,
        )
    return cells


def from_behind(shard, axis, by):
    length = lax.axis_size(axis)
    pairs = [(i, i + by) for i in range(length) if 0 <= i + by < length]
    return lax.ppermute(shard, axis, pairs)


def look_mean(values_field):
    dims_shape = values_field.shape
    split_field = values_field.reshape(
        dims_shape[:-2] + (dims_shape[-2] // LOOK_AZ, LOOK_AZ, dims_shape[-1] // LOOK_RG, LOOK_RG)
    )
    return jnp.mean(split_field, axis=(-3, -1))


def resample_date(block, shift_row, kernel_row, out_width):
    blocks = block.reshape(2, shift_row.shape[0], ROW_BLOCK, block.shape[-1])

    def one_block(block_piece, shift_value, kernel_taps):
        window = lax.dynamic_slice_in_dim(
            block_piece, HALO + shift_value - TAPS // 2, out_width + TAPS - 1, 2
        )
        accumulated = kernel_taps[0] * window[:, :, 0:out_width].astype(jnp.float32)
        for tap_index in range(1, TAPS):
            accumulated = accumulated + kernel_taps[tap_index] * window[
                :, :, tap_index : tap_index + out_width
            ].astype(jnp.float32)
        return accumulated.astype(jnp.bfloat16)

    result = jax.vmap(one_block, in_axes=(1, 0, 0), out_axes=1)(blocks, shift_row, kernel_row)
    return result.reshape(2, block.shape[1], out_width)


def resample_stack(padded, shift_rows, kernel_rows, out_width):
    by_date = jnp.moveaxis(padded, 1, 0)

    def one_date(inputs):
        return resample_date(inputs[0], inputs[1], inputs[2], out_width)

    result = lax.map(one_date, (by_date, shift_rows, kernel_rows))
    return jnp.moveaxis(result, 0, 1)


def local(slc_stack, offsets, kernels, partner, inverse, rate_weights, owners, map_cell):
    date_count = slc_stack.shape[1]
    out_width = slc_stack.shape[3]
    first_date = lax.axis_index("date") * date_count
    my_shifts = lax.dynamic_slice_in_dim(offsets, first_date, date_count, 0)
    my_kernels = lax.dynamic_slice_in_dim(kernels, first_date, date_count, 0)
    padded = extended(slc_stack, (("col", 3),), HALO)
    resampled_local = resample_stack(padded, my_shifts, my_kernels, out_width)
    next_group = from_behind(resampled_local[:, :SPAN], "date", -1)
    stacked = jnp.concatenate([resampled_local, next_group], axis=1)

    def date_power(one_slc):
        real_part = one_slc[0].astype(jnp.float32)
        imag_part = one_slc[1].astype(jnp.float32)
        return look_mean(real_part * real_part + imag_part * imag_part)

    looked_power = lax.map(date_power, jnp.moveaxis(stacked, 1, 0))
    pair_count = partner.shape[0]
    second_index = partner - first_date

    def one_pair(inputs):
        pair_local, second_local = inputs
        first_local = pair_local // PER_DATE
        first_slc = lax.dynamic_index_in_dim(stacked, first_local, 1, keepdims=False).astype(
            jnp.float32
        )
        second_slc = lax.dynamic_index_in_dim(stacked, second_local, 1, keepdims=False).astype(
            jnp.float32
        )
        cross = look_mean(first_slc[1] * second_slc[0] - first_slc[0] * second_slc[1])
        power_first = lax.dynamic_index_in_dim(looked_power, first_local, 0, keepdims=False)
        power_second = lax.dynamic_index_in_dim(looked_power, second_local, 0, keepdims=False)
        return (cross / jnp.sqrt(power_first * power_second + 1e-06)).astype(jnp.bfloat16)

    phase_values = lax.map(one_pair, (jnp.arange(pair_count, dtype=jnp.int32), second_index))
    flat_phase = phase_values.reshape(pair_count, -1)
    date_devices = lax.axis_size("date")
    block_pixels = flat_phase.shape[1] // date_devices
    received = lax.all_to_all(
        flat_phase.reshape(pair_count, date_devices, block_pixels),
        "date",
        split_axis=1,
        concat_axis=0,
        tiled=True,
    )
    matrix = received.reshape(received.shape[0], received.shape[2])
    series_rows = lax.dot_general(
        matrix, inverse, (((0,), (1,)), ((), ())), preferred_element_type=jnp.float32
    )
    velocity = jnp.dot(series_rows, rate_weights, precision=lax.Precision.HIGHEST)
    pixel_rows = jnp.concatenate([series_rows, velocity[:, None]], axis=1).astype(jnp.bfloat16)
    owner_list = owners.reshape(-1)
    cell_list = map_cell.reshape(-1)
    col_devices = lax.axis_size("col")
    capacity = max(2, 2 * block_pixels // col_devices)
    owner_hits = (owner_list[:, None] == jnp.arange(col_devices, dtype=jnp.int32)[None, :]).astype(
        jnp.int32
    )
    earlier = jnp.cumsum(owner_hits, axis=0) - owner_hits
    slot_rank = jnp.sum(earlier * owner_hits, axis=1)
    destination = owner_list * capacity + slot_rank
    select = jnp.arange(col_devices * capacity, dtype=jnp.int32)[:, None] == destination[None, :]
    packed = jnp.dot(
        select.astype(jnp.bfloat16), pixel_rows, preferred_element_type=jnp.float32
    ).astype(jnp.bfloat16)
    packed_cells = jnp.sum(jnp.where(select, cell_list[None, :] + 1, 0), axis=1) - 1
    got_rows, got_cells = (
        lax.all_to_all(
            packed.reshape(col_devices, capacity, -1),
            "col",
            split_axis=0,
            concat_axis=0,
            tiled=True,
        ),
        lax.all_to_all(
            packed_cells.reshape(col_devices, capacity),
            "col",
            split_axis=0,
            concat_axis=0,
            tiled=True,
        ),
    )
    tile_cells = TILE_DEV * date_devices
    landing = jnp.arange(tile_cells, dtype=jnp.int32)[:, None] == got_cells.reshape(1, -1)
    tile_totals = jnp.dot(
        landing.astype(jnp.bfloat16),
        got_rows.reshape(col_devices * capacity, -1),
        preferred_element_type=jnp.float32,
    )
    tile_counts = jnp.sum(landing.astype(jnp.float32), axis=1)
    tile_totals, tile_counts = (
        lax.psum_scatter(
            tile_totals.astype(jnp.bfloat16), "date", scatter_dimension=0, tiled=True
        ).astype(jnp.float32),
        lax.psum_scatter(
            tile_counts.astype(jnp.bfloat16), "date", scatter_dimension=0, tiled=True
        ).astype(jnp.float32),
    )
    geocoded = tile_totals / jnp.maximum(tile_counts, 1.0)[:, None]
    return geocoded.reshape(1, TILE_DEV, -1)


def solution(mesh):
    in_specs = (
        P(None, "date", None, "col"),
        P(),
        P(),
        P("date"),
        P(),
        P(),
        P("col", "date", None),
        P("col", "date"),
    )
    out_specs = P("col", "date", None)
    return jax.shard_map(local, mesh=mesh, in_specs=in_specs, out_specs=out_specs, check_vma=False)
```

profile of v0, /device:TPU:32, one launch (start us, length us, event | category | flops | bytes accessed | tf_op | source)
XLA Modules:
  0.0 702.6 jit_solution(3508804317238187564)
XLA Ops:
  4.7 3.6 collective-permute-start.1
  12.0 4.5 maximum_bitcast_fusion
  16.5 241.9 %while.36 = (s32[]{:T(128)}, bf16[12,2,40,640]{3,2,0,1:T(8,128)(2,1)}, f32[12,2,8]{2,1,0:T(2,128)S(1)}, bf16[12,2,40,656]{3,1,2,0:T(2,128)(2,1)}, s32[12,2]{1,0:T(8,128)S(1)}, /*index=5*/s32[]{:T(128)}) while((s32[]{:T(128)}, bf16[12,2,40,640]{3,2,0,1:T(8,128)(2,1)}, f32[12,2,8]{2,1,0:T(2,128)S(1)}, bf16[12,2,40,656]{3,1,2,0:T(2,128)(2,1)}, ...), condition=%wide.region_4.5_spmd, body=%wide.region_3.4_spmd.sunk | while | flops 1228820 | bytes 7079181 | solution.py:71
  20.8 4.7 fusion.26
  41.0 4.7 fusion.26
  61.1 4.7 fusion.26
  81.3 4.7 fusion.26
  101.4 4.7 fusion.26
  121.6 4.7 fusion.26
  141.7 4.7 fusion.26
  161.9 4.7 fusion.26
  182.0 4.7 fusion.26
  202.2 4.7 fusion.26
  222.4 4.7 fusion.26
  242.5 4.7 fusion.26
  262.4 17.0 %all-to-all-start = ((s32[32,1,2]{2,1,0:T(1,128)}), s32[32,1,2]{2,1,0:T(1,128)S(1)}, u32[]{:S(2)}, u32[]{:S(2)}) async-start(s32[32,1,2]{2,1,0:T(1,128)} %bitcast.15), calls=%async_computation | async-start | bytes 32768 | tf_op jit(solution)/shard_map/all_to_all | solution.py:149
  280.1 2.8 fusion.14
  282.9 43.5 %while.37 = (s32[]{:T(128)}, f32[18,8,32]{2,1,0:T(8,128)}, bf16[18,2,40,640]{3,2,0,1:T(8,128)(2,1)}, s32[]{:T(128)}, f32[]{:T(128)}) while((s32[]{:T(128)}, f32[18,8,32]{2,1,0:T(8,128)}, bf16[18,2,40,640]{3,2,0,1:T(8,128)(2,1)}, s32[]{:T(128)}, f32[]{:T(128)}) %tuple.100), condition=%wide.region_7.8_spmd, body=%wide.region_5.7_spmd.sunk | while | flops 153602 | bytes 723525 | solution.py:91
  326.4 258.4 %while.38 = (s32[]{:T(128)}, bf16[36,8,32]{2,1,0:T(8,128)(2,1)S(1)}, s32[36]{0:T(128)S(1)}, bf16[2,18,40,640]{3,2,1,0:T(8,128)(2,1)S(1)}, s32[36]{0:T(128)S(1)},...) while((s32[]{:T(128)}, ...), condition=%wide.region_10.11_spmd, body=%wide.region_8.10_spmd.sunk | while | flops 205840 | bytes 1443143 | solution.py:109
  585.7 7.9 %all-to-all-start.1 = ((bf16[16,2,288]{2,1,0:T(2,128)(2,1)}), bf16[16,2,288]{2,1,0:T(2,128)(2,1)S(1)}, u32[]{:S(2)}, u32[]{:S(2)}) async-start(bf16[16,2,288]{2,1,0:T(2,128)(2,1)} %reshape.200), calls=%async_computation.1 | async-start | bytes 49152 | tf_op jit(solution)/shard_map/all_to_all | solution.py:113
  596.9 4.4 all-to-all-done.1
  602.9 14.8 %all-to-all-start.2 = ((bf16[32,2,192]{2,1,0:T(2,128)(2,1)}), bf16[32,2,192]{2,1,0:T(2,128)(2,1)S(1)}, u32[]{:S(2)}, u32[]{:S(2)}) async-start(bf16[32,2,192]{2,1,0:T(2,128)(2,1)} %reshape.170), calls=%async_computation.2 | async-start | bytes 65536 | tf_op jit(solution)/shard_map/all_to_all | solution.py:142
  617.8 11.7 %all-to-all-done.2 = bf16[32,2,192]{2,1,0:T(2,128)(2,1)S(1)} async-done(((bf16[32,2,192]{2,1,0:T(2,128)(2,1)}), bf16[32,2,192]{2,1,0:T(2,128)(2,1)S(1)}, u32[]{:S(2)}, u32[]{:S(2)}) %all-to-all-start.2) | async-done | bytes 24608 | tf_op jit(solution)/shard_map/all_to_all | solution.py:142
  629.8 72.0 %all-reduce.3 = (bf16[128,192]{1,0:T(8,128)(2,1)S(1)}, bf16[128]{0:T(256)(128)(2,1)S(1)}) all-reduce(bf16[128,192]{1,0:T(8,128)(2,1)S(1)} %convolution_convert_fusion, bf16[128]{0:T(256)(128)(2,1)S(1)} %convert_reduce_fusion), channel_id=2, replica_groups=mesh['date'=16,'col'=32] {'date'}, use_global_device_ids=true, to_apply=%region_11.12.clone | all-reduce | flops 24704 | bytes 98816
  (714 shorter events, 353.2 us)
Async XLA Ops:
  0.0 601.5 %copy-start = (bf16[191,576]{1,0:T(8,128)(2,1)S(1)}, bf16[191,576]{1,0:T(8,128)(2,1)}, u32[]{:S(2)}) copy-start(bf16[191,576]{1,0:T(8,128)(2,1)} %param.18) | copy-start | bytes 660100
  0.0 8.3 %copy-start.7 = (s32[1,16,1]{1,2,0:T(1,128)S(1)}, s32[1,16,1]{1,2,0:T(1,128)}, u32[]{:S(2)}) copy-start(s32[1,16,1]{1,2,0:T(1,128)} %param.20) | copy-start | bytes 196
  0.0 9.2 %copy-start.6 = (f32[192,2,8]{0,2,1:T(8,128)S(1)}, f32[192,2,8]{0,2,1:T(8,128)}, u32[]{:S(2)}) copy-start(f32[192,2,8]{0,2,1:T(8,128)} %param.16) | copy-start | bytes 36868
  0.0 9.3 %copy-start.9 = (s32[192,2]{0,1:T(2,128)S(1)}, s32[192,2]{0,1:T(2,128)}, u32[]{:S(2)}) copy-start(s32[192,2]{0,1:T(2,128)} %param.15) | copy-start | bytes 4612
  2.8 7.5 %collective-permute-start = (bf16[2,12,40,8]{3,0,2,1:T(2,128)(2,1)S(1)}, bf16[2,12,40,8]{3,0,2,1:T(2,128)(2,1)S(1)}, u32[]{:S(2)}, u32[]{:S(2)}) collective-permute-start(bf16[2,12,40,8]{3,0,2,1:T(2,128)(2,1)S(1)} %get-tuple-element.271), channel_id=1, source_target_pairs={{0,1},{1,2},{2,3},{3,4},{4,5},{5,6},{6,7},{7,8},{8,9},{9,10},{10,1... | collective-permute-start | bytes 46088 | tf_op jit(solution)/shard_map/ppermute | solution.py:24
  4.7 7.3 %collective-permute-start.1 = (bf16[2,12,40,8]{3,0,2,1:T(2,128)(2,1)S(1)}, bf16[2,12,40,8]{3,0,2,1:T(2,128)(2,1)S(1)}, u32[]{:S(2)}, u32[]{:S(2)}) collective-permute-start(bf16[2,12,40,8]{3,0,2,1:T(2,128)(2,1)S(1)} %get-tuple-element.272), channel_id=1, source_target_pairs={{1,0},{2,1},{3,2},{4,3},{5,4},{6,5},{7,6},{8,7},{9,8},{10,9},{11,1... | collective-permute-start | bytes 46088 | tf_op jit(solution)/shard_map/ppermute | solution.py:26
  16.5 244.4 %copy-start.10 = (s32[1,16]{1,0:T(1,128)S(1)}, s32[1,16]{1,0:T(1,128)}, u32[]{:S(2)}) copy-start(s32[1,16]{1,0:T(1,128)} %param.21) | copy-start | bytes 196
  25.5 6.4 copy-start.1
  45.7 6.4 copy-start.1
  65.9 6.4 copy-start.1
  86.0 6.4 copy-start.1
  126.3 6.4 copy-start.1
  146.5 6.4 copy-start.1
  166.6 6.4 copy-start.1
  186.8 6.4 copy-start.1
  207.0 6.4 copy-start.1
  227.1 6.4 copy-start.1
  247.3 6.4 copy-start.1
  259.6 20.5 %collective-permute-start.2 = (bf16[2,6,40,640]{3,2,1,0:T(8,128)(2,1)S(1)}, bf16[2,6,40,640]{3,2,1,0:T(8,128)(2,1)S(1)}, u32[]{:S(2)}, u32[]{:S(2)}) collective-permute-start(bf16[2,6,40,640]{3,2,1,0:T(8,128)(2,1)S(1)} %slice.215), channel_id=1, source_target_pairs={{32,0},{64,32},{96,64},{128,96},{160,128},{192,160},{224,192},{256... | collective-permute-start | bytes 1843208 | tf_op jit(solution)/shard_map/ppermute | solution.py:36
  262.4 323.3 %all-to-all-start = ((s32[32,1,2]{2,1,0:T(1,128)}), s32[32,1,2]{2,1,0:T(1,128)S(1)}, u32[]{:S(2)}, u32[]{:S(2)}) async-start(s32[32,1,2]{2,1,0:T(1,128)} %bitcast.15), calls=%async_computation | async-start | bytes 32768 | tf_op jit(solution)/shard_map/all_to_all | solution.py:149
  326.4 275.3 %copy-start.8 = (f32[191]{0:T(256)S(1)}, f32[191]{0:T(256)}, u32[]{:S(2)}) copy-start(f32[191]{0:T(256)} %param.19) | copy-start | bytes 2296
  326.4 275.6 %copy-start.11 = (s32[16]{0:T(128)S(1)}, s32[16]{0:T(128)}, u32[]{:S(2)}) copy-start(s32[16]{0:T(128)} %multiply_add_fusion.1) | copy-start | bytes 196
  585.7 15.6 %all-to-all-start.1 = ((bf16[16,2,288]{2,1,0:T(2,128)(2,1)}), bf16[16,2,288]{2,1,0:T(2,128)(2,1)S(1)}, u32[]{:S(2)}, u32[]{:S(2)}) async-start(bf16[16,2,288]{2,1,0:T(2,128)(2,1)} %reshape.200), calls=%async_computation.1 | async-start | bytes 49152 | tf_op jit(solution)/shard_map/all_to_all | solution.py:113
  602.9 26.6 %all-to-all-start.2 = ((bf16[32,2,192]{2,1,0:T(2,128)(2,1)}), bf16[32,2,192]{2,1,0:T(2,128)(2,1)S(1)}, u32[]{:S(2)}, u32[]{:S(2)}) async-start(bf16[32,2,192]{2,1,0:T(2,128)(2,1)} %reshape.170), calls=%async_computation.2 | async-start | bytes 65536 | tf_op jit(solution)/shard_map/all_to_all | solution.py:142
  (49 other events, 117.1 us)
where the time goes:
time: 708 us; the launch traced here: 703 us
  local copies, waits for them, and re-layouts  345 us (49%)
  loops' own time  153 us (22%)
  blocking collectives  72 us (10%)
  other arithmetic  65.9 us (9%)
  starting transfers between devices  46.6 us (7%)
  waiting for transfers between devices  18.5 us (3%)
    another operation x1, loops' own time, local(): lax.map(one_pair, (jnp.arange(pair_count, dtype=jnp.int32), second_index))  151 us
    while x216, local copies, waits for them, and re-layouts  113 us
    unnamed x1, blocking collectives  72 us
    slice x24, local copies, waits for them, and re-layouts, one_block(): accumulated = kernel_taps[0] * window[:, :, 0:out_width].astype(jnp.float32)  60.5 us
    dynamic_slice x72, local copies, waits for them, and re-layouts, local(): lax.map(one_pair, (jnp.arange(pair_count, dtype=jnp.int32), second_index))  48.1 us
    gather x12, local copies, waits for them, and re-layouts, one_block(): lax.dynamic_slice_in_dim(block_piece, HALO + shift_value - TAPS // 2, out...  27.6 us
    sub x36, local copies, waits for them, and re-layouts, one_pair(): first_slc[1] * second_slc[0] - first_slc[0] * second_slc[1]  26.7 us
    dynamic_update_slice x36, other arithmetic, local(): lax.map(one_pair, (jnp.arange(pair_count, dtype=jnp.int32), second_index))  25.4 us
  transfers between devices with their start and end apart: 6, of which 4 were waited for; matrix products, arithmetic and copies ran while one was open for 23% of the time, Pallas kernels for 0%

commit v1 on v0

v1 whole, which is shorter than its diff:
```python
import functools

import jax
import jax.numpy as jnp
import numpy as np
from jax import lax
from jax.experimental import pallas as pl
from jax.experimental.pallas import tpu as pltpu
from jax.sharding import PartitionSpec as P

PER_DATE = 3
SPAN = 6
HALF = 3
ROW_BLOCK = 20
TAPS = 8
LOOK_AZ = 5
LOOK_RG = 20
LROWS = 8
LANES = 128
ROWS = 40
DATES = 192
K_ROWS = 64
EXTRA = 9
PAIR_ROWS = 48
F32 = jnp.float32
BF16 = jnp.bfloat16
VMEM_BYTES = 56 * 1024 * 1024

INNER = [(a, a + s) for a in range(6) for s in range(1, 7)]
INNER += [(a, b) for a in range(6, 11) for b in range(a + 1, 12)]
CROSS = [(a, b) for b in range(12, 15) for a in range(b - 6, 12)]
BEFORE = [(a, b) for b in range(15, 18) for a in range(b - 6, 12)]


def iota(shape, dim):
    return lax.broadcasted_iota(jnp.int32, shape, dim)


def lane_left(tiles, by, keep):
    lane = iota(tiles[0].shape, 1)
    turned = [pltpu.roll(t, LANES - by, 1) for t in tiles]
    out = [
        jnp.where(lane < LANES - by, turned[j], turned[j + 1])
        for j in range(len(tiles) - 1)
    ]
    if keep:
        out.append(turned[-1])
    return out


def resample(own, near, far, meta, shifts, taps, part, date, zs, slot):
    first, odd = meta[0], meta[2]
    count = own.shape[-1] // LANES
    at = jnp.clip(first + date, 0, DATES - 1)
    tile_a = near[part, date].astype(F32)
    tile_b = far[part, date].astype(F32)
    is_odd = odd == 1
    left = jnp.where(is_odd, tile_a, tile_b)
    right = jnp.where(is_odd, tile_b, tile_a)
    line = own[part, date].astype(F32)
    tiles = [left] + [line[:, LANES * j : LANES * (j + 1)] for j in range(count)] + [right]
    turn = [4 - shifts[b, at] for b in range(2)]
    lane = iota((24, LANES), 1)
    row = iota((8, LANES), 0)
    top = [pltpu.roll(t[:24], turn[0], 1) for t in tiles]
    low = [pltpu.roll(t[16:], turn[1], 1) for t in tiles]
    for j in range(count + 1):
        upper = jnp.where(lane < turn[0], top[j], top[j + 1])
        lower = jnp.where(lane < turn[1], low[j], low[j + 1])
        zs[slot, j, 0:16, :] = upper[:16]
        zs[slot, j, 16:24, :] = jnp.where(row < 4, upper[16:], lower[:8])
        zs[slot, j, 24:40, :] = lower[8:]
    weight = [
        jnp.where(row < 4, taps[t, at], taps[TAPS + t, at]) for t in range(TAPS)
    ]
    slabs = []
    for k in range(LOOK_AZ):
        z = [
            zs[slot, j, pl.ds(k, LROWS, stride=LOOK_AZ), :] for j in range(count + 1)
        ]
        z1 = lane_left(z, 1, True)
        a = [
            [weight[2 * t] * z[j] + weight[2 * t + 1] * z1[j] for j in range(count + 1)]
            for t in range(4)
        ]
        a1 = lane_left(a[1], 2, True)
        a3 = lane_left(a[3], 2, True)
        b0 = [a[0][j] + a1[j] for j in range(count + 1)]
        b1 = lane_left([a[2][j] + a3[j] for j in range(count + 1)], 4, False)
        slabs.append([(b0[j] + b1[j]).astype(BF16) for j in range(count)])
    return slabs


def column(row, rows, offset):
    wide = row.shape[1]
    at = iota((rows, wide), 1) == iota((rows, wide), 0) + offset
    return jnp.sum(jnp.where(at, row, 0.0), axis=1, keepdims=True)


def edge_kernel(meta, shifts, taps, own, near, far, partner, out0, out1, zs):
    odd_date = meta[1]
    local = column((partner[...] - meta[0]).astype(F32), 16, 36 - EXTRA)
    wide = out0.shape[1]
    for out, base in ((out0, 9 - 9 * odd_date), (out1, 9 * odd_date)):
        def one(i, _):
            for part in range(2):
                slabs = resample(own, near, far, meta, shifts, taps, part, base + i, zs, part)
                for k in range(LOOK_AZ):
                    for j, tile in enumerate(slabs[k]):
                        at = pl.multiple_of(i * 80 + part * 40 + k * 8, 8)
                        out[pl.ds(at, 8), LANES * j : LANES * (j + 1)] = tile
            return 0

        lax.fori_loop(0, HALF, one, 0)
        out[240:256, :] = jnp.broadcast_to(local, (16, wide)).astype(BF16)


def window_matrix(depth):
    col, lane = iota((depth, 256), 0), iota((depth, 256), 1)
    start = (lane % 32) * LOOK_RG
    return ((col >= start) & (col < start + LOOK_RG)).astype(BF16)


def window_sum(values, matrix):
    high = values.astype(BF16)
    low = (values - high.astype(F32)).astype(BF16)
    return jnp.dot(high, matrix, preferred_element_type=F32) + jnp.dot(
        low, matrix, preferred_element_type=F32
    )


def cross_sum(first, second):
    total = None
    for k in range(LOOK_AZ):
        re1, im1 = first(0, k), first(1, k)
        re2, im2 = second(0, k), second(1, k)
        term = im1 * re2 - re1 * im2
        total = term if total is None else total + term
    return total


def power_sum(date):
    total = None
    for k in range(LOOK_AZ):
        re, im = date(0, k), date(1, k)
        term = re * re + im * im
        total = term if total is None else total + term
    return total


def phase_of(cross, power_a, power_b):
    mask = iota((8, 256), 1) // 32 == iota((8, 256), 0)
    scale = 1.0 / (LOOK_AZ * LOOK_RG)
    value = (cross * scale) / jnp.sqrt((power_a * scale) * (power_b * scale) + 1e-06)
    return jnp.where(mask, value, 0.0)


def choose(names, have_a, have_b, reverse):
    a, b = names[0:1, :], names[1:2, :]
    take = ((have_a == a) & (have_b == b)).astype(F32)
    if reverse:
        take = take - ((have_a == b) & (have_b == a)).astype(F32)
    return take.astype(BF16)


def inner_kernel(
    meta, shifts, taps, own, near, far, partner, names, inverse, owners,
    phase_out, power_out, kept_out, weight_out, place_out,
    zs, ys, ps, ss, pm,
):
    width = own.shape[-1]
    count = width // LANES

    def one_date(d, _):
        for part in range(2):
            slabs = resample(own, near, far, meta, shifts, taps, part, d, zs, part)
            for k in range(LOOK_AZ):
                for j, tile in enumerate(slabs[k]):
                    ys[d, part, 8 * k : 8 * k + 8, LANES * j : LANES * (j + 1)] = tile.astype(F32)

        def date(part, k):
            return ys[d, part, 8 * k : 8 * k + 8, :]

        ps[pl.ds(pl.multiple_of(d * 8, 8), 8), :] = power_sum(date)
        return 0

    lax.fori_loop(0, 12, one_date, 0)
    for d in range(9):
        for part in range(2):
            at = d * 80 + part * 40
            kept_out[at : at + 40, :] = ys[d + 3, part].astype(BF16)

    def reader(d):
        return lambda part, k: ys[d, part, 8 * k : 8 * k + 8, :]

    def one_first(a, _):
        for s in range(SPAN):
            at = pl.multiple_of((a * SPAN + s) * 8, 8)
            ss[pl.ds(at, 8), :] = cross_sum(reader(a), reader(a + s + 1))
        return 0

    lax.fori_loop(0, 6, one_first, 0)
    for c in range(36, len(INNER)):
        a, b = INNER[c]
        ss[c * 8 : c * 8 + 8, :] = cross_sum(reader(a), reader(b))
    ss[len(INNER) * 8 :, :] = jnp.zeros_like(ss[len(INNER) * 8 :, :])
    matrix = window_matrix(width)
    power_out[...] = window_sum(ps[...], matrix)
    sums = window_sum(ss[...], matrix)
    for c, (a, b) in enumerate(INNER):
        rows = slice(8 * c, 8 * c + 8)
        pm[rows, :] = phase_of(
            sums[rows], power_out[8 * a : 8 * a + 8, :], power_out[8 * b : 8 * b + 8, :]
        )
    pm[len(INNER) * 8 :, :] = jnp.zeros_like(pm[len(INNER) * 8 :, :])
    local = column((partner[...] - meta[0]).astype(F32), PAIR_ROWS, 0)
    row = iota((PAIR_ROWS, 1), 0)
    have_a = jnp.where(row < 36, row // PER_DATE, -9).astype(F32)
    take = choose(names, have_a, local, True)
    phase_out[...] = jnp.dot(take, pm[...].astype(BF16), preferred_element_type=F32)

    rows = weight_out.shape[0]
    group, k = iota((rows, 1), 0) // K_ROWS, iota((rows, 1), 0) % K_ROWS
    target = jnp.where(k < 36, 36 * group + k, jnp.where(k < 45, 36 * group + k - 45, -1))
    gather = (iota((rows, inverse.shape[1]), 1) == target).astype(BF16)
    weight_out[...] = lax.dot_general(
        gather, inverse[...], (((1,), (1,)), ((), ())), preferred_element_type=F32
    ).astype(BF16)

    own_row = owners[...].astype(F32)
    n = own_row.shape[1]
    own_col = column(own_row, n, 0)
    earlier = (own_col == own_row) & (iota((n, n), 0) < iota((n, n), 1))
    rank = jnp.sum(earlier.astype(F32), axis=0, keepdims=True)
    dest = (own_row * 2 + rank).astype(jnp.int32)
    place_out[...] = (iota(place_out.shape, 0) == dest).astype(BF16)


def outer_kernel(
    meta, got0, got1, kept, power, phase, partner, names, out, rs, ps, ss, pm
):
    width = got0.shape[1]
    odd_date = meta[1]
    after, before = 3 * odd_date, 3 - 3 * odd_date
    for part in range(2):
        for i in range(HALF):
            at = i * 80 + part * 40
            rs[i, part] = got0[at : at + 40, :].astype(F32)
            rs[i + 3, part] = got1[at : at + 40, :].astype(F32)

    def there(d):
        return lambda part, k: rs[d, part, 8 * k : 8 * k + 8, :]

    def here(d):
        def read(part, k):
            at = (d - 3) * 80 + part * 40 + k * 8
            return kept[at : at + 8, :].astype(F32)
        return read

    for i in range(HALF):
        ps[8 * i : 8 * i + 8, :] = power_sum(there(after + i))
        ps[24 + 8 * i : 32 + 8 * i, :] = power_sum(there(before + i))
    for c, (a, b) in enumerate(CROSS):
        ss[8 * c : 8 * c + 8, :] = cross_sum(here(a), there(after + b - 12))
    for c, (a, b) in enumerate(BEFORE, len(CROSS)):
        ss[8 * c : 8 * c + 8, :] = cross_sum(there(before + a - 9), here(b - 12))
    matrix = window_matrix(width)
    powers = window_sum(ps[...], matrix)
    last = 8 * (len(CROSS) + len(BEFORE))
    ss[last:, :] = jnp.zeros_like(ss[last:, :])
    sums = window_sum(ss[...], matrix)
    for c, (a, b) in enumerate(CROSS + BEFORE):
        rows = slice(8 * c, 8 * c + 8)
        if c < len(CROSS):
            pa = power[8 * a : 8 * a + 8, :]
            pb = powers[8 * (b - 12) : 8 * (b - 12) + 8]
        else:
            pa = powers[24 + 8 * (a - 9) : 32 + 8 * (a - 9)]
            pb = power[8 * (b - 12) : 8 * (b - 12) + 8, :]
        pm[rows, :] = phase_of(sums[rows], pa, pb)
    pm[last:, :] = jnp.zeros_like(pm[last:, :])
    local = column((partner[...] - meta[0]).astype(F32), PAIR_ROWS, 0)
    row = iota((PAIR_ROWS, 1), 0)
    told = jnp.where(odd_date == 1, got0[240:256, 0:LANES], got1[240:256, 0:LANES]).astype(F32)
    told = jnp.max(told, axis=1, keepdims=True)
    spread = (iota((PAIR_ROWS, 16), 0) - 36 == iota((PAIR_ROWS, 16), 1)).astype(BF16)
    moved = jnp.dot(
        spread, jnp.broadcast_to(told, (16, LANES)).astype(BF16), preferred_element_type=F32
    )[:, 0:1]
    mine = jnp.where(row < 36, jnp.where(local < 15, local, -5.0), jnp.where(row < 45, moved, -5.0))
    mine = jnp.where((row >= 36) & (mine < 15), -5.0, mine)
    have_a = jnp.where(row < 36, row // PER_DATE, 9 + (row - 36) // PER_DATE).astype(F32)
    take = choose(names, have_a, mine, False)
    total = phase[...] + jnp.dot(take, pm[...].astype(BF16), preferred_element_type=F32)
    wide = jnp.concatenate([total, jnp.zeros((LANES - PAIR_ROWS, 256), F32)], axis=0)
    turned = jnp.concatenate([wide[:, 0:128].T, wide[:, 128:256].T], axis=0)
    out[...] = pltpu.roll(turned, K_ROWS * odd_date, 1).astype(BF16)


def series_kernel(got, weight, rates, place, cells, out):
    n = got.shape[1]
    pairs = [(got[2 * h].astype(F32) + got[2 * h + 1].astype(F32)).astype(BF16) for h in range(got.shape[0] // 2)]
    phases = jnp.concatenate(pairs, axis=1)
    series = jnp.dot(phases, weight[...], preferred_element_type=F32)
    velocity = jnp.sum(series * rates[...], axis=1, keepdims=True)
    cell = column(cells[...].astype(F32), n, 0) + 1.0
    lane = iota((n, 256), 1)
    rows = jnp.concatenate([series, jnp.zeros((n, 256 - series.shape[1]), F32)], axis=1)
    rows = jnp.where(lane == 191, velocity, rows)
    rows = jnp.where(lane == 192, 1.0, rows)
    rows = jnp.where(lane == 193, cell, rows)
    out[...] = jnp.dot(place[...], rows.astype(BF16), preferred_element_type=F32).astype(BF16)


def landing_kernel(got, out):
    rows = got[...]
    pick = (iota((8, 256), 1) == 193).astype(BF16)
    cells = lax.dot_general(pick, rows, (((1,), (1,)), ((), ())), preferred_element_type=F32)
    land = (cells[0:1, :] - 1.0 == iota((LANES, rows.shape[0]), 0).astype(F32)).astype(BF16)
    out[...] = jnp.dot(land, rows, preferred_element_type=F32).astype(BF16)


def final_kernel(got, out):
    total = got[0].astype(F32)
    for g in range(1, got.shape[0]):
        total = total + got[g].astype(F32)
    counts = jnp.sum(jnp.where(iota(total.shape, 1) == 192, total, 0.0), axis=1, keepdims=True)
    mean = total / jnp.maximum(counts, 1.0)
    out[...] = mean[:, 0:192]


SMEM = pl.BlockSpec(memory_space=pltpu.SMEM)
VMEM = pl.BlockSpec(memory_space=pltpu.VMEM)


def call(kernel, smem, vmem, outs, scratch=()):
    return pl.pallas_call(
        kernel,
        in_specs=[SMEM] * len(smem) + [VMEM] * len(vmem),
        out_specs=[VMEM] * len(outs),
        out_shape=[jax.ShapeDtypeStruct(s, t) for s, t in outs],
        scratch_shapes=list(scratch),
        compiler_params=pltpu.CompilerParams(vmem_limit_bytes=VMEM_BYTES),
    )(*smem, *vmem)


def swaps(count, start):
    return [p for i in range(start, count - 1, 2) for p in ((i, i + 1), (i + 1, i))]


def pair_names(pairs, rows):
    names = np.full((2, rows), -20.0, np.float32)
    for c, (a, b) in enumerate(pairs):
        names[0, 8 * c : 8 * c + 8] = a
        names[1, 8 * c : 8 * c + 8] = b
    return jnp.asarray(names)


def local(slc_stack, offsets, kernels, partner, inverse, rate_weights, owners, map_cell):
    date_count, width = slc_stack.shape[1], slc_stack.shape[3]
    groups, strips = lax.axis_size("date"), lax.axis_size("col")
    group, strip = lax.axis_index("date"), lax.axis_index("col")
    meta = jnp.stack([group * date_count, group % 2, strip % 2]).astype(jnp.int32)
    shifts = offsets.T
    taps = jnp.transpose(kernels, (1, 2, 0)).reshape(2 * TAPS, DATES)
    partner_row = partner.reshape(1, -1)

    head, tail = slc_stack[..., :LANES], slc_stack[..., width - LANES :]
    even = strip % 2 == 0
    near = lax.ppermute(jnp.where(even, tail, head), "col", swaps(strips, 0))
    far = lax.ppermute(jnp.where(even, head, tail), "col", swaps(strips, 1))
    scratch_z = pltpu.VMEM((2, width // LANES + 1, ROWS, LANES), F32)
    edge0, edge1 = call(
        edge_kernel,
        (meta, shifts, taps),
        (slc_stack, near, far, partner_row),
        [((256, width), BF16)] * 2,
        [scratch_z],
    )
    got0 = lax.ppermute(edge0, "date", swaps(groups, 0))
    got1 = lax.ppermute(edge1, "date", swaps(groups, 1))
    inner_rows = 8 * (len(INNER) + 1)
    outer_rows = 8 * (len(CROSS) + len(BEFORE) + 1)
    phase, power, kept, weight, place = call(
        inner_kernel,
        (meta, shifts, taps),
        (
            slc_stack, near, far, partner_row, pair_names(INNER, inner_rows), inverse,
            owners.reshape(1, -1),
        ),
        [
            ((PAIR_ROWS, 256), F32),
            ((96, 256), F32),
            ((720, width), BF16),
            ((groups * K_ROWS, inverse.shape[0]), BF16),
            ((2 * strips, 256 // groups), BF16),
        ],
        [
            scratch_z,
            pltpu.VMEM((12, 2, ROWS, width), F32),
            pltpu.VMEM((96, width), F32),
            pltpu.VMEM((inner_rows, width), F32),
            pltpu.VMEM((inner_rows, 256), F32),
        ],
    )
    (sent,) = call(
        outer_kernel,
        (meta,),
        (got0, got1, kept, power, phase, partner_row, pair_names(CROSS + BEFORE, outer_rows)),
        [((256, LANES), BF16)],
        [
            pltpu.VMEM((6, 2, ROWS, width), F32),
            pltpu.VMEM((48, width), F32),
            pltpu.VMEM((outer_rows, width), F32),
            pltpu.VMEM((outer_rows, 256), F32),
        ],
    )
    block = 256 // groups
    phases = lax.all_to_all(sent.reshape(groups, block, LANES), "date", 0, 0, tiled=True)
    (routed,) = call(
        series_kernel,
        (),
        (phases, weight, rate_weights.reshape(1, -1), place, map_cell),
        [((2 * strips, 256), BF16)],
    )
    landed = lax.all_to_all(routed.reshape(strips, 2, 256), "col", 0, 0, tiled=True)
    (totals,) = call(landing_kernel, (), (landed.reshape(2 * strips, 256),), [((LANES, 256), BF16)])
    parts = lax.all_to_all(
        totals.reshape(groups, LANES // groups, 256), "date", 0, 0, tiled=True
    )
    (mean,) = call(final_kernel, (), (parts,), [((LANES // groups, DATES), F32)])
    return mean.reshape(1, LANES // groups, DATES)


def solution(mesh):
    in_specs = (
        P(None, "date", None, "col"),
        P(),
        P(),
        P("date"),
        P(),
        P(),
        P("col", "date", None),
        P("col", "date"),
    )
    out_specs = P("col", "date", None)
    return jax.shard_map(local, mesh=mesh, in_specs=in_specs, out_specs=out_specs, check_vma=False)
```

time: 708 us -> 98.1 us (0.14)
  the two profiles are of different devices: /device:TPU:32 before, /device:TPU:1 now
where the time goes in v1:
time: 98.1 us; the launch traced here: 97.5 us
  blocking collectives  55.9 us (57%)
  Pallas kernels  24.3 us (25%)
  starting transfers between devices  12.1 us (12%)
  local copies, waits for them, and re-layouts  2.92 us (3%)
  other arithmetic  1.69 us (2%)
    all_to_all x1, blocking collectives, local(): lax.all_to_all(routed.reshape(strips, 2, 256), 'col', 0, 0, tiled=True)  30.6 us
    pallas_call x6, Pallas kernels, call(): pl.pallas_call(kernel, in_specs=[SMEM] * len(smem) + [VMEM] * len(vmem),...  24.3 us
    all_to_all x1, blocking collectives, local(): lax.all_to_all(sent.reshape(groups, block, LANES), 'date', 0, 0, tiled=True)  14.6 us
    all_to_all x1, blocking collectives, local(): lax.all_to_all(totals.reshape(groups, LANES // groups, 256), 'date', 0, 0...  10.7 us
    ppermute x1, starting transfers between devices, local(): far = lax.ppermute(jnp.where(even, head, tail), 'col', swaps(strips, 1))  4.94 us
    ppermute x1, starting transfers between devices, local(): near = lax.ppermute(jnp.where(even, tail, head), 'col', swaps(strips, 0))  4.53 us
  transfers between devices with their start and end apart: 4, of which 1 were waited for; matrix products, arithmetic and copies ran while one was open for 1% of the time, Pallas kernels for 11%

profile of v1, /device:TPU:1, one launch (start us, length us, event | category | flops | bytes accessed | tf_op | source)
XLA Modules:
  0.0 97.5 jit_solution(10103885029910848940)
XLA Ops:
  0.0 1.1 %broadcast_select_fusion = (bf16[2,12,40,128]{3,2,1,0:T(8,128)(2,1)S(1)}, bf16[2,12,40,128]{3,2,1,0:T(8,128)(2,1)S(1)}) fusion(pred[]{:T(512)S(6)} %eq.7, bf16[2,12,40,640]{3,2,1,0:T(8,128)(2,1)} %own.3), kind=kLoop, calls=%fused_computation | loop fusion | flops 245760 | bytes 983041 | tf_op jit(solution)/shard_map/jit(_where)/select_n | solution.py:371
  1.1 4.9 %collective-permute-start.1 = (bf16[2,12,40,128]{3,2,1,0:T(8,128)(2,1)S(1)}, bf16[2,12,40,128]{3,2,1,0:T(8,128)(2,1)S(1)}, u32[]{:S(2)}, u32[]{:S(2)}) collective-permute-start(bf16[2,12,40,128]{3,2,1,0:T(8,128)(2,1)S(1)} %get-tuple-element.19), channel_id=1, source_target_pairs={{1,2},{2,1},{3,4},{4,3},{5,6},{6,5},{7,8},{8,7},{9,10},{10,9},{11,... | collective-permute-start | bytes 737288 | tf_op jit(solution)/shard_map/ppermute | solution.py:371
  6.1 4.5 %collective-permute-start = (bf16[2,12,40,128]{3,2,1,0:T(8,128)(2,1)S(1)}, bf16[2,12,40,128]{3,2,1,0:T(8,128)(2,1)S(1)}, u32[]{:S(2)}, u32[]{:S(2)}) collective-permute-start(bf16[2,12,40,128]{3,2,1,0:T(8,128)(2,1)S(1)} %get-tuple-element.20), channel_id=1, source_target_pairs={{0,1},{1,0},{2,3},{3,2},{4,5},{5,4},{6,7},{7,6},{8,9},{9,8},{10,11... | collective-permute-start | bytes 737288 | tf_op jit(solution)/shard_map/ppermute | solution.py:370
  10.6 0.6 pad_add_fusion.meta
  11.2 0.5 collective-permute-done.near
  11.7 0.2 copy-done
  11.9 0.5 copy-done.1
  12.4 5.2 %shard_map.100 = (bf16[256,640]{1,0:T(8,128)(2,1)}, bf16[256,640]{1,0:T(8,128)(2,1)}) custom-call(s32[3]{0:T(128)} %pad_add_fusion.meta, s32[2,192]{1,0:T(2,128)} %bitcast.17, f32[16,192]{1,0:T(8,128)} %bitcast.15, bf16[2,12,40,640]{3,2,1,0:T(8,128)(2,1)} %own.3, bf16[2,12,40,128]{3,2,1,0:T(8,128)(2,1)} %copy-done.1, bf16[2,12,40,128]{3,2,1,0:T(8,128)(2,1)} %copy-done, ...), custom_call_target="tpu_custom_call" | custom-call | tf_op jit(solution)/shard_map/pallas_call | solution.py:337
  17.6 1.9 %collective-permute-start.2 = (bf16[256,640]{1,0:T(8,128)(2,1)}, bf16[256,640]{1,0:T(8,128)(2,1)S(1)}, u32[]{:S(2)}, u32[]{:S(2)}) collective-permute-start(bf16[256,640]{1,0:T(8,128)(2,1)} %get-tuple-element.12), channel_id=1, source_target_pairs={{0,32},{32,0},{64,96},{96,64},{128,160},{160,128},{192,224},{224,1... | collective-permute-start | bytes 983048 | tf_op jit(solution)/shard_map/ppermute | solution.py:380
  19.5 0.7 collective-permute-start.3
  20.2 10.6 %shard_map.101 = (f32[48,256]{1,0:T(8,128)}, f32[96,256]{1,0:T(8,128)}, bf16[720,640]{1,0:T(8,128)(2,1)}, bf16[1024,191]{1,0:T(8,128)(2,1)}, bf16[64,16]{1,0:T(8,128)(2,1)}) custom-call(s32[3]{0:T(128)} %pad_add_fusion.meta, s32[2,192]{1,0:T(2,128)} %bitcast.18, f32[16,192]{1,0:T(8,128)} %bitcast.16, bf16[2,12,40,640]{3,2,1,0:T(8,128)(2,1)} %own.3, ...), custom_call_target="tpu_custom_call" | custom-call | tf_op jit(solution)/shard_map/pallas_call | solution.py:337
  30.7 0.0 collective-permute-done.2.got0
  30.8 0.0 collective-permute-done.3.got1
  30.8 0.7 copy-done.2
  31.5 0.1 copy-done.3
  31.6 3.4 %shard_map.102 = bf16[256,128]{1,0:T(8,128)(2,1)} custom-call(s32[3]{0:T(128)} %pad_add_fusion.meta, bf16[256,640]{1,0:T(8,128)(2,1)} %copy-done.2, bf16[256,640]{1,0:T(8,128)(2,1)} %copy-done.3, bf16[720,640]{1,0:T(8,128)(2,1)} %get-tuple-element.14.kept, f32[96,256]{1,0:T(8,128)} %get-tuple-element.15.power, f32[48,256]{1,0:T(8,128)} %get-tuple-element.16.phase, ...), custom_call_target="tpu_custom_call" | custom-call | tf_op jit(solution)/shard_map/pallas_call | solution.py:337
  35.0 14.6 %all_to_all.15.got = bf16[16,16,128]{2,1,0:T(8,128)(2,1)} all-to-all(bf16[16,16,128]{2,1,0:T(8,128)(2,1)} %bitcast.14), channel_id=1, replica_groups=mesh['date'=16,'col'=32] {'date'}, dimensions={0} | all-to-all | bytes 131072 | tf_op jit(solution)/shard_map/all_to_all | solution.py:419
  49.6 2.0 %shard_map.103 = bf16[64,256]{1,0:T(8,128)(2,1)} custom-call(bf16[16,16,128]{2,1,0:T(8,128)(2,1)} %all_to_all.15.got, bf16[1024,191]{1,0:T(8,128)(2,1)} %get-tuple-element.17.weight, f32[1,191]{1,0:T(1,128)} %bitcast.22, bf16[64,16]{1,0:T(8,128)(2,1)} %get-tuple-element.18.place, s32[1,16]{1,0:T(1,128)} %cells.1), custom_call_target="tpu_custom_call" | custom-call | tf_op jit(solution)/shard_map/pallas_call | solution.py:337
  51.6 0.8 reshape.32
  52.4 30.6 %all_to_all.16 = bf16[32,2,256]{2,1,0:T(2,128)(2,1)S(1)} all-to-all(bf16[32,2,256]{2,1,0:T(2,128)(2,1)S(1)} %reshape.32), channel_id=1, replica_groups=mesh['date'=16,'col'=32] {'col'}, dimensions={0} | all-to-all | bytes 65536 | tf_op jit(solution)/shard_map/all_to_all | solution.py:426
  83.0 0.6 reshape.33.got
  83.6 1.7 %shard_map.104 = bf16[128,256]{1,0:T(8,128)(2,1)} custom-call(bf16[64,256]{1,0:T(8,128)(2,1)} %reshape.33.got), custom_call_target="tpu_custom_call" | custom-call | tf_op jit(solution)/shard_map/pallas_call | solution.py:337
  85.3 10.7 %all_to_all.17.got = bf16[16,8,256]{2,1,0:T(8,128)(2,1)} all-to-all(bf16[16,8,256]{2,1,0:T(8,128)(2,1)} %bitcast.13), channel_id=1, replica_groups=mesh['date'=16,'col'=32] {'date'}, dimensions={0} | all-to-all | bytes 131072 | tf_op jit(solution)/shard_map/all_to_all | solution.py:428
  95.9 1.5 %shard_map.105 = f32[8,192]{1,0:T(8,128)} custom-call(bf16[16,8,256]{2,1,0:T(8,128)(2,1)} %all_to_all.17.got), custom_call_target="tpu_custom_call" | custom-call | tf_op jit(solution)/shard_map/pallas_call | solution.py:337
  (5 shorter events, 0.0 us)
Async XLA Ops:
  1.1 10.1 %collective-permute-start.1 = (bf16[2,12,40,128]{3,2,1,0:T(8,128)(2,1)S(1)}, bf16[2,12,40,128]{3,2,1,0:T(8,128)(2,1)S(1)}, u32[]{:S(2)}, u32[]{:S(2)}) collective-permute-start(bf16[2,12,40,128]{3,2,1,0:T(8,128)(2,1)S(1)} %get-tuple-element.19), channel_id=1, source_target_pairs={{1,2},{2,1},{3,4},{4,3},{5,6},{6,5},{7,8},{8,7},{9,10},{10,9},{11,... | collective-permute-start | bytes 737288 | tf_op jit(solution)/shard_map/ppermute | solution.py:371
  6.1 5.7 %collective-permute-start = (bf16[2,12,40,128]{3,2,1,0:T(8,128)(2,1)S(1)}, bf16[2,12,40,128]{3,2,1,0:T(8,128)(2,1)S(1)}, u32[]{:S(2)}, u32[]{:S(2)}) collective-permute-start(bf16[2,12,40,128]{3,2,1,0:T(8,128)(2,1)S(1)} %get-tuple-element.20), channel_id=1, source_target_pairs={{0,1},{1,0},{2,3},{3,2},{4,5},{5,4},{6,7},{7,6},{8,9},{9,8},{10,11... | collective-permute-start | bytes 737288 | tf_op jit(solution)/shard_map/ppermute | solution.py:370
  11.2 0.7 copy-start
  11.7 0.7 copy-start.1
  17.6 13.2 %collective-permute-start.2 = (bf16[256,640]{1,0:T(8,128)(2,1)}, bf16[256,640]{1,0:T(8,128)(2,1)S(1)}, u32[]{:S(2)}, u32[]{:S(2)}) collective-permute-start(bf16[256,640]{1,0:T(8,128)(2,1)} %get-tuple-element.12), channel_id=1, source_target_pairs={{0,32},{32,0},{64,96},{96,64},{128,160},{160,128},{192,224},{224,1... | collective-permute-start | bytes 983048 | tf_op jit(solution)/shard_map/ppermute | solution.py:380
  19.5 11.3 %collective-permute-start.3 = (bf16[256,640]{1,0:T(8,128)(2,1)}, bf16[256,640]{1,0:T(8,128)(2,1)S(1)}, u32[]{:S(2)}, u32[]{:S(2)}) collective-permute-start(bf16[256,640]{1,0:T(8,128)(2,1)} %get-tuple-element.13), channel_id=1, source_target_pairs={{32,64},{64,32},{96,128},{128,96},{160,192},{192,160},{224,256},{2... | collective-permute-start | bytes 983048 | tf_op jit(solution)/shard_map/ppermute | solution.py:381
  30.7 0.7 copy-start.2
  30.8 0.8 copy-start.3

commit v2 on v1

--- a/solution.py
+++ b/solution.py
@@ -19,12 +19,11 @@
 LANES = 128
 ROWS = 40
 DATES = 192
-K_ROWS = 64
 EXTRA = 9
 PAIR_ROWS = 48
 F32 = jnp.float32
 BF16 = jnp.bfloat16
-VMEM_BYTES = 56 * 1024 * 1024
+VMEM_BYTES = 24 * 1024 * 1024
 
 INNER = [(a, a + s) for a in range(6) for s in range(1, 7)]
 INNER += [(a, b) for a in range(6, 11) for b in range(a + 1, 12)]
@@ -111,7 +110,7 @@
                         out[pl.ds(at, 8), LANES * j : LANES * (j + 1)] = tile
             return 0
 
-        lax.fori_loop(0, HALF, one, 0)
+        lax.fori_loop(0, HALF, one, 0, unroll=True)
         out[240:256, :] = jnp.broadcast_to(local, (16, wide)).astype(BF16)
 
 
@@ -164,8 +163,8 @@
 
 
 def inner_kernel(
-    meta, shifts, taps, own, near, far, partner, names, inverse, owners,
-    phase_out, power_out, kept_out, weight_out, place_out,
+    meta, shifts, taps, own, near, far, partner, names, inverse, rates, owners, cells,
+    phase_out, power_out, kept_out, weight_out, rates_out,
     zs, ys, ps, ss, pm,
 ):
     width = own.shape[-1]
@@ -184,7 +183,7 @@
         ps[pl.ds(pl.multiple_of(d * 8, 8), 8), :] = power_sum(date)
         return 0
 
-    lax.fori_loop(0, 12, one_date, 0)
+    lax.fori_loop(0, 12, one_date, 0, unroll=2)
     for d in range(9):
         for part in range(2):
             at = d * 80 + part * 40
@@ -217,23 +216,23 @@
     row = iota((PAIR_ROWS, 1), 0)
     have_a = jnp.where(row < 36, row // PER_DATE, -9).astype(F32)
     take = choose(names, have_a, local, True)
-    phase_out[...] = jnp.dot(take, pm[...].astype(BF16), preferred_element_type=F32)
-
-    rows = weight_out.shape[0]
-    group, k = iota((rows, 1), 0) // K_ROWS, iota((rows, 1), 0) % K_ROWS
+
+    spots = iota((1, weight_out.shape[1]), 1)
+    group, k = spots // PAIR_ROWS, spots % PAIR_ROWS
     target = jnp.where(k < 36, 36 * group + k, jnp.where(k < 45, 36 * group + k - 45, -1))
-    gather = (iota((rows, inverse.shape[1]), 1) == target).astype(BF16)
-    weight_out[...] = lax.dot_general(
-        gather, inverse[...], (((1,), (1,)), ((), ())), preferred_element_type=F32
-    ).astype(BF16)
-
-    own_row = owners[...].astype(F32)
-    n = own_row.shape[1]
-    own_col = column(own_row, n, 0)
-    earlier = (own_col == own_row) & (iota((n, n), 0) < iota((n, n), 1))
-    rank = jnp.sum(earlier.astype(F32), axis=0, keepdims=True)
-    dest = (own_row * 2 + rank).astype(jnp.int32)
-    place_out[...] = (iota(place_out.shape, 0) == dest).astype(BF16)
+    gather = (iota((inverse.shape[1], weight_out.shape[1]), 0) == target).astype(BF16)
+    weight_out[0:191, :] = jnp.dot(inverse[...], gather, preferred_element_type=F32).astype(BF16)
+    weight_out[191:192, :] = jnp.zeros((1, weight_out.shape[1]), BF16)
+    rates_out[...] = jnp.broadcast_to(column(rates[...], DATES, 0), rates_out.shape)
+
+    n = owners.shape[1]
+    spread = (iota((n, 256), 1) == iota((n, 256), 0) + n * meta[3]).astype(BF16)
+    codes = jnp.concatenate([owners[...], cells[...]], axis=0).astype(F32).astype(BF16)
+    placed = jnp.dot(codes, spread, preferred_element_type=F32)
+    lines = iota((PAIR_ROWS, 256), 0)
+    phases = jnp.dot(take, pm[...].astype(BF16), preferred_element_type=F32)
+    phases = jnp.where(lines == 46, placed[0:1, :], phases)
+    phase_out[...] = jnp.where(lines == 47, placed[1:2, :], phases)
 
 
 def outer_kernel(
@@ -292,32 +291,30 @@
     have_a = jnp.where(row < 36, row // PER_DATE, 9 + (row - 36) // PER_DATE).astype(F32)
     take = choose(names, have_a, mine, False)
     total = phase[...] + jnp.dot(take, pm[...].astype(BF16), preferred_element_type=F32)
-    wide = jnp.concatenate([total, jnp.zeros((LANES - PAIR_ROWS, 256), F32)], axis=0)
-    turned = jnp.concatenate([wide[:, 0:128].T, wide[:, 128:256].T], axis=0)
-    out[...] = pltpu.roll(turned, K_ROWS * odd_date, 1).astype(BF16)
-
-
-def series_kernel(got, weight, rates, place, cells, out):
-    n = got.shape[1]
-    pairs = [(got[2 * h].astype(F32) + got[2 * h + 1].astype(F32)).astype(BF16) for h in range(got.shape[0] // 2)]
-    phases = jnp.concatenate(pairs, axis=1)
-    series = jnp.dot(phases, weight[...], preferred_element_type=F32)
-    velocity = jnp.sum(series * rates[...], axis=1, keepdims=True)
-    cell = column(cells[...].astype(F32), n, 0) + 1.0
-    lane = iota((n, 256), 1)
-    rows = jnp.concatenate([series, jnp.zeros((n, 256 - series.shape[1]), F32)], axis=1)
-    rows = jnp.where(lane == 191, velocity, rows)
-    rows = jnp.where(lane == 192, 1.0, rows)
-    rows = jnp.where(lane == 193, cell, rows)
-    out[...] = jnp.dot(place[...], rows.astype(BF16), preferred_element_type=F32).astype(BF16)
-
-
-def landing_kernel(got, out):
-    rows = got[...]
-    pick = (iota((8, 256), 1) == 193).astype(BF16)
-    cells = lax.dot_general(pick, rows, (((1,), (1,)), ((), ())), preferred_element_type=F32)
-    land = (cells[0:1, :] - 1.0 == iota((LANES, rows.shape[0]), 0).astype(F32)).astype(BF16)
-    out[...] = jnp.dot(land, rows, preferred_element_type=F32).astype(BF16)
+    for g in range(out.shape[0]):
+        out[g] = total.astype(BF16)
+
+
+def series_kernel(meta, got, weight, rates, out):
+    stack = jnp.concatenate([got[g] for g in range(got.shape[0])], axis=0)
+    series = jnp.dot(weight[...], stack, preferred_element_type=F32)
+    wide = series.shape[1]
+    turned = [series[:, :LANES] * rates[...], series[:, LANES:] * rates[...]]
+    velocity = jnp.sum(jnp.concatenate(turned, axis=1), axis=0, keepdims=True)
+    series = jnp.where(iota(series.shape, 0) == 191, velocity, series)
+    ones = jnp.where(iota((64, wide), 0) == 0, 1.0, 0.0)
+    rows = jnp.concatenate([series, ones], axis=0).astype(BF16)
+    codes = got[0, 40:48, :].astype(F32)
+    for g in range(1, got.shape[0]):
+        codes = codes + got[g, 40:48, :].astype(F32)
+    owner, cell = codes[6:7, :], codes[7:8, :]
+    base = (meta[3] * 8).astype(F32)
+    mine = (cell >= base) & (cell < base + 8)
+    target = jnp.where(mine, owner * 8 + cell - base, -1.0).astype(jnp.int32)
+    select = (iota((out.shape[0], wide), 0) == target).astype(BF16)
+    out[...] = lax.dot_general(
+        select, rows, (((1,), (1,)), ((), ())), preferred_element_type=F32
+    ).astype(BF16)
 
 
 def final_kernel(got, out):
@@ -360,7 +357,7 @@
     date_count, width = slc_stack.shape[1], slc_stack.shape[3]
     groups, strips = lax.axis_size("date"), lax.axis_size("col")
     group, strip = lax.axis_index("date"), lax.axis_index("col")
-    meta = jnp.stack([group * date_count, group % 2, strip % 2]).astype(jnp.int32)
+    meta = jnp.stack([group * date_count, group % 2, strip % 2, group]).astype(jnp.int32)
     shifts = offsets.T
     taps = jnp.transpose(kernels, (1, 2, 0)).reshape(2 * TAPS, DATES)
     partner_row = partner.reshape(1, -1)
@@ -381,19 +378,19 @@
     got1 = lax.ppermute(edge1, "date", swaps(groups, 1))
     inner_rows = 8 * (len(INNER) + 1)
     outer_rows = 8 * (len(CROSS) + len(BEFORE) + 1)
-    phase, power, kept, weight, place = call(
+    phase, power, kept, weight, rates = call(
         inner_kernel,
         (meta, shifts, taps),
         (
             slc_stack, near, far, partner_row, pair_names(INNER, inner_rows), inverse,
-            owners.reshape(1, -1),
+            rate_weights.reshape(1, -1), owners.reshape(1, -1), map_cell,
         ),
         [
             ((PAIR_ROWS, 256), F32),
             ((96, 256), F32),
             ((720, width), BF16),
-            ((groups * K_ROWS, inverse.shape[0]), BF16),
-            ((2 * strips, 256 // groups), BF16),
+            ((DATES, groups * PAIR_ROWS), BF16),
+            ((DATES, LANES), F32),
         ],
         [
             scratch_z,
@@ -407,7 +404,7 @@
         outer_kernel,
         (meta,),
         (got0, got1, kept, power, phase, partner_row, pair_names(CROSS + BEFORE, outer_rows)),
-        [((256, LANES), BF16)],
+        [((groups, PAIR_ROWS, 256), BF16)],
         [
             pltpu.VMEM((6, 2, ROWS, width), F32),
             pltpu.VMEM((48, width), F32),
@@ -415,21 +412,11 @@
             pltpu.VMEM((outer_rows, 256), F32),
         ],
     )
-    block = 256 // groups
-    phases = lax.all_to_all(sent.reshape(groups, block, LANES), "date", 0, 0, tiled=True)
-    (routed,) = call(
-        series_kernel,
-        (),
-        (phases, weight, rate_weights.reshape(1, -1), place, map_cell),
-        [((2 * strips, 256), BF16)],
-    )
-    landed = lax.all_to_all(routed.reshape(strips, 2, 256), "col", 0, 0, tiled=True)
-    (totals,) = call(landing_kernel, (), (landed.reshape(2 * strips, 256),), [((LANES, 256), BF16)])
-    parts = lax.all_to_all(
-        totals.reshape(groups, LANES // groups, 256), "date", 0, 0, tiled=True
-    )
-    (mean,) = call(final_kernel, (), (parts,), [((LANES // groups, DATES), F32)])
-    return mean.reshape(1, LANES // groups, DATES)
+    phases = lax.all_to_all(sent, "date", 0, 0, tiled=True)
+    (routed,) = call(series_kernel, (meta,), (phases, weight, rates), [((8 * strips, 256), BF16)])
+    parts = lax.all_to_all(routed.reshape(strips, 8, 256), "col", 0, 0, tiled=True)
+    (mean,) = call(final_kernel, (), (parts,), [((8, DATES), F32)])
+    return mean.reshape(1, 8, DATES)
 
 
 def solution(mesh):

time: 98.1 us -> 96.3 us (0.982)
  blocking collectives: 55.9 us -> 50 us
  Pallas kernels: 24.3 us -> 28 us
    all_to_all x3 -> x2, blocking collectives: 55.9 us -> 50 us  [the longest x1 33 us: local(): lax.all_to_all(routed.reshape(strips, 8, 256), 'col', 0, 0, tiled=True)]
    pallas_call x6 -> x5, Pallas kernels: 24.3 us -> 28 us  [call(): pl.pallas_call(kernel, in_specs=[SMEM] * len(smem) + [VMEM] * len(vmem),...]
    unnamed x8 -> x20, local copies, waits for them, and re-layouts: 1.52 us -> 3.37 us
    reshape x2 -> x0, local copies, waits for them, and re-layouts: 1.4 us -> none  [the longest x1 0.77 us: local(): routed.reshape(strips, 2, 256)]
  transfers between devices with their start and end apart: 4 -> 4, of which waited for: 1 -> 1; matrix products, arithmetic and copies ran while one was open for 1% -> 0% of each run, Pallas kernels for 11% -> 15%
where the time goes in v2:
time: 96.3 us; the launch traced here: 95.9 us
  blocking collectives  50 us (52%)
  Pallas kernels  28 us (29%)
  starting transfers between devices  12 us (12%)
  local copies, waits for them, and re-layouts  3.37 us (3%)
  other arithmetic  1.23 us (1%)
  waiting for transfers between devices  1.03 us (1%)
    all_to_all x1, blocking collectives, local(): lax.all_to_all(routed.reshape(strips, 8, 256), 'col', 0, 0, tiled=True)  33 us
    pallas_call x5, Pallas kernels, call(): pl.pallas_call(kernel, in_specs=[SMEM] * len(smem) + [VMEM] * len(vmem),...  28 us
    all_to_all x1, blocking collectives, local(): phases = lax.all_to_all(sent, 'date', 0, 0, tiled=True)  17 us
    ppermute x1, starting transfers between devices, local(): far = lax.ppermute(jnp.where(even, head, tail), 'col', swaps(strips, 1))  4.94 us
    ppermute x1, starting transfers between devices, local(): near = lax.ppermute(jnp.where(even, tail, head), 'col', swaps(strips, 0))  4.51 us
    unnamed x20, local copies, waits for them, and re-layouts  3.37 us
  transfers between devices with their start and end apart: 4, of which 1 were waited for; matrix products, arithmetic and copies ran while one was open for 0% of the time, Pallas kernels for 15%

profile of v2, /device:TPU:1, one launch (start us, length us, event | category | flops | bytes accessed | tf_op | source)
XLA Modules:
  0.0 95.9 jit_solution(742254217138782329)
XLA Ops:
  0.0 0.0 copy-start.8
  0.0 0.0 copy-start.9
  0.0 1.2 %broadcast_select_fusion = (bf16[2,12,40,128]{3,2,1,0:T(8,128)(2,1)S(1)}, bf16[2,12,40,128]{3,2,1,0:T(8,128)(2,1)S(1)}) fusion(pred[]{:T(512)S(6)} %eq.7, bf16[2,12,40,640]{3,2,1,0:T(8,128)(2,1)} %own.3), kind=kLoop, calls=%fused_computation | loop fusion | flops 245760 | bytes 983041 | tf_op jit(solution)/shard_map/jit(_where)/select_n | solution.py:368
  1.2 4.9 %collective-permute-start.1 = (bf16[2,12,40,128]{3,2,1,0:T(8,128)(2,1)S(1)}, bf16[2,12,40,128]{3,2,1,0:T(8,128)(2,1)S(1)}, u32[]{:S(2)}, u32[]{:S(2)}) collective-permute-start(bf16[2,12,40,128]{3,2,1,0:T(8,128)(2,1)S(1)} %get-tuple-element.19), channel_id=1, source_target_pairs={{1,2},{2,1},{3,4},{4,3},{5,6},{6,5},{7,8},{8,7},{9,10},{10,9},{11,... | collective-permute-start | bytes 737288 | tf_op jit(solution)/shard_map/ppermute | solution.py:368
  6.1 4.5 %collective-permute-start = (bf16[2,12,40,128]{3,2,1,0:T(8,128)(2,1)S(1)}, bf16[2,12,40,128]{3,2,1,0:T(8,128)(2,1)S(1)}, u32[]{:S(2)}, u32[]{:S(2)}) collective-permute-start(bf16[2,12,40,128]{3,2,1,0:T(8,128)(2,1)S(1)} %get-tuple-element.20), channel_id=1, source_target_pairs={{0,1},{1,0},{2,3},{3,2},{4,5},{5,4},{6,7},{7,6},{8,9},{9,8},{10,11... | collective-permute-start | bytes 737288 | tf_op jit(solution)/shard_map/ppermute | solution.py:367
  10.7 0.1 pad_add_fusion.meta
  10.7 0.0 collective-permute-done.1.far
  10.7 1.0 %collective-permute-done.near = bf16[2,12,40,128]{3,2,1,0:T(8,128)(2,1)S(1)} collective-permute-done((bf16[2,12,40,128]{3,2,1,0:T(8,128)(2,1)S(1)}, bf16[2,12,40,128]{3,2,1,0:T(8,128)(2,1)S(1)}, u32[]{:S(2)}, u32[]{:S(2)}) %collective-permute-start) | collective-permute-done | bytes 245792 | tf_op jit(solution)/shard_map/ppermute | solution.py:367
  11.8 1.3 %copy-done = bf16[2,12,40,640]{3,2,1,0:T(8,128)(2,1)S(1)} copy-done((bf16[2,12,40,640]{3,2,1,0:T(8,128)(2,1)S(1)}, bf16[2,12,40,640]{3,2,1,0:T(8,128)(2,1)}, u32[]{:S(2)}) %copy-start) | copy-done | bytes 1228824
  13.1 0.7 copy-done.2
  13.8 0.7 copy-done.3
  14.5 0.7 copy-done.4
  15.1 9.9 %shard_map.100 = (bf16[256,640]{1,0:T(8,128)(2,1)S(1)}, bf16[256,640]{1,0:T(8,128)(2,1)S(1)}) custom-call(s32[4]{0:T(128)S(1)} %pad_add_fusion.meta, s32[2,192]{1,0:T(2,128)S(1)} %bitcast.16, f32[16,192]{1,0:T(8,128)S(1)} %bitcast.14, bf16[2,12,40,640]{3,2,1,0:T(8,128)(2,1)S(1)} %copy-done, bf16[2,12,40,128]{3,2,1,0:T(8,128)(2,1)S(1)} %collective-permute-done.near, ...), custom_call_target="tpu_custom_call" | custom-call | tf_op jit(solution)/shard_map/pallas_call | solution.py:334
  25.0 0.0 copy-start.6
  25.0 1.9 %collective-permute-start.2 = (bf16[256,640]{1,0:T(8,128)(2,1)S(1)}, bf16[256,640]{1,0:T(8,128)(2,1)S(1)}, u32[]{:S(2)}, u32[]{:S(2)}) collective-permute-start(bf16[256,640]{1,0:T(8,128)(2,1)S(1)} %get-tuple-element.12), channel_id=1, source_target_pairs={{0,32},{32,0},{64,96},{96,64},{128,160},{160,128},{192,224},{224,1... | collective-permute-start | bytes 983048 | tf_op jit(solution)/shard_map/ppermute | solution.py:377
  26.9 0.7 collective-permute-start.3
  27.7 14.8 %shard_map.101 = (f32[48,256]{1,0:T(8,128)S(1)}, f32[96,256]{1,0:T(8,128)S(1)}, bf16[720,640]{1,0:T(8,128)(2,1)S(1)}, bf16[192,768]{1,0:T(8,128)(2,1)S(1)}, f32[192,128]{1,0:T(8,128)S(1)}) custom-call(s32[4]{0:T(128)S(1)} %pad_add_fusion.meta, s32[2,192]{1,0:T(2,128)S(1)} %bitcast.17, f32[16,192]{1,0:T(8,128)S(1)} %bitcast.15, ...), custom_call_target="tpu_custom_call" | custom-call | tf_op jit(solution)/shard_map/pallas_call | solution.py:334
  42.4 0.0 collective-permute-done.2.got0
  42.5 0.0 collective-permute-done.3.got1
  42.5 1.7 %shard_map.102 = bf16[16,48,256]{2,1,0:T(8,128)(2,1)S(1)} custom-call(s32[4]{0:T(128)S(1)} %pad_add_fusion.meta, bf16[256,640]{1,0:T(8,128)(2,1)S(1)} %collective-permute-done.2.got0, bf16[256,640]{1,0:T(8,128)(2,1)S(1)} %collective-permute-done.3.got1, bf16[720,640]{1,0:T(8,128)(2,1)S(1)} %get-tuple-element.14.kept, f32[96,256]{1,0:T(8,128)S(1)} %get-tuple-element.15.power, ...), custom_call_target="tpu_custom_call" | custom-call | tf_op jit(solution)/shard_map/pallas_call | solution.py:334
  44.2 17.0 %all_to_all.10.got = bf16[16,48,256]{2,1,0:T(8,128)(2,1)S(1)} all-to-all(bf16[16,48,256]{2,1,0:T(8,128)(2,1)S(1)} %shard_map.102), channel_id=1, replica_groups=mesh['date'=16,'col'=32] {'date'}, dimensions={0} | all-to-all | bytes 786432 | tf_op jit(solution)/shard_map/all_to_all | solution.py:415
  61.2 1.0 %shard_map.103 = bf16[256,256]{1,0:T(8,128)(2,1)S(1)} custom-call(s32[4]{0:T(128)S(1)} %pad_add_fusion.meta, bf16[16,48,256]{2,1,0:T(8,128)(2,1)S(1)} %all_to_all.10.got, bf16[192,768]{1,0:T(8,128)(2,1)S(1)} %get-tuple-element.17.weight, f32[192,128]{1,0:T(8,128)S(1)} %get-tuple-element.18.rates), custom_call_target="tpu_custom_call" | custom-call | tf_op jit(solution)/shard_map/pallas_call | solution.py:334
  62.2 33.0 %all_to_all.11.got = bf16[32,8,256]{2,1,0:T(8,128)(2,1)S(1)} all-to-all(bf16[32,8,256]{2,1,0:T(8,128)(2,1)S(1)} %bitcast.13), channel_id=1, replica_groups=mesh['date'=16,'col'=32] {'col'}, dimensions={0} | all-to-all | bytes 262144 | tf_op jit(solution)/shard_map/all_to_all | solution.py:417
  95.2 0.7 shard_map.104
  (13 shorter events, 0.0 us)
Async XLA Ops:
  0.0 27.6 %copy-start.1 = (bf16[191,576]{1,0:T(8,128)(2,1)S(1)}, bf16[191,576]{1,0:T(8,128)(2,1)}, u32[]{:S(2)}) copy-start(bf16[191,576]{1,0:T(8,128)(2,1)} %inverse.1) | copy-start | bytes 660100
  0.0 27.6 %copy-start.5 = (f32[2,416]{1,0:T(2,128)S(1)}, f32[2,416]{1,0:T(2,128)}, u32[]{:S(2)}) copy-start(f32[2,416]{1,0:T(2,128)} %constant.35.clone.names) | copy-start | bytes 9988
  0.0 27.6 %copy-start.7 = (f32[191]{0:T(256)S(1)}, f32[191]{0:T(256)}, u32[]{:S(2)}) copy-start(f32[191]{0:T(256)} %param.15) | copy-start | bytes 2296
  0.0 27.6 %copy-start.8 = (s32[1,16,1]{1,2,0:T(1,128)S(1)}, s32[1,16,1]{1,2,0:T(1,128)}, u32[]{:S(2)}) copy-start(s32[1,16,1]{1,2,0:T(1,128)} %param.16) | copy-start | bytes 196
  0.0 27.6 %copy-start.9 = (s32[1,16]{1,0:T(1,128)S(1)}, s32[1,16]{1,0:T(1,128)}, u32[]{:S(2)}) copy-start(s32[1,16]{1,0:T(1,128)} %cells.1) | copy-start | bytes 196
  1.2 9.6 %collective-permute-start.1 = (bf16[2,12,40,128]{3,2,1,0:T(8,128)(2,1)S(1)}, bf16[2,12,40,128]{3,2,1,0:T(8,128)(2,1)S(1)}, u32[]{:S(2)}, u32[]{:S(2)}) collective-permute-start(bf16[2,12,40,128]{3,2,1,0:T(8,128)(2,1)S(1)} %get-tuple-element.19), channel_id=1, source_target_pairs={{1,2},{2,1},{3,4},{4,3},{5,6},{6,5},{7,8},{8,7},{9,10},{10,9},{11,... | collective-permute-start | bytes 737288 | tf_op jit(solution)/shard_map/ppermute | solution.py:368
  6.1 5.6 %collective-permute-start = (bf16[2,12,40,128]{3,2,1,0:T(8,128)(2,1)S(1)}, bf16[2,12,40,128]{3,2,1,0:T(8,128)(2,1)S(1)}, u32[]{:S(2)}, u32[]{:S(2)}) collective-permute-start(bf16[2,12,40,128]{3,2,1,0:T(8,128)(2,1)S(1)} %get-tuple-element.20), channel_id=1, source_target_pairs={{0,1},{1,0},{2,3},{3,2},{4,5},{5,4},{6,7},{7,6},{8,9},{9,8},{10,11... | collective-permute-start | bytes 737288 | tf_op jit(solution)/shard_map/ppermute | solution.py:367
  11.8 1.3 %copy-start = (bf16[2,12,40,640]{3,2,1,0:T(8,128)(2,1)S(1)}, bf16[2,12,40,640]{3,2,1,0:T(8,128)(2,1)}, u32[]{:S(2)}) copy-start(bf16[2,12,40,640]{3,2,1,0:T(8,128)(2,1)} %own.3) | copy-start | bytes 3686404
  13.1 0.7 copy-start.2
  13.8 0.7 copy-start.3
  14.5 0.7 copy-start.4
  25.0 17.5 %copy-start.6 = (f32[2,176]{1,0:T(2,128)S(1)}, f32[2,176]{1,0:T(2,128)}, u32[]{:S(2)}) copy-start(f32[2,176]{1,0:T(2,128)} %constant.36.clone.names) | copy-start | bytes 4228
  25.0 17.5 %collective-permute-start.2 = (bf16[256,640]{1,0:T(8,128)(2,1)S(1)}, bf16[256,640]{1,0:T(8,128)(2,1)S(1)}, u32[]{:S(2)}, u32[]{:S(2)}) collective-permute-start(bf16[256,640]{1,0:T(8,128)(2,1)S(1)} %get-tuple-element.12), channel_id=1, source_target_pairs={{0,32},{32,0},{64,96},{96,64},{128,160},{160,128},{192,224},{224,1... | collective-permute-start | bytes 983048 | tf_op jit(solution)/shard_map/ppermute | solution.py:377
  26.9 15.5 %collective-permute-start.3 = (bf16[256,640]{1,0:T(8,128)(2,1)S(1)}, bf16[256,640]{1,0:T(8,128)(2,1)S(1)}, u32[]{:S(2)}, u32[]{:S(2)}) collective-permute-start(bf16[256,640]{1,0:T(8,128)(2,1)S(1)} %get-tuple-element.13), channel_id=1, source_target_pairs={{32,64},{64,32},{96,128},{128,96},{160,192},{192,160},{224,256},{2... | collective-permute-start | bytes 983048 | tf_op jit(solution)/shard_map/ppermute | solution.py:378

commit v3 on v2

--- a/solution.py
+++ b/solution.py
@@ -35,6 +35,14 @@
     return lax.broadcasted_iota(jnp.int32, shape, dim)
 
 
+def fact(table, n):
+    return table[2 * TAPS + 3, n].astype(jnp.int32)
+
+
+def partner_row(table, lines):
+    return lines[2 * TAPS + 2 : 2 * TAPS + 3, 0:36] - table[2 * TAPS + 3, 0]
+
+
 def lane_left(tiles, by, keep):
     lane = iota(tiles[0].shape, 1)
     turned = [pltpu.roll(t, LANES - by, 1) for t in tiles]
@@ -47,8 +55,8 @@
     return out
 
 
-def resample(own, near, far, meta, shifts, taps, part, date, zs, slot):
-    first, odd = meta[0], meta[2]
+def resample(own, near, far, table, part, date, zs, slot):
+    first, odd = fact(table, 0), fact(table, 2)
     count = own.shape[-1] // LANES
     at = jnp.clip(first + date, 0, DATES - 1)
     tile_a = near[part, date].astype(F32)
@@ -58,7 +66,7 @@
     right = jnp.where(is_odd, tile_b, tile_a)
     line = own[part, date].astype(F32)
     tiles = [left] + [line[:, LANES * j : LANES * (j + 1)] for j in range(count)] + [right]
-    turn = [4 - shifts[b, at] for b in range(2)]
+    turn = [4 - table[2 * TAPS + b, at].astype(jnp.int32) for b in range(2)]
     lane = iota((24, LANES), 1)
     row = iota((8, LANES), 0)
     top = [pltpu.roll(t[:24], turn[0], 1) for t in tiles]
@@ -70,7 +78,7 @@
         zs[slot, j, 16:24, :] = jnp.where(row < 4, upper[16:], lower[:8])
         zs[slot, j, 24:40, :] = lower[8:]
     weight = [
-        jnp.where(row < 4, taps[t, at], taps[TAPS + t, at]) for t in range(TAPS)
+        jnp.where(row < 4, table[t, at], table[TAPS + t, at]) for t in range(TAPS)
     ]
     slabs = []
     for k in range(LOOK_AZ):
@@ -96,22 +104,27 @@
     return jnp.sum(jnp.where(at, row, 0.0), axis=1, keepdims=True)
 
 
-def edge_kernel(meta, shifts, taps, own, near, far, partner, out0, out1, zs):
-    odd_date = meta[1]
-    local = column((partner[...] - meta[0]).astype(F32), 16, 36 - EXTRA)
+def edge_kernel(table, own, near, far, lines, out0, out1, zs):
+    odd_date = fact(table, 1)
+    local = column(partner_row(table, lines), 16, 36 - EXTRA)
     wide = out0.shape[1]
-    for out, base in ((out0, 9 - 9 * odd_date), (out1, 9 * odd_date)):
-        def one(i, _):
-            for part in range(2):
-                slabs = resample(own, near, far, meta, shifts, taps, part, base + i, zs, part)
-                for k in range(LOOK_AZ):
-                    for j, tile in enumerate(slabs[k]):
-                        at = pl.multiple_of(i * 80 + part * 40 + k * 8, 8)
-                        out[pl.ds(at, 8), LANES * j : LANES * (j + 1)] = tile
-            return 0
-
-        lax.fori_loop(0, HALF, one, 0, unroll=True)
-        out[240:256, :] = jnp.broadcast_to(local, (16, wide)).astype(BF16)
+    told = jnp.broadcast_to(local, (16, wide)).astype(BF16)
+    out0[240:256, :] = told
+    out1[240:256, :] = told
+
+    def one(n, _):
+        i, part = n // 2, n % 2
+        for out, base in ((out0, 9 - 9 * odd_date), (out1, 9 * odd_date)):
+            slabs = resample(
+                own, near, far, table, part, base + i, zs, 0 if out is out0 else 1
+            )
+            for k in range(LOOK_AZ):
+                for j, tile in enumerate(slabs[k]):
+                    at = pl.multiple_of(n * 40 + k * 8, 8)
+                    out[pl.ds(at, 8), LANES * j : LANES * (j + 1)] = tile
+        return 0
+
+    lax.fori_loop(0, 2 * HALF, one, 0)
 
 
 def window_matrix(depth):
@@ -162,8 +175,21 @@
     return take.astype(BF16)
 
 
+def phases_of(pairs, first, sums, powers_a, powers_b, pm):
+    def one(n, _):
+        for u in range(4):
+            c = 4 * n + u
+            rows = pl.ds(pl.multiple_of(c * 8, 8), 8)
+            row_a = pl.ds(pl.multiple_of(pairs[0, c] * 8, 8), 8)
+            row_b = pl.ds(pl.multiple_of(pairs[1, c] * 8, 8), 8)
+            pm[rows, :] = phase_of(sums[rows, :], powers_a[row_a, :], powers_b[row_b, :])
+        return 0
+
+    lax.fori_loop(0, first // 4, one, 0)
+
+
 def inner_kernel(
-    meta, shifts, taps, own, near, far, partner, names, inverse, rates, owners, cells,
+    table, pairs, own, near, far, lines, names, inverse, rates, owners, cells,
     phase_out, power_out, kept_out, weight_out, rates_out,
     zs, ys, ps, ss, pm,
 ):
@@ -172,7 +198,7 @@
 
     def one_date(d, _):
         for part in range(2):
-            slabs = resample(own, near, far, meta, shifts, taps, part, d, zs, part)
+            slabs = resample(own, near, far, table, part, d, zs, part)
             for k in range(LOOK_AZ):
                 for j, tile in enumerate(slabs[k]):
                     ys[d, part, 8 * k : 8 * k + 8, LANES * j : LANES * (j + 1)] = tile.astype(F32)
@@ -183,36 +209,37 @@
         ps[pl.ds(pl.multiple_of(d * 8, 8), 8), :] = power_sum(date)
         return 0
 
-    lax.fori_loop(0, 12, one_date, 0, unroll=2)
-    for d in range(9):
-        for part in range(2):
-            at = d * 80 + part * 40
-            kept_out[at : at + 40, :] = ys[d + 3, part].astype(BF16)
+    lax.fori_loop(0, 12, one_date, 0)
+
+    def keep(n, _):
+        at = pl.multiple_of(n * 80, 16)
+        kept_out[pl.ds(at, 80), :] = jnp.concatenate([ys[n + 3, 0], ys[n + 3, 1]], axis=0).astype(BF16)
+        return 0
+
+    lax.fori_loop(0, 9, keep, 0)
 
     def reader(d):
         return lambda part, k: ys[d, part, 8 * k : 8 * k + 8, :]
 
-    def one_first(a, _):
-        for s in range(SPAN):
-            at = pl.multiple_of((a * SPAN + s) * 8, 8)
-            ss[pl.ds(at, 8), :] = cross_sum(reader(a), reader(a + s + 1))
-        return 0
-
-    lax.fori_loop(0, 6, one_first, 0)
-    for c in range(36, len(INNER)):
-        a, b = INNER[c]
-        ss[c * 8 : c * 8 + 8, :] = cross_sum(reader(a), reader(b))
-    ss[len(INNER) * 8 :, :] = jnp.zeros_like(ss[len(INNER) * 8 :, :])
+    def one_pair(c, _):
+        at = pl.multiple_of(c * 8, 8)
+        ss[pl.ds(at, 8), :] = cross_sum(reader(pairs[0, c]), reader(pairs[1, c]))
+        return 0
+
+    total = ss.shape[0] // 8
+    lax.fori_loop(0, total, one_pair, 0)
     matrix = window_matrix(width)
     power_out[...] = window_sum(ps[...], matrix)
-    sums = window_sum(ss[...], matrix)
-    for c, (a, b) in enumerate(INNER):
-        rows = slice(8 * c, 8 * c + 8)
-        pm[rows, :] = phase_of(
-            sums[rows], power_out[8 * a : 8 * a + 8, :], power_out[8 * b : 8 * b + 8, :]
-        )
-    pm[len(INNER) * 8 :, :] = jnp.zeros_like(pm[len(INNER) * 8 :, :])
-    local = column((partner[...] - meta[0]).astype(F32), PAIR_ROWS, 0)
+    block = ss.shape[0] // 4
+
+    def one_block(n, _):
+        rows = pl.ds(pl.multiple_of(n * block, 8), block)
+        pm[rows, :] = window_sum(ss[rows, :], matrix)
+        return 0
+
+    lax.fori_loop(0, 4, one_block, 0)
+    phases_of(pairs, total, pm, power_out, power_out, pm)
+    local = column(partner_row(table, lines), PAIR_ROWS, 0)
     row = iota((PAIR_ROWS, 1), 0)
     have_a = jnp.where(row < 36, row // PER_DATE, -9).astype(F32)
     take = choose(names, have_a, local, True)
@@ -226,7 +253,7 @@
     rates_out[...] = jnp.broadcast_to(column(rates[...], DATES, 0), rates_out.shape)
 
     n = owners.shape[1]
-    spread = (iota((n, 256), 1) == iota((n, 256), 0) + n * meta[3]).astype(BF16)
+    spread = (iota((n, 256), 1) == iota((n, 256), 0) + n * fact(table, 3)).astype(BF16)
     codes = jnp.concatenate([owners[...], cells[...]], axis=0).astype(F32).astype(BF16)
     placed = jnp.dot(codes, spread, preferred_element_type=F32)
     lines = iota((PAIR_ROWS, 256), 0)
@@ -236,49 +263,52 @@
 
 
 def outer_kernel(
-    meta, got0, got1, kept, power, phase, partner, names, out, rs, ps, ss, pm
+    table, pairs, got0, got1, kept, power, phase, lines, names, out, rs, ps, ss, pm, pw
 ):
     width = got0.shape[1]
-    odd_date = meta[1]
-    after, before = 3 * odd_date, 3 - 3 * odd_date
-    for part in range(2):
-        for i in range(HALF):
-            at = i * 80 + part * 40
-            rs[i, part] = got0[at : at + 40, :].astype(F32)
-            rs[i + 3, part] = got1[at : at + 40, :].astype(F32)
-
-    def there(d):
+    odd_date = fact(table, 1)
+
+    def fill(n, _):
+        at = pl.multiple_of(n * 80, 16)
+        both = kept[pl.ds(at, 80), :].astype(F32)
+        rs[n, 0], rs[n, 1] = both[:40], both[40:]
+        return 0
+
+    lax.fori_loop(0, 9, fill, 0)
+
+    def fill_far(n, _):
+        at = pl.multiple_of(n * 80, 16)
+        one, two = got0[pl.ds(at, 80), :].astype(F32), got1[pl.ds(at, 80), :].astype(F32)
+        first = jnp.where(odd_date == 1, two, one)
+        second = jnp.where(odd_date == 1, one, two)
+        rs[n + 9, 0], rs[n + 9, 1] = first[:40], first[40:]
+        rs[n + 12, 0], rs[n + 12, 1] = second[:40], second[40:]
+        return 0
+
+    lax.fori_loop(0, HALF, fill_far, 0)
+
+    def reader(d):
         return lambda part, k: rs[d, part, 8 * k : 8 * k + 8, :]
 
-    def here(d):
-        def read(part, k):
-            at = (d - 3) * 80 + part * 40 + k * 8
-            return kept[at : at + 8, :].astype(F32)
-        return read
-
-    for i in range(HALF):
-        ps[8 * i : 8 * i + 8, :] = power_sum(there(after + i))
-        ps[24 + 8 * i : 32 + 8 * i, :] = power_sum(there(before + i))
-    for c, (a, b) in enumerate(CROSS):
-        ss[8 * c : 8 * c + 8, :] = cross_sum(here(a), there(after + b - 12))
-    for c, (a, b) in enumerate(BEFORE, len(CROSS)):
-        ss[8 * c : 8 * c + 8, :] = cross_sum(there(before + a - 9), here(b - 12))
+    def one_power(n, _):
+        ps[pl.ds(pl.multiple_of(n * 8, 8), 8), :] = power_sum(reader(n + 9))
+        return 0
+
+    lax.fori_loop(0, 2 * HALF, one_power, 0)
+
+    def one_pair(c, _):
+        at = pl.multiple_of(c * 8, 8)
+        ss[pl.ds(at, 8), :] = cross_sum(reader(pairs[0, c]), reader(pairs[1, c]))
+        return 0
+
+    total = ss.shape[0] // 8
+    lax.fori_loop(0, total, one_pair, 0)
     matrix = window_matrix(width)
-    powers = window_sum(ps[...], matrix)
-    last = 8 * (len(CROSS) + len(BEFORE))
-    ss[last:, :] = jnp.zeros_like(ss[last:, :])
-    sums = window_sum(ss[...], matrix)
-    for c, (a, b) in enumerate(CROSS + BEFORE):
-        rows = slice(8 * c, 8 * c + 8)
-        if c < len(CROSS):
-            pa = power[8 * a : 8 * a + 8, :]
-            pb = powers[8 * (b - 12) : 8 * (b - 12) + 8]
-        else:
-            pa = powers[24 + 8 * (a - 9) : 32 + 8 * (a - 9)]
-            pb = power[8 * (b - 12) : 8 * (b - 12) + 8, :]
-        pm[rows, :] = phase_of(sums[rows], pa, pb)
-    pm[last:, :] = jnp.zeros_like(pm[last:, :])
-    local = column((partner[...] - meta[0]).astype(F32), PAIR_ROWS, 0)
+    pw[0:72, :] = power[24:96, :]
+    pw[72:120, :] = window_sum(ps[...], matrix)
+    pm[...] = window_sum(ss[...], matrix)
+    phases_of(pairs, total, pm, pw, pw, pm)
+    local = column(partner_row(table, lines), PAIR_ROWS, 0)
     row = iota((PAIR_ROWS, 1), 0)
     told = jnp.where(odd_date == 1, got0[240:256, 0:LANES], got1[240:256, 0:LANES]).astype(F32)
     told = jnp.max(told, axis=1, keepdims=True)
@@ -295,7 +325,7 @@
         out[g] = total.astype(BF16)
 
 
-def series_kernel(meta, got, weight, rates, out):
+def series_kernel(table, got, weight, rates, out):
     stack = jnp.concatenate([got[g] for g in range(got.shape[0])], axis=0)
     series = jnp.dot(weight[...], stack, preferred_element_type=F32)
     wide = series.shape[1]
@@ -308,7 +338,7 @@
     for g in range(1, got.shape[0]):
         codes = codes + got[g, 40:48, :].astype(F32)
     owner, cell = codes[6:7, :], codes[7:8, :]
-    base = (meta[3] * 8).astype(F32)
+    base = table[2 * TAPS + 3, 3] * 8.0
     mine = (cell >= base) & (cell < base + 8)
     target = jnp.where(mine, owner * 8 + cell - base, -1.0).astype(jnp.int32)
     select = (iota((out.shape[0], wide), 0) == target).astype(BF16)
@@ -353,36 +383,52 @@
     return jnp.asarray(names)
 
 
+def pair_table(pairs, rows):
+    table = np.zeros((2, rows // 8), np.int32)
+    table[:, : len(pairs)] = np.array(pairs, np.int32).T
+    return jnp.asarray(table)
+
+
 def local(slc_stack, offsets, kernels, partner, inverse, rate_weights, owners, map_cell):
     date_count, width = slc_stack.shape[1], slc_stack.shape[3]
     groups, strips = lax.axis_size("date"), lax.axis_size("col")
     group, strip = lax.axis_index("date"), lax.axis_index("col")
-    meta = jnp.stack([group * date_count, group % 2, strip % 2, group]).astype(jnp.int32)
-    shifts = offsets.T
-    taps = jnp.transpose(kernels, (1, 2, 0)).reshape(2 * TAPS, DATES)
-    partner_row = partner.reshape(1, -1)
-
-    head, tail = slc_stack[..., :LANES], slc_stack[..., width - LANES :]
+    rows = [
+        jnp.transpose(kernels, (1, 2, 0)).reshape(2 * TAPS, DATES),
+        offsets.T.astype(F32),
+        jnp.pad(partner.reshape(1, -1).astype(F32), ((0, 0), (0, DATES - partner.shape[0]))),
+    ]
+    facts = jnp.stack([group * date_count, group % 2, strip % 2, group]).astype(F32)
+    rows.append(jnp.pad(facts.reshape(1, -1), ((0, 4), (0, DATES - 4))))
+    table, at = jnp.zeros((24, DATES), F32), 0
+    for part in rows:
+        table = table + jnp.pad(part, ((at, 24 - at - part.shape[0]), (0, 0)))
+        at += part.shape[0]
+
+    own = lax.reduce_precision(slc_stack, 8, 7)
+    head, tail = own[..., :LANES], own[..., width - LANES :]
     even = strip % 2 == 0
-    near = lax.ppermute(jnp.where(even, tail, head), "col", swaps(strips, 0))
-    far = lax.ppermute(jnp.where(even, head, tail), "col", swaps(strips, 1))
+    tile0, tile1 = jnp.where(even, tail, head), jnp.where(even, head, tail)
+    near = lax.ppermute(tile0, "col", swaps(strips, 0))
+    far = lax.ppermute(tile1, "col", swaps(strips, 1))
     scratch_z = pltpu.VMEM((2, width // LANES + 1, ROWS, LANES), F32)
     edge0, edge1 = call(
         edge_kernel,
-        (meta, shifts, taps),
-        (slc_stack, near, far, partner_row),
+        (table,),
+        (own, near, far, table),
         [((256, width), BF16)] * 2,
         [scratch_z],
     )
     got0 = lax.ppermute(edge0, "date", swaps(groups, 0))
     got1 = lax.ppermute(edge1, "date", swaps(groups, 1))
     inner_rows = 8 * (len(INNER) + 1)
-    outer_rows = 8 * (len(CROSS) + len(BEFORE) + 1)
+    outer_rows = 8 * (len(CROSS) + len(BEFORE) + 3)
+    outer_pairs = [(a - 3, b - 3) for a, b in CROSS] + [(a + 3, b - 15) for a, b in BEFORE]
     phase, power, kept, weight, rates = call(
         inner_kernel,
-        (meta, shifts, taps),
+        (table, pair_table(INNER, inner_rows)),
         (
-            slc_stack, near, far, partner_row, pair_names(INNER, inner_rows), inverse,
+            own, near, far, table, pair_names(INNER, inner_rows), inverse,
             rate_weights.reshape(1, -1), owners.reshape(1, -1), map_cell,
         ),
         [
@@ -402,18 +448,19 @@
     )
     (sent,) = call(
         outer_kernel,
-        (meta,),
-        (got0, got1, kept, power, phase, partner_row, pair_names(CROSS + BEFORE, outer_rows)),
+        (table, pair_table(outer_pairs, outer_rows)),
+        (got0, got1, kept, power, phase, table, pair_names(CROSS + BEFORE, outer_rows)),
         [((groups, PAIR_ROWS, 256), BF16)],
         [
-            pltpu.VMEM((6, 2, ROWS, width), F32),
+            pltpu.VMEM((15, 2, ROWS, width), F32),
             pltpu.VMEM((48, width), F32),
             pltpu.VMEM((outer_rows, width), F32),
             pltpu.VMEM((outer_rows, 256), F32),
+            pltpu.VMEM((120, 256), F32),
         ],
     )
     phases = lax.all_to_all(sent, "date", 0, 0, tiled=True)
-    (routed,) = call(series_kernel, (meta,), (phases, weight, rates), [((8 * strips, 256), BF16)])
+    (routed,) = call(series_kernel, (table,), (phases, weight, rates), [((8 * strips, 256), BF16)])
     parts = lax.all_to_all(routed.reshape(strips, 8, 256), "col", 0, 0, tiled=True)
     (mean,) = call(final_kernel, (), (parts,), [((8, DATES), F32)])
     return mean.reshape(1, 8, DATES)

time: 96.3 us -> 87 us (0.903)
  Pallas kernels: 28 us -> 19.7 us
  waiting for transfers between devices: 1.03 us -> 5.44 us
  blocking collectives: 50 us -> 46.2 us
  local copies, waits for them, and re-layouts: 3.37 us -> 0.06 us
  starting transfers between devices: 12 us -> 13.4 us
    pallas_call x5, Pallas kernels: 28 us -> 19.7 us  [call(): pl.pallas_call(kernel, in_specs=[SMEM] * len(smem) + [VMEM] * len(vmem),...]
    ppermute x2, waiting for transfers between devices: 1.03 us -> 5.43 us  [the longest x1 5.43 us: local(): far = lax.ppermute(tile1, 'col', swaps(strips, 1))]
    all_to_all x1, blocking collectives: 17 us -> 13.6 us  [local(): phases = lax.all_to_all(sent, 'date', 0, 0, tiled=True)]
    unnamed x20 -> x22, local copies, waits for them, and re-layouts: 3.37 us -> 0.06 us
    reduce_precision x0 -> x1, other arithmetic: none -> 1.43 us  [local(): own = lax.reduce_precision(slc_stack, 8, 7)]
    ppermute x2, starting transfers between devices: 9.44 us -> 10.8 us  [the longest x1 8.91 us: local(): near = lax.ppermute(tile0, 'col', swaps(strips, 0))]
    select_n x1, other arithmetic: 1.15 us -> 0.04 us  [local(): tile0, tile1 = (jnp.where(even, tail, head), jnp.where(even, head, tail))]
  transfers between devices with their start and end apart: 4 -> 4, of which waited for: 1 -> 1; matrix products, arithmetic and copies ran while one was open for 0% -> 0% of each run, Pallas kernels for 15% -> 12%
where the time goes in v3:
time: 87 us; the launch traced here: 86.7 us
  blocking collectives  46.2 us (53%)
  Pallas kernels  19.7 us (23%)
  starting transfers between devices  13.4 us (15%)
  waiting for transfers between devices  5.44 us (6%)
  other arithmetic  1.56 us (2%)
    all_to_all x1, blocking collectives, local(): lax.all_to_all(routed.reshape(strips, 8, 256), 'col', 0, 0, tiled=True)  32.6 us
    pallas_call x5, Pallas kernels, call(): pl.pallas_call(kernel, in_specs=[SMEM] * len(smem) + [VMEM] * len(vmem),...  19.7 us
    all_to_all x1, blocking collectives, local(): phases = lax.all_to_all(sent, 'date', 0, 0, tiled=True)  13.6 us
    ppermute x1, starting transfers between devices, local(): near = lax.ppermute(tile0, 'col', swaps(strips, 0))  8.91 us
    ppermute x1, waiting for transfers between devices, local(): far = lax.ppermute(tile1, 'col', swaps(strips, 1))  5.43 us
    ppermute x1, starting transfers between devices, local(): far = lax.ppermute(tile1, 'col', swaps(strips, 1))  1.92 us
    ppermute x1, starting transfers between devices, local(): got0 = lax.ppermute(edge0, 'date', swaps(groups, 0))  1.92 us
  transfers between devices with their start and end apart: 4, of which 1 were waited for; matrix products, arithmetic and copies ran while one was open for 0% of the time, Pallas kernels for 12%

profile of v3, /device:TPU:1, one launch (start us, length us, event | category | flops | bytes accessed | tf_op | source)
XLA Modules:
  0.0 86.7 jit_solution(7008904318010528182)
XLA Ops:
  0.0 1.4 %reduce_precision.3.own = bf16[2,12,40,640]{3,2,1,0:T(8,128)(2,1)S(1)} reduce-precision(bf16[2,12,40,640]{3,2,1,0:T(8,128)(2,1)} %param.12), exponent_bits=8, mantissa_bits=7 | non-fusion elementwise | flops 614400 | bytes 2457600 | tf_op jit(solution)/shard_map/reduce_precision | solution.py:408
  1.5 0.0 copy-start
  1.5 0.0 copy-start.1
  1.5 0.0 copy-start.3
  1.5 0.0 copy-start.5
  1.5 0.0 copy-start.6
  1.5 0.0 copy-start.7
  1.6 8.9 %collective-permute-start = (bf16[2,12,40,128]{3,2,1,0:T(8,128)(2,1)S(1)}, bf16[2,12,40,128]{3,2,1,0:T(8,128)(2,1)S(1)}, u32[]{:S(2)}, u32[]{:S(2)}) collective-permute-start(bf16[2,12,40,128]{3,2,1,0:T(8,128)(2,1)S(1)} %get-tuple-element.20), channel_id=1, source_target_pairs={{0,1},{1,0},{2,3},{3,2},{4,5},{5,4},{6,7},{7,6},{8,9},{9,8},{10,11... | collective-permute-start | bytes 737288 | tf_op jit(solution)/shard_map/ppermute | solution.py:412
  10.5 1.9 %collective-permute-start.1 = (bf16[2,12,40,128]{3,2,1,0:T(8,128)(2,1)S(1)}, bf16[2,12,40,128]{3,2,1,0:T(8,128)(2,1)S(1)}, u32[]{:S(2)}, u32[]{:S(2)}) collective-permute-start(bf16[2,12,40,128]{3,2,1,0:T(8,128)(2,1)S(1)} %get-tuple-element.19), channel_id=1, source_target_pairs={{1,2},{2,1},{3,4},{4,3},{5,6},{6,5},{7,8},{8,7},{9,10},{10,9},{11,... | collective-permute-start | bytes 737288 | tf_op jit(solution)/shard_map/ppermute | solution.py:413
  12.5 0.1 add_convert_fusion
  12.6 5.4 %collective-permute-done.1.far = bf16[2,12,40,128]{3,2,1,0:T(8,128)(2,1)S(1)} collective-permute-done((bf16[2,12,40,128]{3,2,1,0:T(8,128)(2,1)S(1)}, bf16[2,12,40,128]{3,2,1,0:T(8,128)(2,1)S(1)}, u32[]{:S(2)}, u32[]{:S(2)}) %collective-permute-start.1) | collective-permute-done | bytes 245792 | tf_op jit(solution)/shard_map/ppermute | solution.py:413
  18.0 3.9 %shard_map.118 = (bf16[256,640]{1,0:T(8,128)(2,1)S(1)}, bf16[256,640]{1,0:T(8,128)(2,1)S(1)}) custom-call(f32[24,192]{1,0:T(8,128)S(1)} %pad_add_fusion.table.lines, bf16[2,12,40,640]{3,2,1,0:T(8,128)(2,1)S(1)} %reduce_precision.3.own, bf16[2,12,40,128]{3,2,1,0:T(8,128)(2,1)S(1)} %collective-permute-done.near, ...), custom_call_target="tpu_custom_call" | custom-call | tf_op jit(solution)/shard_map/pallas_call | solution.py:364
  21.9 0.0 copy-start.2
  21.9 0.0 copy-start.4
  21.9 1.9 %collective-permute-start.2 = (bf16[256,640]{1,0:T(8,128)(2,1)S(1)}, bf16[256,640]{1,0:T(8,128)(2,1)S(1)}, u32[]{:S(2)}, u32[]{:S(2)}) collective-permute-start(bf16[256,640]{1,0:T(8,128)(2,1)S(1)} %get-tuple-element.12), channel_id=1, source_target_pairs={{0,32},{32,0},{64,96},{96,64},{128,160},{160,128},{192,224},{224,1... | collective-permute-start | bytes 983048 | tf_op jit(solution)/shard_map/ppermute | solution.py:422
  23.8 0.7 collective-permute-start.3
  24.6 10.6 %shard_map.119 = (f32[48,256]{1,0:T(8,128)S(1)}, f32[96,256]{1,0:T(8,128)S(1)}, bf16[720,640]{1,0:T(8,128)(2,1)S(1)}, bf16[192,768]{1,0:T(8,128)(2,1)S(1)}, f32[192,128]{1,0:T(8,128)S(1)}) custom-call(f32[24,192]{1,0:T(8,128)S(1)} %pad_add_fusion.table.lines, s32[2,52]{1,0:T(2,128)S(1)} %copy-done.5, bf16[2,12,40,640]{3,2,1,0:T(8,128)(2,1)S(1)} %reduce_precision.3.own, ...), custom_call_target="tpu_custom_call" | custom-call | tf_op jit(solution)/shard_map/pallas_call | solution.py:364
  35.2 0.0 collective-permute-done.2.got0
  35.2 0.0 collective-permute-done.3.got1
  35.2 3.1 %shard_map.120 = bf16[16,48,256]{2,1,0:T(8,128)(2,1)S(1)} custom-call(f32[24,192]{1,0:T(8,128)S(1)} %pad_add_fusion.table.lines, s32[2,24]{1,0:T(2,128)S(1)} %copy-done.4, bf16[256,640]{1,0:T(8,128)(2,1)S(1)} %collective-permute-done.2.got0, bf16[256,640]{1,0:T(8,128)(2,1)S(1)} %collective-permute-done.3.got1, bf16[720,640]{1,0:T(8,128)(2,1)S(1)} %get-tuple-element.14.kept, ...), custom_call_target="tpu_custom_call" | custom-call | tf_op jit(solution)/shard_map/pallas_call | solution.py:364
  38.4 13.6 %all_to_all.10.got = bf16[16,48,256]{2,1,0:T(8,128)(2,1)S(1)} all-to-all(bf16[16,48,256]{2,1,0:T(8,128)(2,1)S(1)} %shard_map.120), channel_id=1, replica_groups=mesh['date'=16,'col'=32] {'date'}, dimensions={0} | all-to-all | bytes 786432 | tf_op jit(solution)/shard_map/all_to_all | solution.py:462
  52.0 1.4 %shard_map.121 = bf16[256,256]{1,0:T(8,128)(2,1)S(1)} custom-call(f32[24,192]{1,0:T(8,128)S(1)} %pad_add_fusion.table.lines, bf16[16,48,256]{2,1,0:T(8,128)(2,1)S(1)} %all_to_all.10.got, bf16[192,768]{1,0:T(8,128)(2,1)S(1)} %get-tuple-element.17.weight, f32[192,128]{1,0:T(8,128)S(1)} %get-tuple-element.18.rates), custom_call_target="tpu_custom_call" | custom-call | tf_op jit(solution)/shard_map/pallas_call | solution.py:364
  53.4 32.6 %all_to_all.11.got = bf16[32,8,256]{2,1,0:T(8,128)(2,1)S(1)} all-to-all(bf16[32,8,256]{2,1,0:T(8,128)(2,1)S(1)} %bitcast.15), channel_id=1, replica_groups=mesh['date'=16,'col'=32] {'col'}, dimensions={0} | all-to-all | bytes 262144 | tf_op jit(solution)/shard_map/all_to_all | solution.py:464
  86.0 0.7 shard_map.122
  (19 shorter events, 0.1 us)
Async XLA Ops:
  0.0 12.4 %copy-start.9 = (s32[192,2]{0,1:T(2,128)S(1)}, s32[192,2]{0,1:T(2,128)}, u32[]{:S(2)}) copy-start(s32[192,2]{0,1:T(2,128)} %param.13) | copy-start | bytes 4612
  0.0 12.4 %copy-start.10 = (s32[36]{0:T(128)S(1)}, s32[36]{0:T(128)}, u32[]{:S(2)}) copy-start(s32[36]{0:T(128)} %param.15) | copy-start | bytes 436
  0.0 12.6 %copy-start.8 = (f32[192,2,8]{0,2,1:T(8,128)S(1)}, f32[192,2,8]{0,2,1:T(8,128)}, u32[]{:S(2)}) copy-start(f32[192,2,8]{0,2,1:T(8,128)} %param.14) | copy-start | bytes 36868
  1.5 23.1 %copy-start = (bf16[191,576]{1,0:T(8,128)(2,1)S(1)}, bf16[191,576]{1,0:T(8,128)(2,1)}, u32[]{:S(2)}) copy-start(bf16[191,576]{1,0:T(8,128)(2,1)} %inverse.1) | copy-start | bytes 660100
  1.5 23.1 %copy-start.1 = (f32[2,416]{1,0:T(2,128)S(1)}, f32[2,416]{1,0:T(2,128)}, u32[]{:S(2)}) copy-start(f32[2,416]{1,0:T(2,128)} %constant.42.clone.names) | copy-start | bytes 9988
  1.5 23.1 %copy-start.3 = (f32[191]{0:T(256)S(1)}, f32[191]{0:T(256)}, u32[]{:S(2)}) copy-start(f32[191]{0:T(256)} %param.17) | copy-start | bytes 2296
  1.5 23.1 %copy-start.5 = (s32[2,52]{1,0:T(2,128)S(1)}, s32[2,52]{1,0:T(2,128)}, u32[]{:S(2)}) copy-start(s32[2,52]{1,0:T(2,128)} %constant.41.clone.pairs) | copy-start | bytes 1252
  1.5 23.1 %copy-start.6 = (s32[1,16,1]{1,2,0:T(1,128)S(1)}, s32[1,16,1]{1,2,0:T(1,128)}, u32[]{:S(2)}) copy-start(s32[1,16,1]{1,2,0:T(1,128)} %param.18) | copy-start | bytes 196
  1.5 23.1 %copy-start.7 = (s32[1,16]{1,0:T(1,128)S(1)}, s32[1,16]{1,0:T(1,128)}, u32[]{:S(2)}) copy-start(s32[1,16]{1,0:T(1,128)} %cells.1) | copy-start | bytes 196
  1.6 11.0 %collective-permute-start = (bf16[2,12,40,128]{3,2,1,0:T(8,128)(2,1)S(1)}, bf16[2,12,40,128]{3,2,1,0:T(8,128)(2,1)S(1)}, u32[]{:S(2)}, u32[]{:S(2)}) collective-permute-start(bf16[2,12,40,128]{3,2,1,0:T(8,128)(2,1)S(1)} %get-tuple-element.20), channel_id=1, source_target_pairs={{0,1},{1,0},{2,3},{3,2},{4,5},{5,4},{6,7},{7,6},{8,9},{9,8},{10,11... | collective-permute-start | bytes 737288 | tf_op jit(solution)/shard_map/ppermute | solution.py:412
  10.5 7.5 %collective-permute-start.1 = (bf16[2,12,40,128]{3,2,1,0:T(8,128)(2,1)S(1)}, bf16[2,12,40,128]{3,2,1,0:T(8,128)(2,1)S(1)}, u32[]{:S(2)}, u32[]{:S(2)}) collective-permute-start(bf16[2,12,40,128]{3,2,1,0:T(8,128)(2,1)S(1)} %get-tuple-element.19), channel_id=1, source_target_pairs={{1,2},{2,1},{3,4},{4,3},{5,6},{6,5},{7,8},{8,7},{9,10},{10,9},{11,... | collective-permute-start | bytes 737288 | tf_op jit(solution)/shard_map/ppermute | solution.py:413
  21.9 13.3 %copy-start.2 = (f32[2,192]{1,0:T(2,128)S(1)}, f32[2,192]{1,0:T(2,128)}, u32[]{:S(2)}) copy-start(f32[2,192]{1,0:T(2,128)} %constant.44.clone.names) | copy-start | bytes 4612
  21.9 13.3 %copy-start.4 = (s32[2,24]{1,0:T(2,128)S(1)}, s32[2,24]{1,0:T(2,128)}, u32[]{:S(2)}) copy-start(s32[2,24]{1,0:T(2,128)} %constant.43.clone.pairs) | copy-start | bytes 580
  21.9 13.3 %collective-permute-start.2 = (bf16[256,640]{1,0:T(8,128)(2,1)S(1)}, bf16[256,640]{1,0:T(8,128)(2,1)S(1)}, u32[]{:S(2)}, u32[]{:S(2)}) collective-permute-start(bf16[256,640]{1,0:T(8,128)(2,1)S(1)} %get-tuple-element.12), channel_id=1, source_target_pairs={{0,32},{32,0},{64,96},{96,64},{128,160},{160,128},{192,224},{224,1... | collective-permute-start | bytes 983048 | tf_op jit(solution)/shard_map/ppermute | solution.py:422
  23.8 11.4 %collective-permute-start.3 = (bf16[256,640]{1,0:T(8,128)(2,1)S(1)}, bf16[256,640]{1,0:T(8,128)(2,1)S(1)}, u32[]{:S(2)}, u32[]{:S(2)}) collective-permute-start(bf16[256,640]{1,0:T(8,128)(2,1)S(1)} %get-tuple-element.13), channel_id=1, source_target_pairs={{32,64},{64,32},{96,128},{128,96},{160,192},{192,160},{224,256},{2... | collective-permute-start | bytes 983048 | tf_op jit(solution)/shard_map/ppermute | solution.py:423

commit v4 on v3

--- a/solution.py
+++ b/solution.py
@@ -13,6 +13,7 @@
 HALF = 3
 ROW_BLOCK = 20
 TAPS = 8
+HALO = 8
 LOOK_AZ = 5
 LOOK_RG = 20
 LROWS = 8
@@ -59,11 +60,12 @@
     first, odd = fact(table, 0), fact(table, 2)
     count = own.shape[-1] // LANES
     at = jnp.clip(first + date, 0, DATES - 1)
-    tile_a = near[part, date].astype(F32)
-    tile_b = far[part, date].astype(F32)
+    tile_a, tile_b = near[part].astype(F32), far[part].astype(F32)
     is_odd = odd == 1
-    left = jnp.where(is_odd, tile_a, tile_b)
-    right = jnp.where(is_odd, tile_b, tile_a)
+    left = pltpu.roll(jnp.where(is_odd, tile_a, tile_b), LANES - HALO - HALO * date, 1)
+    right = pltpu.roll(
+        jnp.where(is_odd, tile_b, tile_a), lax.rem(LANES - HALO * date, LANES), 1
+    )
     line = own[part, date].astype(F32)
     tiles = [left] + [line[:, LANES * j : LANES * (j + 1)] for j in range(count)] + [right]
     turn = [4 - table[2 * TAPS + b, at].astype(jnp.int32) for b in range(2)]
@@ -104,6 +106,27 @@
     return jnp.sum(jnp.where(at, row, 0.0), axis=1, keepdims=True)
 
 
+def pack_kernel(odd, own, out0, out1, acc):
+    far = own.shape[3] - LANES
+    even = odd[0] == 0
+    acc[...] = jnp.zeros_like(acc)
+
+    def one(d, _):
+        for part in range(2):
+            head = own[part, d, :, 0:LANES].astype(F32)
+            tail = own[part, d, :, far : far + LANES].astype(F32)
+            head = pltpu.roll(head, HALO * d, 1)
+            tail = pltpu.roll(tail, HALO * d + HALO, 1)
+            here = iota(head.shape, 1) // HALO == d
+            for n, tile in enumerate((jnp.where(even, tail, head), jnp.where(even, head, tail))):
+                acc[n, part] = jnp.where(here, tile, acc[n, part])
+        return 0
+
+    lax.fori_loop(0, own.shape[1], one, 0)
+    out0[...] = acc[0].astype(BF16)
+    out1[...] = acc[1].astype(BF16)
+
+
 def edge_kernel(table, own, near, far, lines, out0, out1, zs):
     odd_date = fact(table, 1)
     local = column(partner_row(table, lines), 16, 36 - EXTRA)
@@ -160,11 +183,10 @@
     return total
 
 
-def phase_of(cross, power_a, power_b):
-    mask = iota((8, 256), 1) // 32 == iota((8, 256), 0)
+def phase_of(cross, power_a, power_b, mask):
     scale = 1.0 / (LOOK_AZ * LOOK_RG)
-    value = (cross * scale) / jnp.sqrt((power_a * scale) * (power_b * scale) + 1e-06)
-    return jnp.where(mask, value, 0.0)
+    product = (power_a * scale) * (power_b * scale) + 1e-06
+    return jnp.where(mask, (cross * scale) * lax.rsqrt(product), 0.0)
 
 
 def choose(names, have_a, have_b, reverse):
@@ -175,23 +197,27 @@
     return take.astype(BF16)
 
 
-def phases_of(pairs, first, sums, powers_a, powers_b, pm):
+def phases_of(pairs, count, pm, powers):
+    mask = iota((8, 256), 1) // 32 == iota((8, 256), 0)
+
     def one(n, _):
-        for u in range(4):
-            c = 4 * n + u
+        done = []
+        for u in range(8):
+            c = 8 * n + u
             rows = pl.ds(pl.multiple_of(c * 8, 8), 8)
             row_a = pl.ds(pl.multiple_of(pairs[0, c] * 8, 8), 8)
             row_b = pl.ds(pl.multiple_of(pairs[1, c] * 8, 8), 8)
-            pm[rows, :] = phase_of(sums[rows, :], powers_a[row_a, :], powers_b[row_b, :])
-        return 0
-
-    lax.fori_loop(0, first // 4, one, 0)
+            done.append(phase_of(pm[rows, :], powers[row_a, :], powers[row_b, :], mask))
+        pm[pl.ds(pl.multiple_of(n * 64, 64), 64), :] = jnp.concatenate(done, axis=0)
+        return 0
+
+    lax.fori_loop(0, count // 8, one, 0)
 
 
 def inner_kernel(
-    table, pairs, own, near, far, lines, names, inverse, rates, owners, cells,
-    phase_out, power_out, kept_out, weight_out, rates_out,
-    zs, ys, ps, ss, pm,
+    table, pairs, own, near, far, lines, names, inverse, owners, cells,
+    phase_out, power_out, ys, weight_out,
+    zs, ps, ss, pm, gather,
 ):
     width = own.shape[-1]
     count = width // LANES
@@ -211,13 +237,6 @@
 
     lax.fori_loop(0, 12, one_date, 0)
 
-    def keep(n, _):
-        at = pl.multiple_of(n * 80, 16)
-        kept_out[pl.ds(at, 80), :] = jnp.concatenate([ys[n + 3, 0], ys[n + 3, 1]], axis=0).astype(BF16)
-        return 0
-
-    lax.fori_loop(0, 9, keep, 0)
-
     def reader(d):
         return lambda part, k: ys[d, part, 8 * k : 8 * k + 8, :]
 
@@ -238,7 +257,7 @@
         return 0
 
     lax.fori_loop(0, 4, one_block, 0)
-    phases_of(pairs, total, pm, power_out, power_out, pm)
+    phases_of(pairs, total, pm, power_out)
     local = column(partner_row(table, lines), PAIR_ROWS, 0)
     row = iota((PAIR_ROWS, 1), 0)
     have_a = jnp.where(row < 36, row // PER_DATE, -9).astype(F32)
@@ -247,10 +266,17 @@
     spots = iota((1, weight_out.shape[1]), 1)
     group, k = spots // PAIR_ROWS, spots % PAIR_ROWS
     target = jnp.where(k < 36, 36 * group + k, jnp.where(k < 45, 36 * group + k - 45, -1))
-    gather = (iota((inverse.shape[1], weight_out.shape[1]), 0) == target).astype(BF16)
-    weight_out[0:191, :] = jnp.dot(inverse[...], gather, preferred_element_type=F32).astype(BF16)
+
+    def one_rows(n, _):
+        at = pl.multiple_of(n * 16, 16)
+        gather[pl.ds(at, 16), :] = (iota((16, gather.shape[1]), 0) + at == target).astype(BF16)
+        return 0
+
+    lax.fori_loop(0, gather.shape[0] // 16, one_rows, 0)
+    weight_out[0:191, :] = jnp.dot(
+        inverse[...], gather[...], preferred_element_type=F32
+    ).astype(BF16)
     weight_out[191:192, :] = jnp.zeros((1, weight_out.shape[1]), BF16)
-    rates_out[...] = jnp.broadcast_to(column(rates[...], DATES, 0), rates_out.shape)
 
     n = owners.shape[1]
     spread = (iota((n, 256), 1) == iota((n, 256), 0) + n * fact(table, 3)).astype(BF16)
@@ -263,51 +289,54 @@
 
 
 def outer_kernel(
-    table, pairs, got0, got1, kept, power, phase, lines, names, out, rs, ps, ss, pm, pw
+    table, pairs, got0, got1, ys, power, phase, lines, names, out, rs, ps, ss, pm, pw
 ):
     width = got0.shape[1]
     odd_date = fact(table, 1)
-
-    def fill(n, _):
-        at = pl.multiple_of(n * 80, 16)
-        both = kept[pl.ds(at, 80), :].astype(F32)
-        rs[n, 0], rs[n, 1] = both[:40], both[40:]
-        return 0
-
-    lax.fori_loop(0, 9, fill, 0)
 
     def fill_far(n, _):
         at = pl.multiple_of(n * 80, 16)
         one, two = got0[pl.ds(at, 80), :].astype(F32), got1[pl.ds(at, 80), :].astype(F32)
         first = jnp.where(odd_date == 1, two, one)
         second = jnp.where(odd_date == 1, one, two)
-        rs[n + 9, 0], rs[n + 9, 1] = first[:40], first[40:]
-        rs[n + 12, 0], rs[n + 12, 1] = second[:40], second[40:]
+        rs[n, 0], rs[n, 1] = first[:40], first[40:]
+        rs[n + 3, 0], rs[n + 3, 1] = second[:40], second[40:]
         return 0
 
     lax.fori_loop(0, HALF, fill_far, 0)
 
-    def reader(d):
+    def here(d):
+        return lambda part, k: ys[d, part, 8 * k : 8 * k + 8, :]
+
+    def there(d):
         return lambda part, k: rs[d, part, 8 * k : 8 * k + 8, :]
 
     def one_power(n, _):
-        ps[pl.ds(pl.multiple_of(n * 8, 8), 8), :] = power_sum(reader(n + 9))
+        ps[pl.ds(pl.multiple_of(n * 8, 8), 8), :] = power_sum(there(n))
         return 0
 
     lax.fori_loop(0, 2 * HALF, one_power, 0)
 
-    def one_pair(c, _):
+    def one_after(c, _):
         at = pl.multiple_of(c * 8, 8)
-        ss[pl.ds(at, 8), :] = cross_sum(reader(pairs[0, c]), reader(pairs[1, c]))
+        ss[pl.ds(at, 8), :] = cross_sum(here(pairs[0, c]), there(pairs[1, c] - 12))
+        return 0
+
+    def one_before(c, _):
+        at = pl.multiple_of(c * 8, 8)
+        ss[pl.ds(at, 8), :] = cross_sum(there(pairs[0, c] - 12), here(pairs[1, c]))
         return 0
 
     total = ss.shape[0] // 8
-    lax.fori_loop(0, total, one_pair, 0)
+    lax.fori_loop(0, len(CROSS), one_after, 0)
+    lax.fori_loop(len(CROSS), len(CROSS) + len(BEFORE), one_before, 0)
+    last = 8 * (len(CROSS) + len(BEFORE))
+    ss[last:, :] = jnp.zeros_like(ss[last:, :])
     matrix = window_matrix(width)
-    pw[0:72, :] = power[24:96, :]
-    pw[72:120, :] = window_sum(ps[...], matrix)
+    pw[0:96, :] = power[...]
+    pw[96:144, :] = window_sum(ps[...], matrix)
     pm[...] = window_sum(ss[...], matrix)
-    phases_of(pairs, total, pm, pw, pw, pm)
+    phases_of(pairs, total, pm, pw)
     local = column(partner_row(table, lines), PAIR_ROWS, 0)
     row = iota((PAIR_ROWS, 1), 0)
     told = jnp.where(odd_date == 1, got0[240:256, 0:LANES], got1[240:256, 0:LANES]).astype(F32)
@@ -325,15 +354,12 @@
         out[g] = total.astype(BF16)
 
 
-def series_kernel(table, got, weight, rates, out):
+def series_kernel(table, got, weight, out):
     stack = jnp.concatenate([got[g] for g in range(got.shape[0])], axis=0)
     series = jnp.dot(weight[...], stack, preferred_element_type=F32)
     wide = series.shape[1]
-    turned = [series[:, :LANES] * rates[...], series[:, LANES:] * rates[...]]
-    velocity = jnp.sum(jnp.concatenate(turned, axis=1), axis=0, keepdims=True)
-    series = jnp.where(iota(series.shape, 0) == 191, velocity, series)
-    ones = jnp.where(iota((64, wide), 0) == 0, 1.0, 0.0)
-    rows = jnp.concatenate([series, ones], axis=0).astype(BF16)
+    rows = jnp.where(iota(series.shape, 0) == 191, 1.0, series)
+    rows = jnp.concatenate([rows, jnp.zeros((64, wide), F32)], axis=0).astype(BF16)
     codes = got[0, 40:48, :].astype(F32)
     for g in range(1, got.shape[0]):
         codes = codes + got[g, 40:48, :].astype(F32)
@@ -347,13 +373,16 @@
     ).astype(BF16)
 
 
-def final_kernel(got, out):
+def final_kernel(got, rates, out):
     total = got[0].astype(F32)
     for g in range(1, got.shape[0]):
         total = total + got[g].astype(F32)
-    counts = jnp.sum(jnp.where(iota(total.shape, 1) == 192, total, 0.0), axis=1, keepdims=True)
-    mean = total / jnp.maximum(counts, 1.0)
-    out[...] = mean[:, 0:192]
+    total = total[:, 0:DATES]
+    lane = iota(total.shape, 1)
+    counts = jnp.sum(jnp.where(lane == DATES - 1, total, 0.0), axis=1, keepdims=True)
+    velocity = jnp.sum(total * rates[...], axis=1, keepdims=True)
+    total = jnp.where(lane == DATES - 1, velocity, total)
+    out[...] = total / jnp.maximum(counts, 1.0)
 
 
 SMEM = pl.BlockSpec(memory_space=pltpu.SMEM)
@@ -406,9 +435,13 @@
         at += part.shape[0]
 
     own = lax.reduce_precision(slc_stack, 8, 7)
-    head, tail = own[..., :LANES], own[..., width - LANES :]
-    even = strip % 2 == 0
-    tile0, tile1 = jnp.where(even, tail, head), jnp.where(even, head, tail)
+    tile0, tile1 = call(
+        pack_kernel,
+        ((strip % 2).astype(jnp.int32).reshape(1),),
+        (own,),
+        [((2, ROWS, LANES), BF16)] * 2,
+        [pltpu.VMEM((2, 2, ROWS, LANES), F32)],
+    )
     near = lax.ppermute(tile0, "col", swaps(strips, 0))
     far = lax.ppermute(tile1, "col", swaps(strips, 1))
     scratch_z = pltpu.VMEM((2, width // LANES + 1, ROWS, LANES), F32)
@@ -421,48 +454,48 @@
     )
     got0 = lax.ppermute(edge0, "date", swaps(groups, 0))
     got1 = lax.ppermute(edge1, "date", swaps(groups, 1))
-    inner_rows = 8 * (len(INNER) + 1)
+    inner_rows = 8 * (len(INNER) + 5)
     outer_rows = 8 * (len(CROSS) + len(BEFORE) + 3)
-    outer_pairs = [(a - 3, b - 3) for a, b in CROSS] + [(a + 3, b - 15) for a, b in BEFORE]
-    phase, power, kept, weight, rates = call(
+    outer_pairs = CROSS + [(a + 6, b - 12) for a, b in BEFORE]
+    phase, power, ys, weight = call(
         inner_kernel,
         (table, pair_table(INNER, inner_rows)),
         (
             own, near, far, table, pair_names(INNER, inner_rows), inverse,
-            rate_weights.reshape(1, -1), owners.reshape(1, -1), map_cell,
+            owners.reshape(1, -1), map_cell,
         ),
         [
             ((PAIR_ROWS, 256), F32),
             ((96, 256), F32),
-            ((720, width), BF16),
+            ((12, 2, ROWS, width), F32),
             ((DATES, groups * PAIR_ROWS), BF16),
-            ((DATES, LANES), F32),
         ],
         [
             scratch_z,
-            pltpu.VMEM((12, 2, ROWS, width), F32),
             pltpu.VMEM((96, width), F32),
             pltpu.VMEM((inner_rows, width), F32),
             pltpu.VMEM((inner_rows, 256), F32),
+            pltpu.VMEM((inverse.shape[1], groups * PAIR_ROWS), BF16),
         ],
     )
     (sent,) = call(
         outer_kernel,
         (table, pair_table(outer_pairs, outer_rows)),
-        (got0, got1, kept, power, phase, table, pair_names(CROSS + BEFORE, outer_rows)),
+        (got0, got1, ys, power, phase, table, pair_names(CROSS + BEFORE, outer_rows)),
         [((groups, PAIR_ROWS, 256), BF16)],
         [
-            pltpu.VMEM((15, 2, ROWS, width), F32),
+            pltpu.VMEM((6, 2, ROWS, width), F32),
             pltpu.VMEM((48, width), F32),
             pltpu.VMEM((outer_rows, width), F32),
             pltpu.VMEM((outer_rows, 256), F32),
-            pltpu.VMEM((120, 256), F32),
+            pltpu.VMEM((144, 256), F32),
         ],
     )
     phases = lax.all_to_all(sent, "date", 0, 0, tiled=True)
-    (routed,) = call(series_kernel, (table,), (phases, weight, rates), [((8 * strips, 256), BF16)])
+    (routed,) = call(series_kernel, (table,), (phases, weight), [((8 * strips, 256), BF16)])
     parts = lax.all_to_all(routed.reshape(strips, 8, 256), "col", 0, 0, tiled=True)
-    (mean,) = call(final_kernel, (), (parts,), [((8, DATES), F32)])
+    rates = jnp.pad(rate_weights.reshape(1, -1), ((0, 0), (0, 1)))
+    (mean,) = call(final_kernel, (), (parts, rates), [((8, DATES), F32)])
     return mean.reshape(1, 8, DATES)
 
 

time: 87 us -> 87.3 us (level)
  blocking collectives: 46.2 us -> 13.6 us
  starting transfers between devices: 13.4 us -> 30.2 us
  waiting for transfers between devices: 5.44 us -> 18.8 us
  Pallas kernels: 19.7 us -> 22.5 us
    all_to_all x1 -> x0, blocking collectives: 32.6 us -> none  [local(): lax.all_to_all(routed.reshape(strips, 8, 256), 'col', 0, 0, tiled=True)]
    all_to_all x0 -> x1, starting transfers between devices: none -> 16.9 us  [local(): lax.all_to_all(routed.reshape(strips, 8, 256), 'col', 0, 0, tiled=True)]
    all_to_all x0 -> x1, waiting for transfers between devices: none -> 15.8 us  [local(): lax.all_to_all(routed.reshape(strips, 8, 256), 'col', 0, 0, tiled=True)]
    pallas_call x5 -> x6, Pallas kernels: 19.7 us -> 22.5 us  [call(): pl.pallas_call(kernel, in_specs=[SMEM] * len(smem) + [VMEM] * len(vmem),...]
    ppermute x1, waiting for transfers between devices: 5.43 us -> 2.98 us  [local(): far = lax.ppermute(tile1, 'col', swaps(strips, 1))]
  transfers between devices with their start and end apart: 4 -> 5, of which waited for: 1 -> 2; matrix products, arithmetic and copies ran while one was open for 0% -> 0% of each run, Pallas kernels for 12% -> 13%
where the time goes in v4:
time: 87.3 us; the launch traced here: 87 us
  starting transfers between devices  30.2 us (35%)
  Pallas kernels  22.5 us (26%)
  waiting for transfers between devices  18.8 us (22%)
  blocking collectives  13.6 us (16%)
  other arithmetic  1.49 us (2%)
    pallas_call x6, Pallas kernels, call(): pl.pallas_call(kernel, in_specs=[SMEM] * len(smem) + [VMEM] * len(vmem),...  22.5 us
    all_to_all x1, starting transfers between devices, local(): lax.all_to_all(routed.reshape(strips, 8, 256), 'col', 0, 0, tiled=True)  16.9 us
    all_to_all x1, waiting for transfers between devices, local(): lax.all_to_all(routed.reshape(strips, 8, 256), 'col', 0, 0, tiled=True)  15.8 us
    all_to_all x1, blocking collectives, local(): phases = lax.all_to_all(sent, 'date', 0, 0, tiled=True)  13.6 us
    ppermute x1, starting transfers between devices, local(): near = lax.ppermute(tile0, 'col', swaps(strips, 0))  8.79 us
    ppermute x1, waiting for transfers between devices, local(): far = lax.ppermute(tile1, 'col', swaps(strips, 1))  2.98 us
    ppermute x1, starting transfers between devices, local(): far = lax.ppermute(tile1, 'col', swaps(strips, 1))  1.92 us
    ppermute x1, starting transfers between devices, local(): got0 = lax.ppermute(edge0, 'date', swaps(groups, 0))  1.92 us
  transfers between devices with their start and end apart: 5, of which 2 were waited for; matrix products, arithmetic and copies ran while one was open for 0% of the time, Pallas kernels for 13%

profile of v4, /device:TPU:1, one launch (start us, length us, event | category | flops | bytes accessed | tf_op | source)
XLA Modules:
  0.0 87.0 jit_solution(13013351330504856399)
XLA Ops:
  0.0 1.4 %reduce_precision.3.own = bf16[2,12,40,640]{3,2,1,0:T(8,128)(2,1)S(1)} reduce-precision(bf16[2,12,40,640]{3,2,1,0:T(8,128)(2,1)} %param.12), exponent_bits=8, mantissa_bits=7 | non-fusion elementwise | flops 614400 | bytes 2457600 | tf_op jit(solution)/shard_map/reduce_precision | solution.py:437
  1.4 0.0 copy-start.10
  1.4 0.0 copy-start.7
  1.5 0.0 copy-start.1
  1.5 0.0 copy-start.3
  1.5 0.0 copy-start.5
  1.5 0.0 copy-start.6
  1.5 1.0 %shard_map.118 = (bf16[2,40,128]{2,1,0:T(8,128)(2,1)S(1)}, bf16[2,40,128]{2,1,0:T(8,128)(2,1)S(1)}) custom-call(s32[1]{0:T(128)} %bitcast.8.odd, bf16[2,12,40,640]{3,2,1,0:T(8,128)(2,1)S(1)} %reduce_precision.3.own), custom_call_target="tpu_custom_call" | custom-call | tf_op jit(solution)/shard_map/pallas_call | solution.py:393
  2.5 8.8 %collective-permute-start = (bf16[2,40,128]{2,1,0:T(8,128)(2,1)S(1)}, bf16[2,40,128]{2,1,0:T(8,128)(2,1)S(1)}, u32[]{:S(2)}, u32[]{:S(2)}) collective-permute-start(bf16[2,40,128]{2,1,0:T(8,128)(2,1)S(1)} %get-tuple-element.13), channel_id=1, source_target_pairs={{0,1},{1,0},{2,3},{3,2},{4,5},{5,4},{6,7},{7,6},{8,9},{9,8},{10,11... | collective-permute-start | bytes 61448 | tf_op jit(solution)/shard_map/ppermute | solution.py:445
  11.3 1.9 %collective-permute-start.1 = (bf16[2,40,128]{2,1,0:T(8,128)(2,1)S(1)}, bf16[2,40,128]{2,1,0:T(8,128)(2,1)S(1)}, u32[]{:S(2)}, u32[]{:S(2)}) collective-permute-start(bf16[2,40,128]{2,1,0:T(8,128)(2,1)S(1)} %get-tuple-element.14), channel_id=1, source_target_pairs={{1,2},{2,1},{3,4},{4,3},{5,6},{6,5},{7,8},{8,7},{9,10},{10,9},{11,... | collective-permute-start | bytes 61448 | tf_op jit(solution)/shard_map/ppermute | solution.py:446
  13.3 0.1 add_convert_fusion
  13.4 0.0 copy-start.2
  13.4 0.0 copy-start.4
  13.5 3.0 %collective-permute-done.1.far = bf16[2,40,128]{2,1,0:T(8,128)(2,1)S(1)} collective-permute-done((bf16[2,40,128]{2,1,0:T(8,128)(2,1)S(1)}, bf16[2,40,128]{2,1,0:T(8,128)(2,1)S(1)}, u32[]{:S(2)}, u32[]{:S(2)}) %collective-permute-start.1) | collective-permute-done | bytes 20512 | tf_op jit(solution)/shard_map/ppermute | solution.py:446
  16.4 4.4 %shard_map.119 = (bf16[256,640]{1,0:T(8,128)(2,1)S(1)}, bf16[256,640]{1,0:T(8,128)(2,1)S(1)}) custom-call(f32[24,192]{1,0:T(8,128)S(1)} %pad_add_fusion.table.lines, bf16[2,12,40,640]{3,2,1,0:T(8,128)(2,1)S(1)} %reduce_precision.3.own, bf16[2,40,128]{2,1,0:T(8,128)(2,1)S(1)} %collective-permute-done.near, ...), custom_call_target="tpu_custom_call" | custom-call | tf_op jit(solution)/shard_map/pallas_call | solution.py:393
  20.8 1.9 %collective-permute-start.2 = (bf16[256,640]{1,0:T(8,128)(2,1)S(1)}, bf16[256,640]{1,0:T(8,128)(2,1)S(1)}, u32[]{:S(2)}, u32[]{:S(2)}) collective-permute-start(bf16[256,640]{1,0:T(8,128)(2,1)S(1)} %get-tuple-element.15), channel_id=1, source_target_pairs={{0,32},{32,0},{64,96},{96,64},{128,160},{160,128},{192,224},{224,1... | collective-permute-start | bytes 983048 | tf_op jit(solution)/shard_map/ppermute | solution.py:455
  22.8 0.7 collective-permute-start.3
  23.5 11.5 %shard_map.120 = (f32[48,256]{1,0:T(8,128)S(1)}, f32[96,256]{1,0:T(8,128)S(1)}, f32[12,2,40,640]{3,2,1,0:T(8,128)S(1)}, bf16[192,768]{1,0:T(8,128)(2,1)S(1)}) custom-call(f32[24,192]{1,0:T(8,128)S(1)} %pad_add_fusion.table.lines, s32[2,56]{1,0:T(2,128)S(1)} %copy-done.3, bf16[2,12,40,640]{3,2,1,0:T(8,128)(2,1)S(1)} %reduce_precision.3.own, ...), custom_call_target="tpu_custom_call" | custom-call | tf_op jit(solution)/shard_map/pallas_call | solution.py:393
  35.0 2.8 %shard_map.121 = bf16[16,48,256]{2,1,0:T(8,128)(2,1)S(1)} custom-call(f32[24,192]{1,0:T(8,128)S(1)} %pad_add_fusion.table.lines, s32[2,24]{1,0:T(2,128)S(1)} %copy-done.4, bf16[256,640]{1,0:T(8,128)(2,1)S(1)} %collective-permute-done.2.got0, bf16[256,640]{1,0:T(8,128)(2,1)S(1)} %collective-permute-done.3.got1, f32[12,2,40,640]{3,2,1,0:T(8,128)S(1)} %get-tuple-element.17.ys, ...), custom_call_target="tpu_custom_call" | custom-call | tf_op jit(solution)/shard_map/pallas_call | solution.py:393
  37.9 13.6 %all_to_all.10.got = bf16[16,48,256]{2,1,0:T(8,128)(2,1)S(1)} all-to-all(bf16[16,48,256]{2,1,0:T(8,128)(2,1)S(1)} %shard_map.121), channel_id=1, replica_groups=mesh['date'=16,'col'=32] {'date'}, dimensions={0} | all-to-all | bytes 786432 | tf_op jit(solution)/shard_map/all_to_all | solution.py:494
  51.5 2.0 %shard_map.122 = bf16[256,256]{1,0:T(8,128)(2,1)} custom-call(f32[24,192]{1,0:T(8,128)S(1)} %pad_add_fusion.table.lines, bf16[16,48,256]{2,1,0:T(8,128)(2,1)S(1)} %all_to_all.10.got, bf16[192,768]{1,0:T(8,128)(2,1)S(1)} %get-tuple-element.20.weight), custom_call_target="tpu_custom_call" | custom-call | tf_op jit(solution)/shard_map/pallas_call | solution.py:393
  53.6 16.9 %all-to-all-start.1 = ((bf16[32,8,256]{2,1,0:T(8,128)(2,1)}), bf16[32,8,256]{2,1,0:T(8,128)(2,1)S(1)}, u32[]{:S(2)}, u32[]{:S(2)}) async-start(bf16[32,8,256]{2,1,0:T(8,128)(2,1)} %bitcast.10), calls=%async_computation.1 | async-start | bytes 262144 | tf_op jit(solution)/shard_map/all_to_all | solution.py:496
  70.5 15.8 %all-to-all-done.1.got = bf16[32,8,256]{2,1,0:T(8,128)(2,1)S(1)} async-done(((bf16[32,8,256]{2,1,0:T(8,128)(2,1)}), bf16[32,8,256]{2,1,0:T(8,128)(2,1)S(1)}, u32[]{:S(2)}, u32[]{:S(2)}) %all-to-all-start.1) | async-done | bytes 131104 | tf_op jit(solution)/shard_map/all_to_all | solution.py:496
  86.3 0.7 shard_map.123
  (21 shorter events, 0.1 us)
Async XLA Ops:
  1.4 11.9 %copy-start.10 = (s32[36]{0:T(128)S(1)}, s32[36]{0:T(128)}, u32[]{:S(2)}) copy-start(s32[36]{0:T(128)} %param.15) | copy-start | bytes 436
  1.4 11.9 %copy-start.8 = (s32[192,2]{0,1:T(2,128)S(1)}, s32[192,2]{0,1:T(2,128)}, u32[]{:S(2)}) copy-start(s32[192,2]{0,1:T(2,128)} %param.13) | copy-start | bytes 4612
  1.4 12.0 %copy-start.7 = (f32[192,2,8]{0,2,1:T(8,128)S(1)}, f32[192,2,8]{0,2,1:T(8,128)}, u32[]{:S(2)}) copy-start(f32[192,2,8]{0,2,1:T(8,128)} %param.14) | copy-start | bytes 36868
  1.4 22.0 %copy-start = (bf16[191,576]{1,0:T(8,128)(2,1)S(1)}, bf16[191,576]{1,0:T(8,128)(2,1)}, u32[]{:S(2)}) copy-start(bf16[191,576]{1,0:T(8,128)(2,1)} %inverse.1) | copy-start | bytes 660100
  1.5 22.0 %copy-start.1 = (f32[2,448]{1,0:T(2,128)S(1)}, f32[2,448]{1,0:T(2,128)}, u32[]{:S(2)}) copy-start(f32[2,448]{1,0:T(2,128)} %constant.42.clone.names) | copy-start | bytes 10756
  1.5 22.0 %copy-start.3 = (s32[2,56]{1,0:T(2,128)S(1)}, s32[2,56]{1,0:T(2,128)}, u32[]{:S(2)}) copy-start(s32[2,56]{1,0:T(2,128)} %constant.41.clone.pairs) | copy-start | bytes 1348
  1.5 22.0 %copy-start.5 = (s32[1,16,1]{1,2,0:T(1,128)S(1)}, s32[1,16,1]{1,2,0:T(1,128)}, u32[]{:S(2)}) copy-start(s32[1,16,1]{1,2,0:T(1,128)} %param.18) | copy-start | bytes 196
  1.5 22.0 %copy-start.6 = (s32[1,16]{1,0:T(1,128)S(1)}, s32[1,16]{1,0:T(1,128)}, u32[]{:S(2)}) copy-start(s32[1,16]{1,0:T(1,128)} %cells.1) | copy-start | bytes 196
  2.5 10.9 %collective-permute-start = (bf16[2,40,128]{2,1,0:T(8,128)(2,1)S(1)}, bf16[2,40,128]{2,1,0:T(8,128)(2,1)S(1)}, u32[]{:S(2)}, u32[]{:S(2)}) collective-permute-start(bf16[2,40,128]{2,1,0:T(8,128)(2,1)S(1)} %get-tuple-element.13), channel_id=1, source_target_pairs={{0,1},{1,0},{2,3},{3,2},{4,5},{5,4},{6,7},{7,6},{8,9},{9,8},{10,11... | collective-permute-start | bytes 61448 | tf_op jit(solution)/shard_map/ppermute | solution.py:445
  11.3 5.1 %collective-permute-start.1 = (bf16[2,40,128]{2,1,0:T(8,128)(2,1)S(1)}, bf16[2,40,128]{2,1,0:T(8,128)(2,1)S(1)}, u32[]{:S(2)}, u32[]{:S(2)}) collective-permute-start(bf16[2,40,128]{2,1,0:T(8,128)(2,1)S(1)} %get-tuple-element.14), channel_id=1, source_target_pairs={{1,2},{2,1},{3,4},{4,3},{5,6},{6,5},{7,8},{8,7},{9,10},{10,9},{11,... | collective-permute-start | bytes 61448 | tf_op jit(solution)/shard_map/ppermute | solution.py:446
  13.4 21.6 %copy-start.2 = (f32[2,192]{1,0:T(2,128)S(1)}, f32[2,192]{1,0:T(2,128)}, u32[]{:S(2)}) copy-start(f32[2,192]{1,0:T(2,128)} %constant.44.clone.names) | copy-start | bytes 4612
  13.4 21.6 %copy-start.4 = (s32[2,24]{1,0:T(2,128)S(1)}, s32[2,24]{1,0:T(2,128)}, u32[]{:S(2)}) copy-start(s32[2,24]{1,0:T(2,128)} %constant.43.clone.pairs) | copy-start | bytes 580
  20.8 14.1 %collective-permute-start.2 = (bf16[256,640]{1,0:T(8,128)(2,1)S(1)}, bf16[256,640]{1,0:T(8,128)(2,1)S(1)}, u32[]{:S(2)}, u32[]{:S(2)}) collective-permute-start(bf16[256,640]{1,0:T(8,128)(2,1)S(1)} %get-tuple-element.15), channel_id=1, source_target_pairs={{0,32},{32,0},{64,96},{96,64},{128,160},{160,128},{192,224},{224,1... | collective-permute-start | bytes 983048 | tf_op jit(solution)/shard_map/ppermute | solution.py:455
  22.8 12.2 %collective-permute-start.3 = (bf16[256,640]{1,0:T(8,128)(2,1)S(1)}, bf16[256,640]{1,0:T(8,128)(2,1)S(1)}, u32[]{:S(2)}, u32[]{:S(2)}) collective-permute-start(bf16[256,640]{1,0:T(8,128)(2,1)S(1)} %get-tuple-element.16), channel_id=1, source_target_pairs={{32,64},{64,32},{96,128},{128,96},{160,192},{192,160},{224,256},{2... | collective-permute-start | bytes 983048 | tf_op jit(solution)/shard_map/ppermute | solution.py:456
  37.9 32.6 %copy-start.9 = (f32[191]{0:T(256)S(1)}, f32[191]{0:T(256)}, u32[]{:S(2)}) copy-start(f32[191]{0:T(256)} %param.17) | copy-start | bytes 2296
  53.6 32.8 %all-to-all-start.1 = ((bf16[32,8,256]{2,1,0:T(8,128)(2,1)}), bf16[32,8,256]{2,1,0:T(8,128)(2,1)S(1)}, u32[]{:S(2)}, u32[]{:S(2)}) async-start(bf16[32,8,256]{2,1,0:T(8,128)(2,1)} %bitcast.10), calls=%async_computation.1 | async-start | bytes 262144 | tf_op jit(solution)/shard_map/all_to_all | solution.py:496

commit v5 on v4

--- a/solution.py
+++ b/solution.py
@@ -44,60 +44,73 @@
     return lines[2 * TAPS + 2 : 2 * TAPS + 3, 0:36] - table[2 * TAPS + 3, 0]
 
 
-def lane_left(tiles, by, keep):
-    lane = iota(tiles[0].shape, 1)
-    turned = [pltpu.roll(t, LANES - by, 1) for t in tiles]
-    out = [
-        jnp.where(lane < LANES - by, turned[j], turned[j + 1])
-        for j in range(len(tiles) - 1)
-    ]
-    if keep:
-        out.append(turned[-1])
-    return out
-
-
-def resample(own, near, far, table, part, date, zs, slot):
-    first, odd = fact(table, 0), fact(table, 2)
+def tap_weights(table, at, weights):
+    lane, row = iota((16, LANES), 1), iota((16, LANES), 0)
+    for b in range(2):
+        start = LANES + 4 - table[2 * TAPS + b, at].astype(jnp.int32)
+        line = jnp.zeros((8, LANES), F32)
+        for t in range(TAPS):
+            here = iota((8, LANES), 1) == lax.rem(start - t, LANES)
+            line = jnp.where(here, table[TAPS * b + t, at], line)
+        cols = slice(LANES * b, LANES * b + LANES)
+        for m in range(0, LANES, 16):
+            both = jnp.concatenate(
+                [pltpu.roll(line, m + 8 * i, 1, stride=1, stride_axis=0) for i in range(2)], axis=0
+            )
+            apart = lane - row - m
+            near = (apart < 64) & (apart > -64)
+            for at_row, tile in ((m, jnp.where(near, both, 0.0)), (LANES + m, jnp.where(near, 0.0, both))):
+                high = tile.astype(BF16)
+                weights[at_row : at_row + 16, cols] = high
+                weights[256 + at_row : 272 + at_row, cols] = (tile - high.astype(F32)).astype(BF16)
+
+
+def resample(own, near, far, table, dates, lhs, weights, zs):
+    is_odd = fact(table, 2) == 1
     count = own.shape[-1] // LANES
-    at = jnp.clip(first + date, 0, DATES - 1)
-    tile_a, tile_b = near[part].astype(F32), far[part].astype(F32)
-    is_odd = odd == 1
-    left = pltpu.roll(jnp.where(is_odd, tile_a, tile_b), LANES - HALO - HALO * date, 1)
-    right = pltpu.roll(
-        jnp.where(is_odd, tile_b, tile_a), lax.rem(LANES - HALO * date, LANES), 1
-    )
-    line = own[part, date].astype(F32)
-    tiles = [left] + [line[:, LANES * j : LANES * (j + 1)] for j in range(count)] + [right]
-    turn = [4 - table[2 * TAPS + b, at].astype(jnp.int32) for b in range(2)]
-    lane = iota((24, LANES), 1)
+    lane = iota((ROWS, LANES), 1)
+    for s, date in enumerate(dates):
+        tap_weights(table, jnp.clip(fact(table, 0) + date, 0, DATES - 1), weights.at[s])
+    for s, date in enumerate(dates):
+        for part in range(2):
+            tile_a, tile_b = near[part].astype(F32), far[part].astype(F32)
+            left = pltpu.roll(jnp.where(is_odd, tile_a, tile_b), LANES - HALO - HALO * date, 1)
+            right = pltpu.roll(
+                jnp.where(is_odd, tile_b, tile_a), lax.rem(LANES - HALO * date, LANES), 1
+            )
+            line = own[part, date].astype(F32)
+            tiles = [left] + [line[:, LANES * j : LANES * (j + 1)] for j in range(count)] + [right]
+            for j in range(count):
+                rows = slice(ROWS * (count * part + j), ROWS * (count * part + j + 1))
+                lhs[s, rows, 0:LANES] = own[part, date, :, LANES * j : LANES * (j + 1)]
+                lhs[s, rows, LANES : 2 * LANES] = jnp.where(
+                    lane < 64, tiles[j + 2], tiles[j]
+                ).astype(BF16)
     row = iota((8, LANES), 0)
-    top = [pltpu.roll(t[:24], turn[0], 1) for t in tiles]
-    low = [pltpu.roll(t[16:], turn[1], 1) for t in tiles]
-    for j in range(count + 1):
-        upper = jnp.where(lane < turn[0], top[j], top[j + 1])
-        lower = jnp.where(lane < turn[1], low[j], low[j + 1])
-        zs[slot, j, 0:16, :] = upper[:16]
-        zs[slot, j, 16:24, :] = jnp.where(row < 4, upper[16:], lower[:8])
-        zs[slot, j, 24:40, :] = lower[8:]
-    weight = [
-        jnp.where(row < 4, table[t, at], table[TAPS + t, at]) for t in range(TAPS)
-    ]
-    slabs = []
-    for k in range(LOOK_AZ):
-        z = [
-            zs[slot, j, pl.ds(k, LROWS, stride=LOOK_AZ), :] for j in range(count + 1)
-        ]
-        z1 = lane_left(z, 1, True)
-        a = [
-            [weight[2 * t] * z[j] + weight[2 * t + 1] * z1[j] for j in range(count + 1)]
-            for t in range(4)
-        ]
-        a1 = lane_left(a[1], 2, True)
-        a3 = lane_left(a[3], 2, True)
-        b0 = [a[0][j] + a1[j] for j in range(count + 1)]
-        b1 = lane_left([a[2][j] + a3[j] for j in range(count + 1)], 4, False)
-        slabs.append([(b0[j] + b1[j]).astype(BF16) for j in range(count)])
-    return slabs
+    outs = []
+    for s in range(len(dates)):
+        taken = lhs[s]
+        outs.append(
+            jnp.dot(
+                jnp.concatenate([taken, taken], axis=1), weights[s], preferred_element_type=F32
+            )
+        )
+    for s, out in enumerate(outs):
+        for part in range(2):
+            for j in range(count):
+                tile = out[ROWS * (count * part + j) : ROWS * (count * part + j + 1)]
+                first, second = tile[:, :LANES], tile[:, LANES:]
+                zs[s, part, j, 0:16, :] = first[:16]
+                zs[s, part, j, 16:24, :] = jnp.where(row < 4, first[16:24], second[16:24])
+                zs[s, part, j, 24:40, :] = second[24:]
+
+
+def slabs(zs, s):
+    for part in range(2):
+        for k in range(LOOK_AZ):
+            for j in range(zs.shape[2]):
+                tile = zs[s, part, j, pl.ds(k, LROWS, stride=LOOK_AZ), :].astype(BF16)
+                yield part, k, slice(LANES * j, LANES * (j + 1)), tile
 
 
 def column(row, rows, offset):
@@ -127,7 +140,7 @@
     out1[...] = acc[1].astype(BF16)
 
 
-def edge_kernel(table, own, near, far, lines, out0, out1, zs):
+def edge_kernel(table, own, near, far, lines, out0, out1, lhs, weights, zs):
     odd_date = fact(table, 1)
     local = column(partner_row(table, lines), 16, 36 - EXTRA)
     wide = out0.shape[1]
@@ -135,33 +148,24 @@
     out0[240:256, :] = told
     out1[240:256, :] = told
 
-    def one(n, _):
-        i, part = n // 2, n % 2
-        for out, base in ((out0, 9 - 9 * odd_date), (out1, 9 * odd_date)):
-            slabs = resample(
-                own, near, far, table, part, base + i, zs, 0 if out is out0 else 1
-            )
-            for k in range(LOOK_AZ):
-                for j, tile in enumerate(slabs[k]):
-                    at = pl.multiple_of(n * 40 + k * 8, 8)
-                    out[pl.ds(at, 8), LANES * j : LANES * (j + 1)] = tile
-        return 0
-
-    lax.fori_loop(0, 2 * HALF, one, 0)
-
-
-def window_matrix(depth):
-    col, lane = iota((depth, 256), 0), iota((depth, 256), 1)
-    start = (lane % 32) * LOOK_RG
-    return ((col >= start) & (col < start + LOOK_RG)).astype(BF16)
+    def one(i, _):
+        dates = (9 - 9 * odd_date + i, 9 * odd_date + i)
+        resample(own, near, far, table, dates, lhs, weights, zs)
+        for s, out in enumerate((out0, out1)):
+            for part, k, cols, tile in slabs(zs, s):
+                out[pl.ds(pl.multiple_of(i * 80 + part * 40 + k * 8, 8), 8), cols] = tile
+        return 0
+
+    lax.fori_loop(0, HALF, one, 0)
 
 
 def window_sum(values, matrix):
     high = values.astype(BF16)
     low = (values - high.astype(F32)).astype(BF16)
-    return jnp.dot(high, matrix, preferred_element_type=F32) + jnp.dot(
-        low, matrix, preferred_element_type=F32
+    both = jnp.dot(
+        jnp.concatenate([high, low], axis=0), matrix[...], preferred_element_type=F32
     )
+    return both[: values.shape[0]] + both[values.shape[0] :]
 
 
 def cross_sum(first, second):
@@ -214,31 +218,44 @@
     lax.fori_loop(0, count // 8, one, 0)
 
 
+def spread_dates(even, odd, parity, dates, first, second):
+    def one(n, _):
+        at = pl.multiple_of(n * 80, 16)
+        one, two = even[pl.ds(at, 80), :].astype(F32), odd[pl.ds(at, 80), :].astype(F32)
+        low, high = jnp.where(parity == 1, two, one), jnp.where(parity == 1, one, two)
+        dates[n + first, 0], dates[n + first, 1] = low[:40], low[40:]
+        dates[n + second, 0], dates[n + second, 1] = high[:40], high[40:]
+        return 0
+
+    lax.fori_loop(0, HALF, one, 0)
+
+
 def inner_kernel(
-    table, pairs, own, near, far, lines, names, inverse, owners, cells,
+    table, pairs, own, near, far, edge0, edge1, lines, matrix, names, inverse, owners, cells,
     phase_out, power_out, ys, weight_out,
-    zs, ps, ss, pm, gather,
+    lhs, weights, zs, ps, ss, pm, gather,
 ):
     width = own.shape[-1]
-    count = width // LANES
-
-    def one_date(d, _):
-        for part in range(2):
-            slabs = resample(own, near, far, table, part, d, zs, part)
-            for k in range(LOOK_AZ):
-                for j, tile in enumerate(slabs[k]):
-                    ys[d, part, 8 * k : 8 * k + 8, LANES * j : LANES * (j + 1)] = tile.astype(F32)
-
-        def date(part, k):
-            return ys[d, part, 8 * k : 8 * k + 8, :]
-
-        ps[pl.ds(pl.multiple_of(d * 8, 8), 8), :] = power_sum(date)
-        return 0
-
-    lax.fori_loop(0, 12, one_date, 0)
+
+    def one_date(n, _):
+        dates = (n + 3, n + 6)
+        resample(own, near, far, table, dates, lhs, weights, zs)
+        for s, d in enumerate(dates):
+            for part, k, cols, tile in slabs(zs, s):
+                ys[d, part, 8 * k : 8 * k + 8, cols] = tile.astype(F32)
+        return 0
+
+    lax.fori_loop(0, HALF, one_date, 0)
+    spread_dates(edge1, edge0, fact(table, 1), ys, 0, 9)
+
+    def one_power(d, _):
+        ps[pl.ds(pl.multiple_of(d * 8, 8), 8), :] = power_sum(reader(d))
+        return 0
 
     def reader(d):
         return lambda part, k: ys[d, part, 8 * k : 8 * k + 8, :]
+
+    lax.fori_loop(0, 12, one_power, 0)
 
     def one_pair(c, _):
         at = pl.multiple_of(c * 8, 8)
@@ -247,16 +264,15 @@
 
     total = ss.shape[0] // 8
     lax.fori_loop(0, total, one_pair, 0)
-    matrix = window_matrix(width)
     power_out[...] = window_sum(ps[...], matrix)
-    block = ss.shape[0] // 4
+    block = ss.shape[0] // 2
 
     def one_block(n, _):
         rows = pl.ds(pl.multiple_of(n * block, 8), block)
         pm[rows, :] = window_sum(ss[rows, :], matrix)
         return 0
 
-    lax.fori_loop(0, 4, one_block, 0)
+    lax.fori_loop(0, 2, one_block, 0)
     phases_of(pairs, total, pm, power_out)
     local = column(partner_row(table, lines), PAIR_ROWS, 0)
     row = iota((PAIR_ROWS, 1), 0)
@@ -289,21 +305,12 @@
 
 
 def outer_kernel(
-    table, pairs, got0, got1, ys, power, phase, lines, names, out, rs, ps, ss, pm, pw
+    table, pairs, got0, got1, ys, power, phase, lines, matrix, names, out, rs, ps, ss, pm, pw
 ):
     width = got0.shape[1]
     odd_date = fact(table, 1)
 
-    def fill_far(n, _):
-        at = pl.multiple_of(n * 80, 16)
-        one, two = got0[pl.ds(at, 80), :].astype(F32), got1[pl.ds(at, 80), :].astype(F32)
-        first = jnp.where(odd_date == 1, two, one)
-        second = jnp.where(odd_date == 1, one, two)
-        rs[n, 0], rs[n, 1] = first[:40], first[40:]
-        rs[n + 3, 0], rs[n + 3, 1] = second[:40], second[40:]
-        return 0
-
-    lax.fori_loop(0, HALF, fill_far, 0)
+    spread_dates(got0, got1, odd_date, rs, 0, 3)
 
     def here(d):
         return lambda part, k: ys[d, part, 8 * k : 8 * k + 8, :]
@@ -332,7 +339,6 @@
     lax.fori_loop(len(CROSS), len(CROSS) + len(BEFORE), one_before, 0)
     last = 8 * (len(CROSS) + len(BEFORE))
     ss[last:, :] = jnp.zeros_like(ss[last:, :])
-    matrix = window_matrix(width)
     pw[0:96, :] = power[...]
     pw[96:144, :] = window_sum(ps[...], matrix)
     pm[...] = window_sum(ss[...], matrix)
@@ -444,16 +450,22 @@
     )
     near = lax.ppermute(tile0, "col", swaps(strips, 0))
     far = lax.ppermute(tile1, "col", swaps(strips, 1))
-    scratch_z = pltpu.VMEM((2, width // LANES + 1, ROWS, LANES), F32)
+    scratch = [
+        pltpu.VMEM((2, 2 * ROWS * width // LANES, 2 * LANES), BF16),
+        pltpu.VMEM((2, 4 * LANES, 2 * LANES), BF16),
+        pltpu.VMEM((2, 2, width // LANES, ROWS, LANES), F32),
+    ]
     edge0, edge1 = call(
         edge_kernel,
         (table,),
         (own, near, far, table),
         [((256, width), BF16)] * 2,
-        [scratch_z],
+        scratch,
     )
     got0 = lax.ppermute(edge0, "date", swaps(groups, 0))
     got1 = lax.ppermute(edge1, "date", swaps(groups, 1))
+    window = np.arange(width)[:, None] // LOOK_RG == np.arange(256)[None, :] % (width // LOOK_RG)
+    matrix = jnp.asarray(window.astype(np.float32)).astype(BF16)
     inner_rows = 8 * (len(INNER) + 5)
     outer_rows = 8 * (len(CROSS) + len(BEFORE) + 3)
     outer_pairs = CROSS + [(a + 6, b - 12) for a, b in BEFORE]
@@ -461,7 +473,7 @@
         inner_kernel,
         (table, pair_table(INNER, inner_rows)),
         (
-            own, near, far, table, pair_names(INNER, inner_rows), inverse,
+            own, near, far, edge0, edge1, table, matrix, pair_names(INNER, inner_rows), inverse,
             owners.reshape(1, -1), map_cell,
         ),
         [
@@ -470,8 +482,8 @@
             ((12, 2, ROWS, width), F32),
             ((DATES, groups * PAIR_ROWS), BF16),
         ],
-        [
-            scratch_z,
+        scratch
+        + [
             pltpu.VMEM((96, width), F32),
             pltpu.VMEM((inner_rows, width), F32),
             pltpu.VMEM((inner_rows, 256), F32),
@@ -481,7 +493,7 @@
     (sent,) = call(
         outer_kernel,
         (table, pair_table(outer_pairs, outer_rows)),
-        (got0, got1, ys, power, phase, table, pair_names(CROSS + BEFORE, outer_rows)),
+        (got0, got1, ys, power, phase, table, matrix, pair_names(CROSS + BEFORE, outer_rows)),
         [((groups, PAIR_ROWS, 256), BF16)],
         [
             pltpu.VMEM((6, 2, ROWS, width), F32),

time: 87.3 us -> 83.7 us (0.959)
  Pallas kernels: 22.5 us -> 16.8 us
  starting transfers between devices: 30.2 us -> 32.2 us
    pallas_call x6, Pallas kernels: 22.5 us -> 16.8 us  [call(): pl.pallas_call(kernel, in_specs=[SMEM] * len(smem) + [VMEM] * len(vmem),...]
    all_to_all x1, starting transfers between devices: 16.9 us -> 18.9 us  [local(): lax.all_to_all(routed.reshape(strips, 8, 256), 'col', 0, 0, tiled=True)]
  transfers between devices with their start and end apart: 5 -> 5, of which waited for: 2 -> 2; matrix products, arithmetic and copies ran while one was open for 0% -> 0% of each run, Pallas kernels for 13% -> 9%
where the time goes in v5:
time: 83.7 us; the launch traced here: 83.4 us
  starting transfers between devices  32.2 us (38%)
  waiting for transfers between devices  18.8 us (22%)
  Pallas kernels  16.8 us (20%)
  blocking collectives  13.6 us (16%)
  other arithmetic  1.49 us (2%)
    all_to_all x1, starting transfers between devices, local(): lax.all_to_all(routed.reshape(strips, 8, 256), 'col', 0, 0, tiled=True)  18.9 us
    pallas_call x6, Pallas kernels, call(): pl.pallas_call(kernel, in_specs=[SMEM] * len(smem) + [VMEM] * len(vmem),...  16.8 us
    all_to_all x1, waiting for transfers between devices, local(): lax.all_to_all(routed.reshape(strips, 8, 256), 'col', 0, 0, tiled=True)  15.8 us
    all_to_all x1, blocking collectives, local(): phases = lax.all_to_all(sent, 'date', 0, 0, tiled=True)  13.6 us
    ppermute x1, starting transfers between devices, local(): near = lax.ppermute(tile0, 'col', swaps(strips, 0))  8.79 us
    ppermute x1, waiting for transfers between devices, local(): far = lax.ppermute(tile1, 'col', swaps(strips, 1))  3.01 us
    ppermute x1, starting transfers between devices, local(): far = lax.ppermute(tile1, 'col', swaps(strips, 1))  1.92 us
    ppermute x1, starting transfers between devices, local(): got0 = lax.ppermute(edge0, 'date', swaps(groups, 0))  1.92 us
  transfers between devices with their start and end apart: 5, of which 2 were waited for; matrix products, arithmetic and copies ran while one was open for 0% of the time, Pallas kernels for 9%

profile of v5, /device:TPU:1, one launch (start us, length us, event | category | flops | bytes accessed | tf_op | source)
XLA Modules:
  0.0 83.4 jit_solution(16067465553718892503)
XLA Ops:
  0.0 1.4 %reduce_precision.3.own = bf16[2,12,40,640]{3,2,1,0:T(8,128)(2,1)S(1)} reduce-precision(bf16[2,12,40,640]{3,2,1,0:T(8,128)(2,1)} %param.13), exponent_bits=8, mantissa_bits=7 | non-fusion elementwise | flops 614400 | bytes 2457600 | tf_op jit(solution)/shard_map/reduce_precision | solution.py:443
  1.4 0.0 copy-start.9
  1.4 0.0 copy-start.8
  1.4 0.0 copy-start
  1.5 0.0 copy-start.1
  1.5 0.0 copy-start.2
  1.5 0.0 copy-start.4
  1.5 1.0 %shard_map.127 = (bf16[2,40,128]{2,1,0:T(8,128)(2,1)S(1)}, bf16[2,40,128]{2,1,0:T(8,128)(2,1)S(1)}) custom-call(s32[1]{0:T(128)} %bitcast.8.odd, bf16[2,12,40,640]{3,2,1,0:T(8,128)(2,1)S(1)} %reduce_precision.3.own), custom_call_target="tpu_custom_call" | custom-call | tf_op jit(solution)/shard_map/pallas_call | solution.py:399
  2.6 8.8 %collective-permute-start = (bf16[2,40,128]{2,1,0:T(8,128)(2,1)S(1)}, bf16[2,40,128]{2,1,0:T(8,128)(2,1)S(1)}, u32[]{:S(2)}, u32[]{:S(2)}) collective-permute-start(bf16[2,40,128]{2,1,0:T(8,128)(2,1)S(1)} %get-tuple-element.13), channel_id=1, source_target_pairs={{0,1},{1,0},{2,3},{3,2},{4,5},{5,4},{6,7},{7,6},{8,9},{9,8},{10,11... | collective-permute-start | bytes 61448 | tf_op jit(solution)/shard_map/ppermute | solution.py:451
  11.3 1.9 %collective-permute-start.1 = (bf16[2,40,128]{2,1,0:T(8,128)(2,1)S(1)}, bf16[2,40,128]{2,1,0:T(8,128)(2,1)S(1)}, u32[]{:S(2)}, u32[]{:S(2)}) collective-permute-start(bf16[2,40,128]{2,1,0:T(8,128)(2,1)S(1)} %get-tuple-element.14), channel_id=1, source_target_pairs={{1,2},{2,1},{3,4},{4,3},{5,6},{6,5},{7,8},{8,7},{9,10},{10,9},{11,... | collective-permute-start | bytes 61448 | tf_op jit(solution)/shard_map/ppermute | solution.py:452
  13.3 0.1 add_convert_fusion
  13.4 3.0 %collective-permute-done.1.far = bf16[2,40,128]{2,1,0:T(8,128)(2,1)S(1)} collective-permute-done((bf16[2,40,128]{2,1,0:T(8,128)(2,1)S(1)}, bf16[2,40,128]{2,1,0:T(8,128)(2,1)S(1)}, u32[]{:S(2)}, u32[]{:S(2)}) %collective-permute-start.1) | collective-permute-done | bytes 20512 | tf_op jit(solution)/shard_map/ppermute | solution.py:452
  16.4 3.1 %shard_map.128 = (bf16[256,640]{1,0:T(8,128)(2,1)S(1)}, bf16[256,640]{1,0:T(8,128)(2,1)S(1)}) custom-call(f32[24,192]{1,0:T(8,128)S(1)} %pad_add_fusion.table.lines, bf16[2,12,40,640]{3,2,1,0:T(8,128)(2,1)S(1)} %reduce_precision.3.own, bf16[2,40,128]{2,1,0:T(8,128)(2,1)S(1)} %collective-permute-done.near, ...), custom_call_target="tpu_custom_call" | custom-call | tf_op jit(solution)/shard_map/pallas_call | solution.py:399
  19.5 1.9 %collective-permute-start.2 = (bf16[256,640]{1,0:T(8,128)(2,1)S(1)}, bf16[256,640]{1,0:T(8,128)(2,1)S(1)}, u32[]{:S(2)}, u32[]{:S(2)}) collective-permute-start(bf16[256,640]{1,0:T(8,128)(2,1)S(1)} %get-tuple-element.15.edge0), channel_id=1, source_target_pairs={{0,32},{32,0},{64,96},{96,64},{128,160},{160,128},{192,224},{224,1... | collective-permute-start | bytes 983048 | tf_op jit(solution)/shard_map/ppermute | solution.py:465
  21.5 0.7 collective-permute-start.3
  22.2 0.0 copy-start.3
  22.2 0.0 copy-start.5
  22.2 7.1 %shard_map.129 = (f32[48,256]{1,0:T(8,128)S(1)}, f32[96,256]{1,0:T(8,128)S(1)}, f32[12,2,40,640]{3,2,1,0:T(8,128)S(1)}, bf16[192,768]{1,0:T(8,128)(2,1)S(1)}) custom-call(f32[24,192]{1,0:T(8,128)S(1)} %pad_add_fusion.table.lines, s32[2,56]{1,0:T(2,128)S(1)} %copy-done.4, bf16[2,12,40,640]{3,2,1,0:T(8,128)(2,1)S(1)} %reduce_precision.3.own, ...), custom_call_target="tpu_custom_call" | custom-call | tf_op jit(solution)/shard_map/pallas_call | solution.py:399
  29.4 2.8 %shard_map.130 = bf16[16,48,256]{2,1,0:T(8,128)(2,1)S(1)} custom-call(f32[24,192]{1,0:T(8,128)S(1)} %pad_add_fusion.table.lines, s32[2,24]{1,0:T(2,128)S(1)} %copy-done.5, bf16[256,640]{1,0:T(8,128)(2,1)S(1)} %collective-permute-done.2.got0, bf16[256,640]{1,0:T(8,128)(2,1)S(1)} %collective-permute-done.3.got1, f32[12,2,40,640]{3,2,1,0:T(8,128)S(1)} %get-tuple-element.17.ys, ...), custom_call_target="tpu_custom_call" | custom-call | tf_op jit(solution)/shard_map/pallas_call | solution.py:399
  32.2 13.6 %all_to_all.10.got = bf16[16,48,256]{2,1,0:T(8,128)(2,1)S(1)} all-to-all(bf16[16,48,256]{2,1,0:T(8,128)(2,1)S(1)} %shard_map.130), channel_id=1, replica_groups=mesh['date'=16,'col'=32] {'date'}, dimensions={0} | all-to-all | bytes 786432 | tf_op jit(solution)/shard_map/all_to_all | solution.py:506
  45.8 2.0 %shard_map.131 = bf16[256,256]{1,0:T(8,128)(2,1)} custom-call(f32[24,192]{1,0:T(8,128)S(1)} %pad_add_fusion.table.lines, bf16[16,48,256]{2,1,0:T(8,128)(2,1)S(1)} %all_to_all.10.got, bf16[192,768]{1,0:T(8,128)(2,1)S(1)} %get-tuple-element.20.weight), custom_call_target="tpu_custom_call" | custom-call | tf_op jit(solution)/shard_map/pallas_call | solution.py:399
  47.9 18.9 %all-to-all-start.1 = ((bf16[32,8,256]{2,1,0:T(8,128)(2,1)}), bf16[32,8,256]{2,1,0:T(8,128)(2,1)S(1)}, u32[]{:S(2)}, u32[]{:S(2)}) async-start(bf16[32,8,256]{2,1,0:T(8,128)(2,1)} %bitcast.10), calls=%async_computation.1 | async-start | bytes 262144 | tf_op jit(solution)/shard_map/all_to_all | solution.py:508
  66.8 15.8 %all-to-all-done.1.got = bf16[32,8,256]{2,1,0:T(8,128)(2,1)S(1)} async-done(((bf16[32,8,256]{2,1,0:T(8,128)(2,1)}), bf16[32,8,256]{2,1,0:T(8,128)(2,1)S(1)}, u32[]{:S(2)}, u32[]{:S(2)}) %all-to-all-start.1) | async-done | bytes 131104 | tf_op jit(solution)/shard_map/all_to_all | solution.py:508
  82.7 0.7 shard_map.132
  (23 shorter events, 0.1 us)
Async XLA Ops:
  1.4 11.9 %copy-start.9 = (s32[192,2]{0,1:T(2,128)S(1)}, s32[192,2]{0,1:T(2,128)}, u32[]{:S(2)}) copy-start(s32[192,2]{0,1:T(2,128)} %param.14) | copy-start | bytes 4612
  1.4 11.9 %copy-start.11 = (s32[36]{0:T(128)S(1)}, s32[36]{0:T(128)}, u32[]{:S(2)}) copy-start(s32[36]{0:T(128)} %param.16) | copy-start | bytes 436
  1.4 12.0 %copy-start.8 = (f32[192,2,8]{0,2,1:T(8,128)S(1)}, f32[192,2,8]{0,2,1:T(8,128)}, u32[]{:S(2)}) copy-start(f32[192,2,8]{0,2,1:T(8,128)} %param.15) | copy-start | bytes 36868
  1.4 20.7 %copy-start = (bf16[640,256]{1,0:T(8,128)(2,1)S(1)}, bf16[640,256]{1,0:T(8,128)(2,1)}, u32[]{:S(2)}) copy-start(bf16[640,256]{1,0:T(8,128)(2,1)} %constant.66.matrix) | copy-start | bytes 983044
  1.5 20.7 %copy-start.1 = (bf16[191,576]{1,0:T(8,128)(2,1)S(1)}, bf16[191,576]{1,0:T(8,128)(2,1)}, u32[]{:S(2)}) copy-start(bf16[191,576]{1,0:T(8,128)(2,1)} %inverse.1) | copy-start | bytes 660100
  1.5 20.7 %copy-start.2 = (f32[2,448]{1,0:T(2,128)S(1)}, f32[2,448]{1,0:T(2,128)}, u32[]{:S(2)}) copy-start(f32[2,448]{1,0:T(2,128)} %constant.45.clone.names) | copy-start | bytes 10756
  1.5 20.7 %copy-start.4 = (s32[2,56]{1,0:T(2,128)S(1)}, s32[2,56]{1,0:T(2,128)}, u32[]{:S(2)}) copy-start(s32[2,56]{1,0:T(2,128)} %constant.44.clone.pairs) | copy-start | bytes 1348
  1.5 20.7 %copy-start.6 = (s32[1,16,1]{1,2,0:T(1,128)S(1)}, s32[1,16,1]{1,2,0:T(1,128)}, u32[]{:S(2)}) copy-start(s32[1,16,1]{1,2,0:T(1,128)} %param.19) | copy-start | bytes 196
  1.5 20.7 %copy-start.7 = (s32[1,16]{1,0:T(1,128)S(1)}, s32[1,16]{1,0:T(1,128)}, u32[]{:S(2)}) copy-start(s32[1,16]{1,0:T(1,128)} %cells.1) | copy-start | bytes 196
  2.6 10.9 %collective-permute-start = (bf16[2,40,128]{2,1,0:T(8,128)(2,1)S(1)}, bf16[2,40,128]{2,1,0:T(8,128)(2,1)S(1)}, u32[]{:S(2)}, u32[]{:S(2)}) collective-permute-start(bf16[2,40,128]{2,1,0:T(8,128)(2,1)S(1)} %get-tuple-element.13), channel_id=1, source_target_pairs={{0,1},{1,0},{2,3},{3,2},{4,5},{5,4},{6,7},{7,6},{8,9},{9,8},{10,11... | collective-permute-start | bytes 61448 | tf_op jit(solution)/shard_map/ppermute | solution.py:451
  11.3 5.1 %collective-permute-start.1 = (bf16[2,40,128]{2,1,0:T(8,128)(2,1)S(1)}, bf16[2,40,128]{2,1,0:T(8,128)(2,1)S(1)}, u32[]{:S(2)}, u32[]{:S(2)}) collective-permute-start(bf16[2,40,128]{2,1,0:T(8,128)(2,1)S(1)} %get-tuple-element.14), channel_id=1, source_target_pairs={{1,2},{2,1},{3,4},{4,3},{5,6},{6,5},{7,8},{8,7},{9,10},{10,9},{11,... | collective-permute-start | bytes 61448 | tf_op jit(solution)/shard_map/ppermute | solution.py:452
  19.5 9.9 %collective-permute-start.2 = (bf16[256,640]{1,0:T(8,128)(2,1)S(1)}, bf16[256,640]{1,0:T(8,128)(2,1)S(1)}, u32[]{:S(2)}, u32[]{:S(2)}) collective-permute-start(bf16[256,640]{1,0:T(8,128)(2,1)S(1)} %get-tuple-element.15.edge0), channel_id=1, source_target_pairs={{0,32},{32,0},{64,96},{96,64},{128,160},{160,128},{192,224},{224,1... | collective-permute-start | bytes 983048 | tf_op jit(solution)/shard_map/ppermute | solution.py:465
  21.5 7.9 %collective-permute-start.3 = (bf16[256,640]{1,0:T(8,128)(2,1)S(1)}, bf16[256,640]{1,0:T(8,128)(2,1)S(1)}, u32[]{:S(2)}, u32[]{:S(2)}) collective-permute-start(bf16[256,640]{1,0:T(8,128)(2,1)S(1)} %get-tuple-element.16.edge1), channel_id=1, source_target_pairs={{32,64},{64,32},{96,128},{128,96},{160,192},{192,160},{224,256},{2... | collective-permute-start | bytes 983048 | tf_op jit(solution)/shard_map/ppermute | solution.py:466
  22.2 7.2 %copy-start.3 = (f32[2,192]{1,0:T(2,128)S(1)}, f32[2,192]{1,0:T(2,128)}, u32[]{:S(2)}) copy-start(f32[2,192]{1,0:T(2,128)} %constant.47.clone.names) | copy-start | bytes 4612
  22.2 7.2 %copy-start.5 = (s32[2,24]{1,0:T(2,128)S(1)}, s32[2,24]{1,0:T(2,128)}, u32[]{:S(2)}) copy-start(s32[2,24]{1,0:T(2,128)} %constant.46.clone.pairs) | copy-start | bytes 580
  32.2 34.6 %copy-start.10 = (f32[191]{0:T(256)S(1)}, f32[191]{0:T(256)}, u32[]{:S(2)}) copy-start(f32[191]{0:T(256)} %param.18) | copy-start | bytes 2296
  47.9 34.8 %all-to-all-start.1 = ((bf16[32,8,256]{2,1,0:T(8,128)(2,1)}), bf16[32,8,256]{2,1,0:T(8,128)(2,1)S(1)}, u32[]{:S(2)}, u32[]{:S(2)}) async-start(bf16[32,8,256]{2,1,0:T(8,128)(2,1)} %bitcast.10), calls=%async_computation.1 | async-start | bytes 262144 | tf_op jit(solution)/shard_map/all_to_all | solution.py:508

commit v6 on v5

--- a/solution.py
+++ b/solution.py
@@ -119,17 +119,23 @@
     return jnp.sum(jnp.where(at, row, 0.0), axis=1, keepdims=True)
 
 
-def pack_kernel(odd, own, out0, out1, acc):
+def pack_kernel(odd, own, out0, out1, ends, acc, sems):
     far = own.shape[3] - LANES
     even = odd[0] == 0
+    copies = [
+        pltpu.make_async_copy(own.at[:, :, :, at : at + LANES], ends.at[n], sems.at[n])
+        for n, at in enumerate((0, far))
+    ]
+    for copy in copies:
+        copy.start()
     acc[...] = jnp.zeros_like(acc)
+    for copy in copies:
+        copy.wait()
 
     def one(d, _):
         for part in range(2):
-            head = own[part, d, :, 0:LANES].astype(F32)
-            tail = own[part, d, :, far : far + LANES].astype(F32)
-            head = pltpu.roll(head, HALO * d, 1)
-            tail = pltpu.roll(tail, HALO * d + HALO, 1)
+            head = pltpu.roll(ends[0, part, d].astype(F32), HALO * d, 1)
+            tail = pltpu.roll(ends[1, part, d].astype(F32), HALO * d + HALO, 1)
             here = iota(head.shape, 1) // HALO == d
             for n, tile in enumerate((jnp.where(even, tail, head), jnp.where(even, head, tail))):
                 acc[n, part] = jnp.where(here, tile, acc[n, part])
@@ -379,14 +385,14 @@
     ).astype(BF16)
 
 
-def final_kernel(got, rates, out):
+def final_kernel(got, lines, out):
     total = got[0].astype(F32)
     for g in range(1, got.shape[0]):
         total = total + got[g].astype(F32)
     total = total[:, 0:DATES]
     lane = iota(total.shape, 1)
     counts = jnp.sum(jnp.where(lane == DATES - 1, total, 0.0), axis=1, keepdims=True)
-    velocity = jnp.sum(total * rates[...], axis=1, keepdims=True)
+    velocity = jnp.sum(total * lines[2 * TAPS + 4 : 2 * TAPS + 5, :], axis=1, keepdims=True)
     total = jnp.where(lane == DATES - 1, velocity, total)
     out[...] = total / jnp.maximum(counts, 1.0)
 
@@ -434,20 +440,27 @@
         jnp.pad(partner.reshape(1, -1).astype(F32), ((0, 0), (0, DATES - partner.shape[0]))),
     ]
     facts = jnp.stack([group * date_count, group % 2, strip % 2, group]).astype(F32)
-    rows.append(jnp.pad(facts.reshape(1, -1), ((0, 4), (0, DATES - 4))))
+    rows.append(jnp.pad(facts.reshape(1, -1), ((0, 0), (0, DATES - 4))))
+    rows.append(jnp.pad(rate_weights.reshape(1, -1), ((0, 0), (0, DATES - rate_weights.shape[0]))))
     table, at = jnp.zeros((24, DATES), F32), 0
     for part in rows:
         table = table + jnp.pad(part, ((at, 24 - at - part.shape[0]), (0, 0)))
         at += part.shape[0]
 
+    tile = jax.ShapeDtypeStruct((2, ROWS, LANES), BF16)
+    tile0, tile1 = pl.pallas_call(
+        pack_kernel,
+        in_specs=[SMEM, pl.BlockSpec(memory_space=pl.ANY)],
+        out_specs=[VMEM] * 2,
+        out_shape=[tile] * 2,
+        scratch_shapes=[
+            pltpu.VMEM((2,) + slc_stack.shape[:3] + (LANES,), BF16),
+            pltpu.VMEM((2, 2, ROWS, LANES), F32),
+            pltpu.SemaphoreType.DMA((2,)),
+        ],
+        compiler_params=pltpu.CompilerParams(vmem_limit_bytes=53 * 1024 * 1024),
+    )((strip % 2).astype(jnp.int32).reshape(1), slc_stack)
     own = lax.reduce_precision(slc_stack, 8, 7)
-    tile0, tile1 = call(
-        pack_kernel,
-        ((strip % 2).astype(jnp.int32).reshape(1),),
-        (own,),
-        [((2, ROWS, LANES), BF16)] * 2,
-        [pltpu.VMEM((2, 2, ROWS, LANES), F32)],
-    )
     near = lax.ppermute(tile0, "col", swaps(strips, 0))
     far = lax.ppermute(tile1, "col", swaps(strips, 1))
     scratch = [
@@ -506,8 +519,7 @@
     phases = lax.all_to_all(sent, "date", 0, 0, tiled=True)
     (routed,) = call(series_kernel, (table,), (phases, weight), [((8 * strips, 256), BF16)])
     parts = lax.all_to_all(routed.reshape(strips, 8, 256), "col", 0, 0, tiled=True)
-    rates = jnp.pad(rate_weights.reshape(1, -1), ((0, 0), (0, 1)))
-    (mean,) = call(final_kernel, (), (parts, rates), [((8, DATES), F32)])
+    (mean,) = call(final_kernel, (), (parts, table), [((8, DATES), F32)])
     return mean.reshape(1, 8, DATES)
 
 

time: 83.7 us -> 82.5 us (0.986)
  blocking collectives: 13.6 us -> 48.2 us
  starting transfers between devices: 32.2 us -> 13.3 us
  waiting for transfers between devices: 18.8 us -> 2.81 us
  other arithmetic: 1.49 us -> 0.21 us
    all_to_all x0 -> x1, blocking collectives: none -> 34.6 us  [local(): lax.all_to_all(routed.reshape(strips, 8, 256), 'col', 0, 0, tiled=True)]
    all_to_all x1 -> x0, starting transfers between devices: 18.9 us -> none  [local(): lax.all_to_all(routed.reshape(strips, 8, 256), 'col', 0, 0, tiled=True)]
    all_to_all x1 -> x0, waiting for transfers between devices: 15.8 us -> none  [local(): lax.all_to_all(routed.reshape(strips, 8, 256), 'col', 0, 0, tiled=True)]
    pallas_call x0 -> x1, Pallas kernels: none -> 2.21 us  [local(): pl.pallas_call(pack_kernel, in_specs=[SMEM, pl.BlockSpec(memory_space=pl....]
    pallas_call x6 -> x5, Pallas kernels: 16.8 us -> 15.1 us  [call(): pl.pallas_call(kernel, in_specs=[SMEM] * len(smem) + [VMEM] * len(vmem),...]
    reduce_precision x1, other arithmetic: 1.39 us -> 0.11 us  [local(): own = lax.reduce_precision(slc_stack, 8, 7)]
  transfers between devices with their start and end apart: 5 -> 4, of which waited for: 2 -> 1; matrix products, arithmetic and copies ran while one was open for 0% -> 0% of each run, Pallas kernels for 9% -> 9%
where the time goes in v6:
time: 82.5 us; the launch traced here: 82.2 us
  blocking collectives  48.2 us (58%)
  Pallas kernels  17.3 us (21%)
  starting transfers between devices  13.3 us (16%)
  waiting for transfers between devices  2.81 us (3%)
    all_to_all x1, blocking collectives, local(): lax.all_to_all(routed.reshape(strips, 8, 256), 'col', 0, 0, tiled=True)  34.6 us
    pallas_call x5, Pallas kernels, call(): pl.pallas_call(kernel, in_specs=[SMEM] * len(smem) + [VMEM] * len(vmem),...  15.1 us
    all_to_all x1, blocking collectives, local(): phases = lax.all_to_all(sent, 'date', 0, 0, tiled=True)  13.6 us
    ppermute x1, starting transfers between devices, local(): near = lax.ppermute(tile0, 'col', swaps(strips, 0))  8.77 us
    ppermute x1, waiting for transfers between devices, local(): far = lax.ppermute(tile1, 'col', swaps(strips, 1))  2.8 us
    pallas_call x1, Pallas kernels, local(): pl.pallas_call(pack_kernel, in_specs=[SMEM, pl.BlockSpec(memory_space=pl....  2.21 us
    ppermute x1, starting transfers between devices, local(): got0 = lax.ppermute(edge0, 'date', swaps(groups, 0))  1.92 us
    ppermute x1, starting transfers between devices, local(): far = lax.ppermute(tile1, 'col', swaps(strips, 1))  1.92 us
  transfers between devices with their start and end apart: 4, of which 1 were waited for; matrix products, arithmetic and copies ran while one was open for 0% of the time, Pallas kernels for 9%

profile of v6, /device:TPU:1, one launch (start us, length us, event | category | flops | bytes accessed | tf_op | source)
XLA Modules:
  0.0 82.2 jit_solution(15767200083918697876)
XLA Ops:
  0.0 2.2 %shard_map.127 = (bf16[2,40,128]{2,1,0:T(8,128)(2,1)S(1)}, bf16[2,40,128]{2,1,0:T(8,128)(2,1)S(1)}) custom-call(s32[1]{0:T(128)} %bitcast.9.odd, bf16[2,12,40,640]{3,2,1,0:T(8,128)(2,1)} %own.1), custom_call_target="tpu_custom_call" | custom-call | tf_op jit(solution)/shard_map/pallas_call | solution.py:451
  2.3 8.8 %collective-permute-start = (bf16[2,40,128]{2,1,0:T(8,128)(2,1)S(1)}, bf16[2,40,128]{2,1,0:T(8,128)(2,1)S(1)}, u32[]{:S(2)}, u32[]{:S(2)}) collective-permute-start(bf16[2,40,128]{2,1,0:T(8,128)(2,1)S(1)} %get-tuple-element.13), channel_id=1, source_target_pairs={{0,1},{1,0},{2,3},{3,2},{4,5},{5,4},{6,7},{7,6},{8,9},{9,8},{10,11... | collective-permute-start | bytes 61448 | tf_op jit(solution)/shard_map/ppermute | solution.py:464
  11.0 1.9 %collective-permute-start.1 = (bf16[2,40,128]{2,1,0:T(8,128)(2,1)S(1)}, bf16[2,40,128]{2,1,0:T(8,128)(2,1)S(1)}, u32[]{:S(2)}, u32[]{:S(2)}) collective-permute-start(bf16[2,40,128]{2,1,0:T(8,128)(2,1)S(1)} %get-tuple-element.14), channel_id=1, source_target_pairs={{1,2},{2,1},{3,4},{4,3},{5,6},{6,5},{7,8},{8,7},{9,10},{10,9},{11,... | collective-permute-start | bytes 61448 | tf_op jit(solution)/shard_map/ppermute | solution.py:465
  13.0 0.1 add_convert_fusion
  13.1 0.1 reduce_precision.3.own
  13.3 0.0 copy-start
  13.3 0.0 copy-start.1
  13.3 0.0 copy-start.2
  13.3 0.0 copy-start.4
  13.3 0.0 copy-start.6
  13.3 0.0 copy-start.7
  13.3 2.8 %collective-permute-done.1.far = bf16[2,40,128]{2,1,0:T(8,128)(2,1)S(1)} collective-permute-done((bf16[2,40,128]{2,1,0:T(8,128)(2,1)S(1)}, bf16[2,40,128]{2,1,0:T(8,128)(2,1)S(1)}, u32[]{:S(2)}, u32[]{:S(2)}) %collective-permute-start.1) | collective-permute-done | bytes 20512 | tf_op jit(solution)/shard_map/ppermute | solution.py:465
  16.1 3.1 %shard_map.128 = (bf16[256,640]{1,0:T(8,128)(2,1)S(1)}, bf16[256,640]{1,0:T(8,128)(2,1)S(1)}) custom-call(f32[24,192]{1,0:T(8,128)S(1)} %pad_add_fusion.table.lines, bf16[2,12,40,640]{3,2,1,0:T(8,128)(2,1)S(1)} %reduce_precision.3.own, bf16[2,40,128]{2,1,0:T(8,128)(2,1)S(1)} %collective-permute-done.near, ...), custom_call_target="tpu_custom_call" | custom-call | tf_op jit(solution)/shard_map/pallas_call | solution.py:405
  19.2 1.9 %collective-permute-start.2 = (bf16[256,640]{1,0:T(8,128)(2,1)S(1)}, bf16[256,640]{1,0:T(8,128)(2,1)S(1)}, u32[]{:S(2)}, u32[]{:S(2)}) collective-permute-start(bf16[256,640]{1,0:T(8,128)(2,1)S(1)} %get-tuple-element.15.edge0), channel_id=1, source_target_pairs={{0,32},{32,0},{64,96},{96,64},{128,160},{160,128},{192,224},{224,1... | collective-permute-start | bytes 983048 | tf_op jit(solution)/shard_map/ppermute | solution.py:478
  21.2 0.7 collective-permute-start.3
  21.9 0.0 copy-start.3
  21.9 0.0 copy-start.5
  21.9 7.2 %shard_map.129 = (f32[48,256]{1,0:T(8,128)S(1)}, f32[96,256]{1,0:T(8,128)S(1)}, f32[12,2,40,640]{3,2,1,0:T(8,128)S(1)}, bf16[192,768]{1,0:T(8,128)(2,1)S(1)}) custom-call(f32[24,192]{1,0:T(8,128)S(1)} %pad_add_fusion.table.lines, s32[2,56]{1,0:T(2,128)S(1)} %copy-done.4, bf16[2,12,40,640]{3,2,1,0:T(8,128)(2,1)S(1)} %reduce_precision.3.own, ...), custom_call_target="tpu_custom_call" | custom-call | tf_op jit(solution)/shard_map/pallas_call | solution.py:405
  29.1 0.0 collective-permute-done.2.got0
  29.1 2.8 %shard_map.130 = bf16[16,48,256]{2,1,0:T(8,128)(2,1)S(1)} custom-call(f32[24,192]{1,0:T(8,128)S(1)} %pad_add_fusion.table.lines, s32[2,24]{1,0:T(2,128)S(1)} %copy-done.5, bf16[256,640]{1,0:T(8,128)(2,1)S(1)} %collective-permute-done.2.got0, bf16[256,640]{1,0:T(8,128)(2,1)S(1)} %collective-permute-done.3.got1, f32[12,2,40,640]{3,2,1,0:T(8,128)S(1)} %get-tuple-element.17.ys, ...), custom_call_target="tpu_custom_call" | custom-call | tf_op jit(solution)/shard_map/pallas_call | solution.py:405
  31.9 13.6 %all_to_all.10.got = bf16[16,48,256]{2,1,0:T(8,128)(2,1)S(1)} all-to-all(bf16[16,48,256]{2,1,0:T(8,128)(2,1)S(1)} %shard_map.130), channel_id=1, replica_groups=mesh['date'=16,'col'=32] {'date'}, dimensions={0} | all-to-all | bytes 786432 | tf_op jit(solution)/shard_map/all_to_all | solution.py:519
  45.5 1.4 %shard_map.131 = bf16[256,256]{1,0:T(8,128)(2,1)S(1)} custom-call(f32[24,192]{1,0:T(8,128)S(1)} %pad_add_fusion.table.lines, bf16[16,48,256]{2,1,0:T(8,128)(2,1)S(1)} %all_to_all.10.got, bf16[192,768]{1,0:T(8,128)(2,1)S(1)} %get-tuple-element.20.weight), custom_call_target="tpu_custom_call" | custom-call | tf_op jit(solution)/shard_map/pallas_call | solution.py:405
  46.9 34.6 %all_to_all.11.got = bf16[32,8,256]{2,1,0:T(8,128)(2,1)S(1)} all-to-all(bf16[32,8,256]{2,1,0:T(8,128)(2,1)S(1)} %bitcast.16), channel_id=1, replica_groups=mesh['date'=16,'col'=32] {'col'}, dimensions={0} | all-to-all | bytes 262144 | tf_op jit(solution)/shard_map/all_to_all | solution.py:521
  81.5 0.7 shard_map.132
  (23 shorter events, 0.1 us)
Async XLA Ops:
  0.0 13.1 %copy-start.8 = (bf16[2,12,40,640]{3,2,1,0:T(8,128)(2,1)S(1)}, bf16[2,12,40,640]{3,2,1,0:T(8,128)(2,1)}, u32[]{:S(2)}) copy-start(bf16[2,12,40,640]{3,2,1,0:T(8,128)(2,1)} %own.1) | copy-start | bytes 3686404
  0.0 13.0 %copy-start.10 = (s32[192,2]{0,1:T(2,128)S(1)}, s32[192,2]{0,1:T(2,128)}, u32[]{:S(2)}) copy-start(s32[192,2]{0,1:T(2,128)} %param.14) | copy-start | bytes 4612
  0.0 13.0 %copy-start.12 = (s32[36]{0:T(128)S(1)}, s32[36]{0:T(128)}, u32[]{:S(2)}) copy-start(s32[36]{0:T(128)} %param.16) | copy-start | bytes 436
  0.0 13.1 %copy-start.9 = (f32[192,2,8]{0,2,1:T(8,128)S(1)}, f32[192,2,8]{0,2,1:T(8,128)}, u32[]{:S(2)}) copy-start(f32[192,2,8]{0,2,1:T(8,128)} %param.15) | copy-start | bytes 36868
  0.0 13.1 %copy-start.11 = (f32[191]{0:T(256)S(1)}, f32[191]{0:T(256)}, u32[]{:S(2)}) copy-start(f32[191]{0:T(256)} %param.18) | copy-start | bytes 2296
  2.3 11.1 %collective-permute-start = (bf16[2,40,128]{2,1,0:T(8,128)(2,1)S(1)}, bf16[2,40,128]{2,1,0:T(8,128)(2,1)S(1)}, u32[]{:S(2)}, u32[]{:S(2)}) collective-permute-start(bf16[2,40,128]{2,1,0:T(8,128)(2,1)S(1)} %get-tuple-element.13), channel_id=1, source_target_pairs={{0,1},{1,0},{2,3},{3,2},{4,5},{5,4},{6,7},{7,6},{8,9},{9,8},{10,11... | collective-permute-start | bytes 61448 | tf_op jit(solution)/shard_map/ppermute | solution.py:464
  11.0 5.1 %collective-permute-start.1 = (bf16[2,40,128]{2,1,0:T(8,128)(2,1)S(1)}, bf16[2,40,128]{2,1,0:T(8,128)(2,1)S(1)}, u32[]{:S(2)}, u32[]{:S(2)}) collective-permute-start(bf16[2,40,128]{2,1,0:T(8,128)(2,1)S(1)} %get-tuple-element.14), channel_id=1, source_target_pairs={{1,2},{2,1},{3,4},{4,3},{5,6},{6,5},{7,8},{8,7},{9,10},{10,9},{11,... | collective-permute-start | bytes 61448 | tf_op jit(solution)/shard_map/ppermute | solution.py:465
  13.3 8.6 %copy-start = (bf16[640,256]{1,0:T(8,128)(2,1)S(1)}, bf16[640,256]{1,0:T(8,128)(2,1)}, u32[]{:S(2)}) copy-start(bf16[640,256]{1,0:T(8,128)(2,1)} %constant.68.matrix) | copy-start | bytes 983044
  13.3 8.6 %copy-start.1 = (bf16[191,576]{1,0:T(8,128)(2,1)S(1)}, bf16[191,576]{1,0:T(8,128)(2,1)}, u32[]{:S(2)}) copy-start(bf16[191,576]{1,0:T(8,128)(2,1)} %inverse.1) | copy-start | bytes 660100
  13.3 8.6 %copy-start.2 = (f32[2,448]{1,0:T(2,128)S(1)}, f32[2,448]{1,0:T(2,128)}, u32[]{:S(2)}) copy-start(f32[2,448]{1,0:T(2,128)} %constant.45.clone.names) | copy-start | bytes 10756
  13.3 8.6 %copy-start.4 = (s32[2,56]{1,0:T(2,128)S(1)}, s32[2,56]{1,0:T(2,128)}, u32[]{:S(2)}) copy-start(s32[2,56]{1,0:T(2,128)} %constant.44.clone.pairs) | copy-start | bytes 1348
  13.3 8.6 %copy-start.6 = (s32[1,16,1]{1,2,0:T(1,128)S(1)}, s32[1,16,1]{1,2,0:T(1,128)}, u32[]{:S(2)}) copy-start(s32[1,16,1]{1,2,0:T(1,128)} %param.19) | copy-start | bytes 196
  13.3 8.6 %copy-start.7 = (s32[1,16]{1,0:T(1,128)S(1)}, s32[1,16]{1,0:T(1,128)}, u32[]{:S(2)}) copy-start(s32[1,16]{1,0:T(1,128)} %cells.1) | copy-start | bytes 196
  19.2 9.9 %collective-permute-start.2 = (bf16[256,640]{1,0:T(8,128)(2,1)S(1)}, bf16[256,640]{1,0:T(8,128)(2,1)S(1)}, u32[]{:S(2)}, u32[]{:S(2)}) collective-permute-start(bf16[256,640]{1,0:T(8,128)(2,1)S(1)} %get-tuple-element.15.edge0), channel_id=1, source_target_pairs={{0,32},{32,0},{64,96},{96,64},{128,160},{160,128},{192,224},{224,1... | collective-permute-start | bytes 983048 | tf_op jit(solution)/shard_map/ppermute | solution.py:478
  21.2 8.0 %collective-permute-start.3 = (bf16[256,640]{1,0:T(8,128)(2,1)S(1)}, bf16[256,640]{1,0:T(8,128)(2,1)S(1)}, u32[]{:S(2)}, u32[]{:S(2)}) collective-permute-start(bf16[256,640]{1,0:T(8,128)(2,1)S(1)} %get-tuple-element.16.edge1), channel_id=1, source_target_pairs={{32,64},{64,32},{96,128},{128,96},{160,192},{192,160},{224,256},{2... | collective-permute-start | bytes 983048 | tf_op jit(solution)/shard_map/ppermute | solution.py:479
  21.9 7.2 %copy-start.3 = (f32[2,192]{1,0:T(2,128)S(1)}, f32[2,192]{1,0:T(2,128)}, u32[]{:S(2)}) copy-start(f32[2,192]{1,0:T(2,128)} %constant.47.clone.names) | copy-start | bytes 4612
  21.9 7.2 %copy-start.5 = (s32[2,24]{1,0:T(2,128)S(1)}, s32[2,24]{1,0:T(2,128)}, u32[]{:S(2)}) copy-start(s32[2,24]{1,0:T(2,128)} %constant.46.clone.pairs) | copy-start | bytes 580

commit v7 on v6

--- a/solution.py
+++ b/solution.py
@@ -21,6 +21,7 @@
 ROWS = 40
 DATES = 192
 EXTRA = 9
+FACTS = 20
 PAIR_ROWS = 48
 F32 = jnp.float32
 BF16 = jnp.bfloat16
@@ -37,11 +38,11 @@
 
 
 def fact(table, n):
-    return table[2 * TAPS + 3, n].astype(jnp.int32)
+    return (table[0, n] if table.shape[0] == 1 else table[FACTS + n, 0]).astype(jnp.int32)
 
 
 def partner_row(table, lines):
-    return lines[2 * TAPS + 2 : 2 * TAPS + 3, 0:36] - table[2 * TAPS + 3, 0]
+    return lines[18:19, 0:36] - fact(table, 0).astype(F32)
 
 
 def tap_weights(table, at, weights):
@@ -70,7 +71,7 @@
     count = own.shape[-1] // LANES
     lane = iota((ROWS, LANES), 1)
     for s, date in enumerate(dates):
-        tap_weights(table, jnp.clip(fact(table, 0) + date, 0, DATES - 1), weights.at[s])
+        tap_weights(table, date, weights.at[s])
     for s, date in enumerate(dates):
         for part in range(2):
             tile_a, tile_b = near[part].astype(F32), far[part].astype(F32)
@@ -237,9 +238,9 @@
 
 
 def inner_kernel(
-    table, pairs, own, near, far, edge0, edge1, lines, matrix, names, inverse, owners, cells,
-    phase_out, power_out, ys, weight_out,
-    lhs, weights, zs, ps, ss, pm, gather,
+    table, pairs, own, near, far, edge0, edge1, lines, matrix, names, owners, cells,
+    phase_out, power_out, ys,
+    lhs, weights, zs, ps, ss, pm,
 ):
     width = own.shape[-1]
 
@@ -284,21 +285,6 @@
     row = iota((PAIR_ROWS, 1), 0)
     have_a = jnp.where(row < 36, row // PER_DATE, -9).astype(F32)
     take = choose(names, have_a, local, True)
-
-    spots = iota((1, weight_out.shape[1]), 1)
-    group, k = spots // PAIR_ROWS, spots % PAIR_ROWS
-    target = jnp.where(k < 36, 36 * group + k, jnp.where(k < 45, 36 * group + k - 45, -1))
-
-    def one_rows(n, _):
-        at = pl.multiple_of(n * 16, 16)
-        gather[pl.ds(at, 16), :] = (iota((16, gather.shape[1]), 0) + at == target).astype(BF16)
-        return 0
-
-    lax.fori_loop(0, gather.shape[0] // 16, one_rows, 0)
-    weight_out[0:191, :] = jnp.dot(
-        inverse[...], gather[...], preferred_element_type=F32
-    ).astype(BF16)
-    weight_out[191:192, :] = jnp.zeros((1, weight_out.shape[1]), BF16)
 
     n = owners.shape[1]
     spread = (iota((n, 256), 1) == iota((n, 256), 0) + n * fact(table, 3)).astype(BF16)
@@ -310,6 +296,23 @@
     phase_out[...] = jnp.where(lines == 47, placed[1:2, :], phases)
 
 
+def weights_kernel(inverse, weight_out, gather):
+    spots = iota((1, weight_out.shape[1]), 1)
+    group, k = spots // PAIR_ROWS, spots % PAIR_ROWS
+    target = jnp.where(k < 36, 36 * group + k, jnp.where(k < 45, 36 * group + k - 45, -1))
+
+    def one_rows(n, _):
+        at = pl.multiple_of(n * 16, 16)
+        gather[pl.ds(at, 16), :] = (iota((16, gather.shape[1]), 0) + at == target).astype(BF16)
+        return 0
+
+    lax.fori_loop(0, gather.shape[0] // 16, one_rows, 0)
+    weight_out[0:191, :] = jnp.dot(
+        inverse[...], gather[...], preferred_element_type=F32
+    ).astype(BF16)
+    weight_out[191:192, :] = jnp.zeros((1, weight_out.shape[1]), BF16)
+
+
 def outer_kernel(
     table, pairs, got0, got1, ys, power, phase, lines, matrix, names, out, rs, ps, ss, pm, pw
 ):
@@ -346,8 +349,9 @@
     last = 8 * (len(CROSS) + len(BEFORE))
     ss[last:, :] = jnp.zeros_like(ss[last:, :])
     pw[0:96, :] = power[...]
-    pw[96:144, :] = window_sum(ps[...], matrix)
-    pm[...] = window_sum(ss[...], matrix)
+    sums = window_sum(jnp.concatenate([ss[...], ps[...]], axis=0), matrix)
+    pm[...] = sums[: ss.shape[0]]
+    pw[96:144, :] = sums[ss.shape[0] :]
     phases_of(pairs, total, pm, pw)
     local = column(partner_row(table, lines), PAIR_ROWS, 0)
     row = iota((PAIR_ROWS, 1), 0)
@@ -376,7 +380,7 @@
     for g in range(1, got.shape[0]):
         codes = codes + got[g, 40:48, :].astype(F32)
     owner, cell = codes[6:7, :], codes[7:8, :]
-    base = table[2 * TAPS + 3, 3] * 8.0
+    base = fact(table, 3).astype(F32) * 8.0
     mine = (cell >= base) & (cell < base + 8)
     target = jnp.where(mine, owner * 8 + cell - base, -1.0).astype(jnp.int32)
     select = (iota((out.shape[0], wide), 0) == target).astype(BF16)
@@ -392,7 +396,7 @@
     total = total[:, 0:DATES]
     lane = iota(total.shape, 1)
     counts = jnp.sum(jnp.where(lane == DATES - 1, total, 0.0), axis=1, keepdims=True)
-    velocity = jnp.sum(total * lines[2 * TAPS + 4 : 2 * TAPS + 5, :], axis=1, keepdims=True)
+    velocity = jnp.sum(total * lines[19:20, :], axis=1, keepdims=True)
     total = jnp.where(lane == DATES - 1, velocity, total)
     out[...] = total / jnp.maximum(counts, 1.0)
 
@@ -439,13 +443,15 @@
         offsets.T.astype(F32),
         jnp.pad(partner.reshape(1, -1).astype(F32), ((0, 0), (0, DATES - partner.shape[0]))),
     ]
+    rows.append(jnp.pad(rate_weights.reshape(1, -1), ((0, 0), (0, DATES - rate_weights.shape[0]))))
     facts = jnp.stack([group * date_count, group % 2, strip % 2, group]).astype(F32)
-    rows.append(jnp.pad(facts.reshape(1, -1), ((0, 0), (0, DATES - 4))))
-    rows.append(jnp.pad(rate_weights.reshape(1, -1), ((0, 0), (0, DATES - rate_weights.shape[0]))))
+    rows.append(jnp.broadcast_to(facts[:, None], (4, DATES)))
+    facts = facts.reshape(1, -1)
     table, at = jnp.zeros((24, DATES), F32), 0
     for part in rows:
         table = table + jnp.pad(part, ((at, 24 - at - part.shape[0]), (0, 0)))
         at += part.shape[0]
+    mine = lax.dynamic_slice(table, (0, group * date_count), (table.shape[0], date_count))
 
     tile = jax.ShapeDtypeStruct((2, ROWS, LANES), BF16)
     tile0, tile1 = pl.pallas_call(
@@ -463,6 +469,14 @@
     own = lax.reduce_precision(slc_stack, 8, 7)
     near = lax.ppermute(tile0, "col", swaps(strips, 0))
     far = lax.ppermute(tile1, "col", swaps(strips, 1))
+    (weight,) = call(
+        weights_kernel,
+        (),
+        (inverse,),
+        [((DATES, groups * PAIR_ROWS), BF16)],
+        [pltpu.VMEM((inverse.shape[1], groups * PAIR_ROWS), BF16)],
+    )
+    far, weight = lax.optimization_barrier((far, weight))
     scratch = [
         pltpu.VMEM((2, 2 * ROWS * width // LANES, 2 * LANES), BF16),
         pltpu.VMEM((2, 4 * LANES, 2 * LANES), BF16),
@@ -470,7 +484,7 @@
     ]
     edge0, edge1 = call(
         edge_kernel,
-        (table,),
+        (mine,),
         (own, near, far, table),
         [((256, width), BF16)] * 2,
         scratch,
@@ -482,30 +496,28 @@
     inner_rows = 8 * (len(INNER) + 5)
     outer_rows = 8 * (len(CROSS) + len(BEFORE) + 3)
     outer_pairs = CROSS + [(a + 6, b - 12) for a, b in BEFORE]
-    phase, power, ys, weight = call(
+    phase, power, ys = call(
         inner_kernel,
-        (table, pair_table(INNER, inner_rows)),
+        (mine, pair_table(INNER, inner_rows)),
         (
-            own, near, far, edge0, edge1, table, matrix, pair_names(INNER, inner_rows), inverse,
+            own, near, far, edge0, edge1, table, matrix, pair_names(INNER, inner_rows),
             owners.reshape(1, -1), map_cell,
         ),
         [
             ((PAIR_ROWS, 256), F32),
             ((96, 256), F32),
             ((12, 2, ROWS, width), F32),
-            ((DATES, groups * PAIR_ROWS), BF16),
         ],
         scratch
         + [
             pltpu.VMEM((96, width), F32),
             pltpu.VMEM((inner_rows, width), F32),
             pltpu.VMEM((inner_rows, 256), F32),
-            pltpu.VMEM((inverse.shape[1], groups * PAIR_ROWS), BF16),
         ],
     )
     (sent,) = call(
         outer_kernel,
-        (table, pair_table(outer_pairs, outer_rows)),
+        (facts, pair_table(outer_pairs, outer_rows)),
         (got0, got1, ys, power, phase, table, matrix, pair_names(CROSS + BEFORE, outer_rows)),
         [((groups, PAIR_ROWS, 256), BF16)],
         [
@@ -517,7 +529,7 @@
         ],
     )
     phases = lax.all_to_all(sent, "date", 0, 0, tiled=True)
-    (routed,) = call(series_kernel, (table,), (phases, weight), [((8 * strips, 256), BF16)])
+    (routed,) = call(series_kernel, (facts,), (phases, weight), [((8 * strips, 256), BF16)])
     parts = lax.all_to_all(routed.reshape(strips, 8, 256), "col", 0, 0, tiled=True)
     (mean,) = call(final_kernel, (), (parts, table), [((8, DATES), F32)])
     return mean.reshape(1, 8, DATES)

time: 82.5 us -> 80.9 us (0.981)
  starting transfers between devices: 13.3 us -> 12 us
  Pallas kernels: 17.3 us -> 16.2 us
  local copies, waits for them, and re-layouts: 0.07 us -> 1.04 us
    ppermute x1, starting transfers between devices: 8.77 us -> 4.5 us  [local(): near = lax.ppermute(tile0, 'col', swaps(strips, 0))]
    ppermute x1, starting transfers between devices: 1.92 us -> 4.94 us  [local(): far = lax.ppermute(tile1, 'col', swaps(strips, 1))]
    ppermute x1, waiting for transfers between devices: 2.8 us -> 0.01 us  [local(): far = lax.ppermute(tile1, 'col', swaps(strips, 1))]
    ppermute x1, waiting for transfers between devices: 0.01 us -> 2.15 us  [local(): got0 = lax.ppermute(edge0, 'date', swaps(groups, 0))]
    all_to_all x1, blocking collectives: 13.6 us -> 15.4 us  [local(): phases = lax.all_to_all(sent, 'date', 0, 0, tiled=True)]
    all_to_all x1, blocking collectives: 34.6 us -> 33.1 us  [local(): lax.all_to_all(routed.reshape(strips, 8, 256), 'col', 0, 0, tiled=True)]
    pallas_call x5 -> x6, Pallas kernels: 15.1 us -> 14 us  [call(): pl.pallas_call(kernel, in_specs=[SMEM] * len(smem) + [VMEM] * len(vmem),...]
  transfers between devices with their start and end apart: 4 -> 4, of which waited for: 1 -> 1; matrix products, arithmetic and copies ran while one was open for 0% -> 1% of each run, Pallas kernels for 9% -> 9%
where the time goes in v7:
time: 80.9 us; the launch traced here: 80.5 us
  blocking collectives  48.5 us (60%)
  Pallas kernels  16.2 us (20%)
  starting transfers between devices  12 us (15%)
  waiting for transfers between devices  2.16 us (3%)
  local copies, waits for them, and re-layouts  1.04 us (1%)
    all_to_all x1, blocking collectives, local(): lax.all_to_all(routed.reshape(strips, 8, 256), 'col', 0, 0, tiled=True)  33.1 us
    all_to_all x1, blocking collectives, local(): phases = lax.all_to_all(sent, 'date', 0, 0, tiled=True)  15.4 us
    pallas_call x6, Pallas kernels, call(): pl.pallas_call(kernel, in_specs=[SMEM] * len(smem) + [VMEM] * len(vmem),...  14 us
    ppermute x1, starting transfers between devices, local(): far = lax.ppermute(tile1, 'col', swaps(strips, 1))  4.94 us
    ppermute x1, starting transfers between devices, local(): near = lax.ppermute(tile0, 'col', swaps(strips, 0))  4.5 us
    pallas_call x1, Pallas kernels, local(): pl.pallas_call(pack_kernel, in_specs=[SMEM, pl.BlockSpec(memory_space=pl....  2.21 us
    ppermute x1, waiting for transfers between devices, local(): got0 = lax.ppermute(edge0, 'date', swaps(groups, 0))  2.15 us
    ppermute x1, starting transfers between devices, local(): got0 = lax.ppermute(edge0, 'date', swaps(groups, 0))  1.92 us
  transfers between devices with their start and end apart: 4, of which 1 were waited for; matrix products, arithmetic and copies ran while one was open for 1% of the time, Pallas kernels for 9%

profile of v7, /device:TPU:1, one launch (start us, length us, event | category | flops | bytes accessed | tf_op | source)
XLA Modules:
  0.0 80.5 jit_solution(16807972780192645887)
XLA Ops:
  0.0 2.2 %shard_map.127 = (bf16[2,40,128]{2,1,0:T(8,128)(2,1)S(1)}, bf16[2,40,128]{2,1,0:T(8,128)(2,1)S(1)}) custom-call(s32[1]{0:T(128)} %bitcast.11.odd, bf16[2,12,40,640]{3,2,1,0:T(8,128)(2,1)} %own.1), custom_call_target="tpu_custom_call" | custom-call | tf_op jit(solution)/shard_map/pallas_call | solution.py:457
  2.3 4.9 %collective-permute-start.1 = (bf16[2,40,128]{2,1,0:T(8,128)(2,1)S(1)}, bf16[2,40,128]{2,1,0:T(8,128)(2,1)S(1)}, u32[]{:S(2)}, u32[]{:S(2)}) collective-permute-start(bf16[2,40,128]{2,1,0:T(8,128)(2,1)S(1)} %get-tuple-element.15), channel_id=1, source_target_pairs={{1,2},{2,1},{3,4},{4,3},{5,6},{6,5},{7,8},{8,7},{9,10},{10,9},{11,... | collective-permute-start | bytes 61448 | tf_op jit(solution)/shard_map/ppermute | solution.py:471
  7.2 4.5 %collective-permute-start = (bf16[2,40,128]{2,1,0:T(8,128)(2,1)S(1)}, bf16[2,40,128]{2,1,0:T(8,128)(2,1)S(1)}, u32[]{:S(2)}, u32[]{:S(2)}) collective-permute-start(bf16[2,40,128]{2,1,0:T(8,128)(2,1)S(1)} %get-tuple-element.14), channel_id=1, source_target_pairs={{0,1},{1,0},{2,3},{3,2},{4,5},{5,4},{6,7},{7,6},{8,9},{9,8},{10,11... | collective-permute-start | bytes 61448 | tf_op jit(solution)/shard_map/ppermute | solution.py:470
  11.8 0.1 add_convert_fusion.1
  11.9 0.1 pad.36
  11.9 0.1 fusion.lines
  12.0 0.1 constant_dynamic-slice_fusion.table
  12.1 0.1 reduce_precision.3.own
  12.2 0.8 %copy-done.1 = bf16[191,576]{1,0:T(8,128)(2,1)S(1)} copy-done((bf16[191,576]{1,0:T(8,128)(2,1)S(1)}, bf16[191,576]{1,0:T(8,128)(2,1)}, u32[]{:S(2)}) %copy-start.1) | copy-done | bytes 220056
  13.0 0.0 copy-start.7
  13.1 0.7 shard_map.128.weight
  13.8 2.9 %shard_map.129 = (bf16[256,640]{1,0:T(8,128)(2,1)S(1)}, bf16[256,640]{1,0:T(8,128)(2,1)S(1)}) custom-call(f32[24,12]{1,0:T(8,128)S(1)} %constant_dynamic-slice_fusion.table, bf16[2,12,40,640]{3,2,1,0:T(8,128)(2,1)S(1)} %reduce_precision.3.own, bf16[2,40,128]{2,1,0:T(8,128)(2,1)S(1)} %collective-permute-done.near, ...), custom_call_target="tpu_custom_call" | custom-call | tf_op jit(solution)/shard_map/pallas_call | solution.py:409
  16.7 0.0 copy-start.3
  16.7 0.0 copy-start.4
  16.8 1.9 %collective-permute-start.2 = (bf16[256,640]{1,0:T(8,128)(2,1)S(1)}, bf16[256,640]{1,0:T(8,128)(2,1)S(1)}, u32[]{:S(2)}, u32[]{:S(2)}) collective-permute-start(bf16[256,640]{1,0:T(8,128)(2,1)S(1)} %get-tuple-element.17.edge0), channel_id=1, source_target_pairs={{0,32},{32,0},{64,96},{96,64},{128,160},{160,128},{192,224},{224,1... | collective-permute-start | bytes 983048 | tf_op jit(solution)/shard_map/ppermute | solution.py:492
  18.7 0.7 collective-permute-start.3
  19.4 0.1 add_convert_fusion.table
  19.5 6.3 %shard_map.130 = (f32[48,256]{1,0:T(8,128)S(1)}, f32[96,256]{1,0:T(8,128)S(1)}, f32[12,2,40,640]{3,2,1,0:T(8,128)S(1)}) custom-call(f32[24,12]{1,0:T(8,128)S(1)} %constant_dynamic-slice_fusion.table, s32[2,56]{1,0:T(2,128)S(1)} %copy-done.5, bf16[2,12,40,640]{3,2,1,0:T(8,128)(2,1)S(1)} %reduce_precision.3.own, ...), custom_call_target="tpu_custom_call" | custom-call | tf_op jit(solution)/shard_map/pallas_call | solution.py:409
  25.8 2.2 %collective-permute-done.2.got0 = bf16[256,640]{1,0:T(8,128)(2,1)S(1)} collective-permute-done((bf16[256,640]{1,0:T(8,128)(2,1)S(1)}, bf16[256,640]{1,0:T(8,128)(2,1)S(1)}, u32[]{:S(2)}, u32[]{:S(2)}) %collective-permute-start.2) | collective-permute-done | bytes 327712 | tf_op jit(solution)/shard_map/ppermute | solution.py:492
  28.0 2.4 %shard_map.131 = bf16[16,48,256]{2,1,0:T(8,128)(2,1)S(1)} custom-call(f32[1,4]{1,0:T(1,128)S(1)} %add_convert_fusion.table, s32[2,24]{1,0:T(2,128)S(1)} %copy-done.4, bf16[256,640]{1,0:T(8,128)(2,1)S(1)} %collective-permute-done.2.got0, bf16[256,640]{1,0:T(8,128)(2,1)S(1)} %collective-permute-done.3.got1, f32[12,2,40,640]{3,2,1,0:T(8,128)S(1)} %get-tuple-element.19.ys, ...), custom_call_target="tpu_custom_call" | custom-call | tf_op jit(solution)/shard_map/pallas_call | solution.py:409
  30.4 15.4 %all_to_all.10.got = bf16[16,48,256]{2,1,0:T(8,128)(2,1)S(1)} all-to-all(bf16[16,48,256]{2,1,0:T(8,128)(2,1)S(1)} %shard_map.131), channel_id=1, replica_groups=mesh['date'=16,'col'=32] {'date'}, dimensions={0} | all-to-all | bytes 786432 | tf_op jit(solution)/shard_map/all_to_all | solution.py:531
  45.7 1.0 %shard_map.132 = bf16[256,256]{1,0:T(8,128)(2,1)S(1)} custom-call(f32[1,4]{1,0:T(1,128)S(1)} %add_convert_fusion.table, bf16[16,48,256]{2,1,0:T(8,128)(2,1)S(1)} %all_to_all.10.got, bf16[192,768]{1,0:T(8,128)(2,1)S(1)} %shard_map.128.weight), custom_call_target="tpu_custom_call" | custom-call | tf_op jit(solution)/shard_map/pallas_call | solution.py:409
  46.7 33.1 %all_to_all.11.got = bf16[32,8,256]{2,1,0:T(8,128)(2,1)S(1)} all-to-all(bf16[32,8,256]{2,1,0:T(8,128)(2,1)S(1)} %bitcast.19), channel_id=1, replica_groups=mesh['date'=16,'col'=32] {'col'}, dimensions={0} | all-to-all | bytes 262144 | tf_op jit(solution)/shard_map/all_to_all | solution.py:533
  79.8 0.7 shard_map.133
  (27 shorter events, 0.1 us)
Async XLA Ops:
  0.0 12.1 %copy-start.8 = (bf16[2,12,40,640]{3,2,1,0:T(8,128)(2,1)S(1)}, bf16[2,12,40,640]{3,2,1,0:T(8,128)(2,1)}, u32[]{:S(2)}) copy-start(bf16[2,12,40,640]{3,2,1,0:T(8,128)(2,1)} %own.1) | copy-start | bytes 3686404
  0.0 11.7 %copy-start.10 = (s32[192,2]{0,1:T(2,128)S(1)}, s32[192,2]{0,1:T(2,128)}, u32[]{:S(2)}) copy-start(s32[192,2]{0,1:T(2,128)} %param.14) | copy-start | bytes 4612
  0.0 11.7 %copy-start.12 = (s32[36]{0:T(128)S(1)}, s32[36]{0:T(128)}, u32[]{:S(2)}) copy-start(s32[36]{0:T(128)} %param.16) | copy-start | bytes 436
  0.0 11.9 %copy-start.9 = (f32[192,2,8]{0,2,1:T(8,128)S(1)}, f32[192,2,8]{0,2,1:T(8,128)}, u32[]{:S(2)}) copy-start(f32[192,2,8]{0,2,1:T(8,128)} %param.15) | copy-start | bytes 36868
  0.0 11.9 %copy-start.11 = (f32[191]{0:T(256)S(1)}, f32[191]{0:T(256)}, u32[]{:S(2)}) copy-start(f32[191]{0:T(256)} %param.18) | copy-start | bytes 2296
  2.3 11.5 %collective-permute-start.1 = (bf16[2,40,128]{2,1,0:T(8,128)(2,1)S(1)}, bf16[2,40,128]{2,1,0:T(8,128)(2,1)S(1)}, u32[]{:S(2)}, u32[]{:S(2)}) collective-permute-start(bf16[2,40,128]{2,1,0:T(8,128)(2,1)S(1)} %get-tuple-element.15), channel_id=1, source_target_pairs={{1,2},{2,1},{3,4},{4,3},{5,6},{6,5},{7,8},{8,7},{9,10},{10,9},{11,... | collective-permute-start | bytes 61448 | tf_op jit(solution)/shard_map/ppermute | solution.py:471
  7.2 6.6 %collective-permute-start = (bf16[2,40,128]{2,1,0:T(8,128)(2,1)S(1)}, bf16[2,40,128]{2,1,0:T(8,128)(2,1)S(1)}, u32[]{:S(2)}, u32[]{:S(2)}) collective-permute-start(bf16[2,40,128]{2,1,0:T(8,128)(2,1)S(1)} %get-tuple-element.14), channel_id=1, source_target_pairs={{0,1},{1,0},{2,3},{3,2},{4,5},{5,4},{6,7},{7,6},{8,9},{9,8},{10,11... | collective-permute-start | bytes 61448 | tf_op jit(solution)/shard_map/ppermute | solution.py:470
  12.1 0.9 %copy-start.1 = (bf16[191,576]{1,0:T(8,128)(2,1)S(1)}, bf16[191,576]{1,0:T(8,128)(2,1)}, u32[]{:S(2)}) copy-start(bf16[191,576]{1,0:T(8,128)(2,1)} %inverse.1) | copy-start | bytes 660100
  13.0 6.4 %copy-start = (bf16[640,256]{1,0:T(8,128)(2,1)S(1)}, bf16[640,256]{1,0:T(8,128)(2,1)}, u32[]{:S(2)}) copy-start(bf16[640,256]{1,0:T(8,128)(2,1)} %constant.68.matrix) | copy-start | bytes 983044
  13.0 6.4 %copy-start.2 = (f32[2,448]{1,0:T(2,128)S(1)}, f32[2,448]{1,0:T(2,128)}, u32[]{:S(2)}) copy-start(f32[2,448]{1,0:T(2,128)} %constant.47.clone.names) | copy-start | bytes 10756
  13.0 6.4 %copy-start.5 = (s32[2,56]{1,0:T(2,128)S(1)}, s32[2,56]{1,0:T(2,128)}, u32[]{:S(2)}) copy-start(s32[2,56]{1,0:T(2,128)} %constant.46.clone.pairs) | copy-start | bytes 1348
  13.0 6.4 %copy-start.6 = (s32[1,16,1]{1,2,0:T(1,128)S(1)}, s32[1,16,1]{1,2,0:T(1,128)}, u32[]{:S(2)}) copy-start(s32[1,16,1]{1,2,0:T(1,128)} %param.19) | copy-start | bytes 196
  13.0 6.4 %copy-start.7 = (s32[1,16]{1,0:T(1,128)S(1)}, s32[1,16]{1,0:T(1,128)}, u32[]{:S(2)}) copy-start(s32[1,16]{1,0:T(1,128)} %cells.1) | copy-start | bytes 196
  16.7 11.3 %copy-start.3 = (f32[2,192]{1,0:T(2,128)S(1)}, f32[2,192]{1,0:T(2,128)}, u32[]{:S(2)}) copy-start(f32[2,192]{1,0:T(2,128)} %constant.49.clone.names) | copy-start | bytes 4612
  16.7 11.2 %copy-start.4 = (s32[2,24]{1,0:T(2,128)S(1)}, s32[2,24]{1,0:T(2,128)}, u32[]{:S(2)}) copy-start(s32[2,24]{1,0:T(2,128)} %constant.48.clone.pairs) | copy-start | bytes 580
  16.8 11.2 %collective-permute-start.2 = (bf16[256,640]{1,0:T(8,128)(2,1)S(1)}, bf16[256,640]{1,0:T(8,128)(2,1)S(1)}, u32[]{:S(2)}, u32[]{:S(2)}) collective-permute-start(bf16[256,640]{1,0:T(8,128)(2,1)S(1)} %get-tuple-element.17.edge0), channel_id=1, source_target_pairs={{0,32},{32,0},{64,96},{96,64},{128,160},{160,128},{192,224},{224,1... | collective-permute-start | bytes 983048 | tf_op jit(solution)/shard_map/ppermute | solution.py:492
  18.7 9.3 %collective-permute-start.3 = (bf16[256,640]{1,0:T(8,128)(2,1)S(1)}, bf16[256,640]{1,0:T(8,128)(2,1)S(1)}, u32[]{:S(2)}, u32[]{:S(2)}) collective-permute-start(bf16[256,640]{1,0:T(8,128)(2,1)S(1)} %get-tuple-element.18.edge1), channel_id=1, source_target_pairs={{32,64},{64,32},{96,128},{128,96},{160,192},{192,160},{224,256},{2... | collective-permute-start | bytes 983048 | tf_op jit(solution)/shard_map/ppermute | solution.py:493

commit v8 on v7

--- a/solution.py
+++ b/solution.py
@@ -147,18 +147,15 @@
     out1[...] = acc[1].astype(BF16)
 
 
-def edge_kernel(table, own, near, far, lines, out0, out1, lhs, weights, zs):
-    odd_date = fact(table, 1)
+def edge_kernel(table, own, near, far, lines, head, tail, lhs, weights, zs):
     local = column(partner_row(table, lines), 16, 36 - EXTRA)
-    wide = out0.shape[1]
-    told = jnp.broadcast_to(local, (16, wide)).astype(BF16)
-    out0[240:256, :] = told
-    out1[240:256, :] = told
+    for out in (head, tail):
+        out[240:256, :] = jnp.broadcast_to(local, (16, out.shape[1])).astype(BF16)
 
     def one(i, _):
-        dates = (9 - 9 * odd_date + i, 9 * odd_date + i)
+        dates = (i, i + 9)
         resample(own, near, far, table, dates, lhs, weights, zs)
-        for s, out in enumerate((out0, out1)):
+        for s, out in enumerate((head, tail)):
             for part, k, cols, tile in slabs(zs, s):
                 out[pl.ds(pl.multiple_of(i * 80 + part * 40 + k * 8, 8), 8), cols] = tile
         return 0
@@ -225,13 +222,10 @@
     lax.fori_loop(0, count // 8, one, 0)
 
 
-def spread_dates(even, odd, parity, dates, first, second):
+def unpack_dates(packed, dates, start):
     def one(n, _):
-        at = pl.multiple_of(n * 80, 16)
-        one, two = even[pl.ds(at, 80), :].astype(F32), odd[pl.ds(at, 80), :].astype(F32)
-        low, high = jnp.where(parity == 1, two, one), jnp.where(parity == 1, one, two)
-        dates[n + first, 0], dates[n + first, 1] = low[:40], low[40:]
-        dates[n + second, 0], dates[n + second, 1] = high[:40], high[40:]
+        both = packed[pl.ds(pl.multiple_of(n * 80, 16), 80), :].astype(F32)
+        dates[n + start, 0], dates[n + start, 1] = both[:40], both[40:]
         return 0
 
     lax.fori_loop(0, HALF, one, 0)
@@ -253,7 +247,8 @@
         return 0
 
     lax.fori_loop(0, HALF, one_date, 0)
-    spread_dates(edge1, edge0, fact(table, 1), ys, 0, 9)
+    unpack_dates(edge0, ys, 0)
+    unpack_dates(edge1, ys, 9)
 
     def one_power(d, _):
         ps[pl.ds(pl.multiple_of(d * 8, 8), 8), :] = power_sum(reader(d))
@@ -313,58 +308,60 @@
     weight_out[191:192, :] = jnp.zeros((1, weight_out.shape[1]), BF16)
 
 
-def outer_kernel(
-    table, pairs, got0, got1, ys, power, phase, lines, matrix, names, out, rs, ps, ss, pm, pw
-):
-    width = got0.shape[1]
-    odd_date = fact(table, 1)
-
-    spread_dates(got0, got1, odd_date, rs, 0, 3)
+def boundary_phases(pairs, count, later, got, ys, power, matrix, rs, ss, pm, pw):
+    unpack_dates(got, rs, 0)
 
     def here(d):
         return lambda part, k: ys[d, part, 8 * k : 8 * k + 8, :]
 
     def there(d):
-        return lambda part, k: rs[d, part, 8 * k : 8 * k + 8, :]
+        return lambda part, k: rs[d - 12, part, 8 * k : 8 * k + 8, :]
+
+    first, second = (here, there) if later else (there, here)
+
+    def one_pair(c, _):
+        at = pl.multiple_of(c * 8, 8)
+        ss[pl.ds(at, 8), :] = cross_sum(first(pairs[0, c]), second(pairs[1, c]))
+        return 0
+
+    lax.fori_loop(0, count, one_pair, 0)
+    rows = pm.shape[0]
 
     def one_power(n, _):
-        ps[pl.ds(pl.multiple_of(n * 8, 8), 8), :] = power_sum(there(n))
-        return 0
-
-    lax.fori_loop(0, 2 * HALF, one_power, 0)
-
-    def one_after(c, _):
-        at = pl.multiple_of(c * 8, 8)
-        ss[pl.ds(at, 8), :] = cross_sum(here(pairs[0, c]), there(pairs[1, c] - 12))
-        return 0
-
-    def one_before(c, _):
-        at = pl.multiple_of(c * 8, 8)
-        ss[pl.ds(at, 8), :] = cross_sum(there(pairs[0, c] - 12), here(pairs[1, c]))
-        return 0
-
-    total = ss.shape[0] // 8
-    lax.fori_loop(0, len(CROSS), one_after, 0)
-    lax.fori_loop(len(CROSS), len(CROSS) + len(BEFORE), one_before, 0)
-    last = 8 * (len(CROSS) + len(BEFORE))
-    ss[last:, :] = jnp.zeros_like(ss[last:, :])
+        ss[pl.ds(pl.multiple_of(rows + n * 8, 8), 8), :] = power_sum(there(n + 12))
+        return 0
+
+    lax.fori_loop(0, HALF, one_power, 0)
+    ss[count * 8 : rows, :] = jnp.zeros_like(ss[count * 8 : rows, :])
     pw[0:96, :] = power[...]
-    sums = window_sum(jnp.concatenate([ss[...], ps[...]], axis=0), matrix)
-    pm[...] = sums[: ss.shape[0]]
-    pw[96:144, :] = sums[ss.shape[0] :]
-    phases_of(pairs, total, pm, pw)
-    local = column(partner_row(table, lines), PAIR_ROWS, 0)
+    sums = window_sum(ss[...], matrix)
+    pm[...] = sums[:rows]
+    pw[96:120, :] = sums[rows:]
+    phases_of(pairs, rows // 8, pm, pw)
+
+
+def after_kernel(
+    facts, pairs, got, ys, power, phase, lines, matrix, names, out, rs, ss, pm, pw
+):
+    boundary_phases(pairs, len(CROSS), True, got, ys, power, matrix, rs, ss, pm, pw)
+    local = column(partner_row(facts, lines), PAIR_ROWS, 0)
     row = iota((PAIR_ROWS, 1), 0)
-    told = jnp.where(odd_date == 1, got0[240:256, 0:LANES], got1[240:256, 0:LANES]).astype(F32)
-    told = jnp.max(told, axis=1, keepdims=True)
+    have_a = jnp.where(row < 36, row // PER_DATE, -9).astype(F32)
+    take = choose(names, have_a, local, False)
+    out[...] = phase[...] + jnp.dot(take, pm[...].astype(BF16), preferred_element_type=F32)
+
+
+def before_kernel(pairs, got, ys, power, phase, matrix, names, out, rs, ss, pm, pw):
+    boundary_phases(pairs, len(BEFORE), False, got, ys, power, matrix, rs, ss, pm, pw)
+    told = jnp.max(got[240:256, 0:LANES].astype(F32), axis=1, keepdims=True)
     spread = (iota((PAIR_ROWS, 16), 0) - 36 == iota((PAIR_ROWS, 16), 1)).astype(BF16)
     moved = jnp.dot(
         spread, jnp.broadcast_to(told, (16, LANES)).astype(BF16), preferred_element_type=F32
     )[:, 0:1]
-    mine = jnp.where(row < 36, jnp.where(local < 15, local, -5.0), jnp.where(row < 45, moved, -5.0))
-    mine = jnp.where((row >= 36) & (mine < 15), -5.0, mine)
-    have_a = jnp.where(row < 36, row // PER_DATE, 9 + (row - 36) // PER_DATE).astype(F32)
-    take = choose(names, have_a, mine, False)
+    row = iota((PAIR_ROWS, 1), 0)
+    theirs = (row >= 36) & (row < 36 + EXTRA)
+    have_a = jnp.where(theirs, 9 + (row - 36) // PER_DATE, -9).astype(F32)
+    take = choose(names, have_a, jnp.where(theirs, moved, -5.0), False)
     total = phase[...] + jnp.dot(take, pm[...].astype(BF16), preferred_element_type=F32)
     for g in range(out.shape[0]):
         out[g] = total.astype(BF16)
@@ -489,13 +486,11 @@
         [((256, width), BF16)] * 2,
         scratch,
     )
-    got0 = lax.ppermute(edge0, "date", swaps(groups, 0))
-    got1 = lax.ppermute(edge1, "date", swaps(groups, 1))
+    later = lax.ppermute(edge0, "date", [(i + 1, i) for i in range(groups - 1)])
+    earlier = lax.ppermute(edge1, "date", [(i, i + 1) for i in range(groups - 1)])
     window = np.arange(width)[:, None] // LOOK_RG == np.arange(256)[None, :] % (width // LOOK_RG)
     matrix = jnp.asarray(window.astype(np.float32)).astype(BF16)
     inner_rows = 8 * (len(INNER) + 5)
-    outer_rows = 8 * (len(CROSS) + len(BEFORE) + 3)
-    outer_pairs = CROSS + [(a + 6, b - 12) for a, b in BEFORE]
     phase, power, ys = call(
         inner_kernel,
         (mine, pair_table(INNER, inner_rows)),
@@ -515,18 +510,37 @@
             pltpu.VMEM((inner_rows, 256), F32),
         ],
     )
-    (sent,) = call(
-        outer_kernel,
-        (facts, pair_table(outer_pairs, outer_rows)),
-        (got0, got1, ys, power, phase, table, matrix, pair_names(CROSS + BEFORE, outer_rows)),
-        [((groups, PAIR_ROWS, 256), BF16)],
-        [
-            pltpu.VMEM((6, 2, ROWS, width), F32),
-            pltpu.VMEM((48, width), F32),
-            pltpu.VMEM((outer_rows, width), F32),
-            pltpu.VMEM((outer_rows, 256), F32),
-            pltpu.VMEM((144, 256), F32),
-        ],
+    def boundary(kernel, smem, vmem, pairs, table_pairs, out):
+        rows = 8 * (-(-len(pairs) // 8) * 8)
+        (result,) = call(
+            kernel,
+            smem + (pair_table(table_pairs, rows),),
+            vmem + (pair_names(pairs, rows),),
+            [out],
+            [
+                pltpu.VMEM((HALF, 2, ROWS, width), F32),
+                pltpu.VMEM((rows + 8 * HALF, width), F32),
+                pltpu.VMEM((rows, 256), F32),
+                pltpu.VMEM((96 + 8 * HALF, 256), F32),
+            ],
+        )
+        return result
+
+    phase = boundary(
+        after_kernel,
+        (facts,),
+        (later, ys, power, phase, table, matrix),
+        CROSS,
+        CROSS,
+        ((PAIR_ROWS, 256), F32),
+    )
+    sent = boundary(
+        before_kernel,
+        (),
+        (earlier, ys, power, phase, matrix),
+        BEFORE,
+        [(a + 3, b - 12) for a, b in BEFORE],
+        ((groups, PAIR_ROWS, 256), BF16),
     )
     phases = lax.all_to_all(sent, "date", 0, 0, tiled=True)
     (routed,) = call(series_kernel, (facts,), (phases, weight), [((8 * strips, 256), BF16)])

time: 80.9 us -> 80.2 us (level)
  starting transfers between devices: 12 us -> 14.7 us
  waiting for transfers between devices: 2.16 us -> 0.01 us
  blocking collectives: 48.5 us -> 46.7 us
    ppermute x2, starting transfers between devices: 2.6 us -> 5.3 us  [the longest x1 4.01 us: local(): lax.ppermute(edge1, 'date', [(i, i + 1) for i in range(groups - 1)])]
    ppermute x2, waiting for transfers between devices: 2.15 us -> 0.01 us  [the longest x1 0.01 us: local(): later = lax.ppermute(edge0, 'date', [(i + 1, i) for i in range(groups - 1)])]
    all_to_all x1, blocking collectives: 15.4 us -> 14 us  [local(): phases = lax.all_to_all(sent, 'date', 0, 0, tiled=True)]
    pallas_call x6 -> x7, Pallas kernels: 14 us -> 14.6 us  [call(): pl.pallas_call(kernel, in_specs=[SMEM] * len(smem) + [VMEM] * len(vmem),...]
  transfers between devices with their start and end apart: 4 -> 4, of which waited for: 1 -> 0; matrix products, arithmetic and copies ran while one was open for 1% -> 1% of each run, Pallas kernels for 9% -> 11%
where the time goes in v8:
time: 80.2 us; the launch traced here: 79.9 us
  blocking collectives  46.7 us (58%)
  Pallas kernels  16.8 us (21%)
  starting transfers between devices  14.7 us (18%)
  local copies, waits for them, and re-layouts  1.05 us (1%)
    all_to_all x1, blocking collectives, local(): lax.all_to_all(routed.reshape(strips, 8, 256), 'col', 0, 0, tiled=True)  32.6 us
    pallas_call x7, Pallas kernels, call(): pl.pallas_call(kernel, in_specs=[SMEM] * len(smem) + [VMEM] * len(vmem),...  14.6 us
    all_to_all x1, blocking collectives, local(): phases = lax.all_to_all(sent, 'date', 0, 0, tiled=True)  14 us
    ppermute x1, starting transfers between devices, local(): far = lax.ppermute(tile1, 'col', swaps(strips, 1))  4.94 us
    ppermute x1, starting transfers between devices, local(): near = lax.ppermute(tile0, 'col', swaps(strips, 0))  4.5 us
    ppermute x1, starting transfers between devices, local(): lax.ppermute(edge1, 'date', [(i, i + 1) for i in range(groups - 1)])  4.01 us
    pallas_call x1, Pallas kernels, local(): pl.pallas_call(pack_kernel, in_specs=[SMEM, pl.BlockSpec(memory_space=pl....  2.21 us
  transfers between devices with their start and end apart: 4, of which 0 were waited for; matrix products, arithmetic and copies ran while one was open for 1% of the time, Pallas kernels for 11%

profile of v8, /device:TPU:1, one launch (start us, length us, event | category | flops | bytes accessed | tf_op | source)
XLA Modules:
  0.0 79.9 jit_solution(7236580420952295859)
XLA Ops:
  0.0 2.2 %shard_map.145 = (bf16[2,40,128]{2,1,0:T(8,128)(2,1)S(1)}, bf16[2,40,128]{2,1,0:T(8,128)(2,1)S(1)}) custom-call(s32[1]{0:T(128)} %bitcast.11.odd, bf16[2,12,40,640]{3,2,1,0:T(8,128)(2,1)} %own.1), custom_call_target="tpu_custom_call" | custom-call | tf_op jit(solution)/shard_map/pallas_call | solution.py:454
  2.3 4.9 %collective-permute-start.1 = (bf16[2,40,128]{2,1,0:T(8,128)(2,1)S(1)}, bf16[2,40,128]{2,1,0:T(8,128)(2,1)S(1)}, u32[]{:S(2)}, u32[]{:S(2)}) collective-permute-start(bf16[2,40,128]{2,1,0:T(8,128)(2,1)S(1)} %get-tuple-element.15), channel_id=1, source_target_pairs={{1,2},{2,1},{3,4},{4,3},{5,6},{6,5},{7,8},{8,7},{9,10},{10,9},{11,... | collective-permute-start | bytes 61448 | tf_op jit(solution)/shard_map/ppermute | solution.py:468
  7.2 4.5 %collective-permute-start = (bf16[2,40,128]{2,1,0:T(8,128)(2,1)S(1)}, bf16[2,40,128]{2,1,0:T(8,128)(2,1)S(1)}, u32[]{:S(2)}, u32[]{:S(2)}) collective-permute-start(bf16[2,40,128]{2,1,0:T(8,128)(2,1)S(1)} %get-tuple-element.14), channel_id=1, source_target_pairs={{0,1},{1,0},{2,3},{3,2},{4,5},{5,4},{6,7},{7,6},{8,9},{9,8},{10,11... | collective-permute-start | bytes 61448 | tf_op jit(solution)/shard_map/ppermute | solution.py:467
  11.8 0.1 add_convert_fusion.1
  11.9 0.1 pad.36
  11.9 0.1 fusion.lines
  12.0 0.1 constant_dynamic-slice_fusion.table
  12.1 0.1 reduce_precision.3.own
  12.2 0.8 %copy-done.1 = bf16[191,576]{1,0:T(8,128)(2,1)S(1)} copy-done((bf16[191,576]{1,0:T(8,128)(2,1)S(1)}, bf16[191,576]{1,0:T(8,128)(2,1)}, u32[]{:S(2)}) %copy-start.1) | copy-done | bytes 220056
  13.1 0.7 shard_map.146.weight
  13.8 2.9 %shard_map.147 = (bf16[256,640]{1,0:T(8,128)(2,1)S(1)}, bf16[256,640]{1,0:T(8,128)(2,1)S(1)}) custom-call(f32[24,12]{1,0:T(8,128)S(1)} %constant_dynamic-slice_fusion.table, bf16[2,12,40,640]{3,2,1,0:T(8,128)(2,1)S(1)} %reduce_precision.3.own, bf16[2,40,128]{2,1,0:T(8,128)(2,1)S(1)} %collective-permute-done.near, ...), custom_call_target="tpu_custom_call" | custom-call | tf_op jit(solution)/shard_map/pallas_call | solution.py:406
  16.7 0.0 copy-start.3
  16.7 0.0 copy-start.4
  16.7 1.3 %collective-permute-start.3 = (bf16[256,640]{1,0:T(8,128)(2,1)S(1)}, bf16[256,640]{1,0:T(8,128)(2,1)S(1)}, u32[]{:S(2)}, u32[]{:S(2)}) collective-permute-start(bf16[256,640]{1,0:T(8,128)(2,1)S(1)} %get-tuple-element.18.edge0), channel_id=1, source_target_pairs={{32,0},{64,32},{96,64},{128,96},{160,128},{192,160},{224,192},{256... | collective-permute-start | bytes 983048 | tf_op jit(solution)/shard_map/ppermute | solution.py:489
  18.0 4.0 %collective-permute-start.2 = (bf16[256,640]{1,0:T(8,128)(2,1)S(1)}, bf16[256,640]{1,0:T(8,128)(2,1)S(1)}, u32[]{:S(2)}, u32[]{:S(2)}) collective-permute-start(bf16[256,640]{1,0:T(8,128)(2,1)S(1)} %get-tuple-element.17.edge1), channel_id=1, source_target_pairs={{0,32},{32,64},{64,96},{96,128},{128,160},{160,192},{192,224},{224... | collective-permute-start | bytes 983048 | tf_op jit(solution)/shard_map/ppermute | solution.py:490
  22.0 0.1 add_convert_fusion.facts.table
  22.1 6.3 %shard_map.148 = (f32[48,256]{1,0:T(8,128)S(1)}, f32[96,256]{1,0:T(8,128)S(1)}, f32[12,2,40,640]{3,2,1,0:T(8,128)S(1)}) custom-call(f32[24,12]{1,0:T(8,128)S(1)} %constant_dynamic-slice_fusion.table, s32[2,56]{1,0:T(2,128)S(1)} %copy-done.7, bf16[2,12,40,640]{3,2,1,0:T(8,128)(2,1)S(1)} %reduce_precision.3.own, ...), custom_call_target="tpu_custom_call" | custom-call | tf_op jit(solution)/shard_map/pallas_call | solution.py:406
  28.5 0.0 copy-start.5
  28.5 1.7 %shard_map.149.phase = f32[48,256]{1,0:T(8,128)S(1)} custom-call(f32[1,4]{1,0:T(1,128)S(1)} %add_convert_fusion.facts.table, s32[2,16]{1,0:T(2,128)S(1)} %copy-done.3, bf16[256,640]{1,0:T(8,128)(2,1)S(1)} %collective-permute-done.3.got, f32[12,2,40,640]{3,2,1,0:T(8,128)S(1)} %get-tuple-element.19.ys, f32[96,256]{1,0:T(8,128)S(1)} %get-tuple-element.20.power, ...), custom_call_target="tpu_custom_call" | custom-call | tf_op jit(solution)/shard_map/pallas_call | solution.py:406
  30.2 1.3 %shard_map.150 = bf16[16,48,256]{2,1,0:T(8,128)(2,1)S(1)} custom-call(s32[2,8]{1,0:T(2,128)S(1)} %copy-done.5, bf16[256,640]{1,0:T(8,128)(2,1)S(1)} %collective-permute-done.2.got, f32[12,2,40,640]{3,2,1,0:T(8,128)S(1)} %get-tuple-element.19.ys, f32[96,256]{1,0:T(8,128)S(1)} %get-tuple-element.20.power, f32[48,256]{1,0:T(8,128)S(1)} %shard_map.149.phase, ...), custom_call_target="tpu_custom_call" | custom-call | tf_op jit(solution)/shard_map/pallas_call | solution.py:406
  31.5 14.0 %all_to_all.10.got = bf16[16,48,256]{2,1,0:T(8,128)(2,1)S(1)} all-to-all(bf16[16,48,256]{2,1,0:T(8,128)(2,1)S(1)} %shard_map.150), channel_id=1, replica_groups=mesh['date'=16,'col'=32] {'date'}, dimensions={0} | all-to-all | bytes 786432 | tf_op jit(solution)/shard_map/all_to_all | solution.py:545
  45.6 1.0 %shard_map.151 = bf16[256,256]{1,0:T(8,128)(2,1)S(1)} custom-call(f32[1,4]{1,0:T(1,128)S(1)} %add_convert_fusion.facts.table, bf16[16,48,256]{2,1,0:T(8,128)(2,1)S(1)} %all_to_all.10.got, bf16[192,768]{1,0:T(8,128)(2,1)S(1)} %shard_map.146.weight), custom_call_target="tpu_custom_call" | custom-call | tf_op jit(solution)/shard_map/pallas_call | solution.py:406
  46.5 32.6 %all_to_all.11.got = bf16[32,8,256]{2,1,0:T(8,128)(2,1)S(1)} all-to-all(bf16[32,8,256]{2,1,0:T(8,128)(2,1)S(1)} %bitcast.19), channel_id=1, replica_groups=mesh['date'=16,'col'=32] {'col'}, dimensions={0} | all-to-all | bytes 262144 | tf_op jit(solution)/shard_map/all_to_all | solution.py:547
  79.2 0.7 shard_map.152
  (32 shorter events, 0.1 us)
Async XLA Ops:
  0.0 12.1 %copy-start.10 = (bf16[2,12,40,640]{3,2,1,0:T(8,128)(2,1)S(1)}, bf16[2,12,40,640]{3,2,1,0:T(8,128)(2,1)}, u32[]{:S(2)}) copy-start(bf16[2,12,40,640]{3,2,1,0:T(8,128)(2,1)} %own.1) | copy-start | bytes 3686404
  0.0 11.7 %copy-start.12 = (s32[192,2]{0,1:T(2,128)S(1)}, s32[192,2]{0,1:T(2,128)}, u32[]{:S(2)}) copy-start(s32[192,2]{0,1:T(2,128)} %param.16) | copy-start | bytes 4612
  0.0 11.7 %copy-start.14 = (s32[36]{0:T(128)S(1)}, s32[36]{0:T(128)}, u32[]{:S(2)}) copy-start(s32[36]{0:T(128)} %param.18) | copy-start | bytes 436
  0.0 11.9 %copy-start.11 = (f32[192,2,8]{0,2,1:T(8,128)S(1)}, f32[192,2,8]{0,2,1:T(8,128)}, u32[]{:S(2)}) copy-start(f32[192,2,8]{0,2,1:T(8,128)} %param.17) | copy-start | bytes 36868
  0.0 11.9 %copy-start.13 = (f32[191]{0:T(256)S(1)}, f32[191]{0:T(256)}, u32[]{:S(2)}) copy-start(f32[191]{0:T(256)} %param.20) | copy-start | bytes 2296
  2.3 11.5 %collective-permute-start.1 = (bf16[2,40,128]{2,1,0:T(8,128)(2,1)S(1)}, bf16[2,40,128]{2,1,0:T(8,128)(2,1)S(1)}, u32[]{:S(2)}, u32[]{:S(2)}) collective-permute-start(bf16[2,40,128]{2,1,0:T(8,128)(2,1)S(1)} %get-tuple-element.15), channel_id=1, source_target_pairs={{1,2},{2,1},{3,4},{4,3},{5,6},{6,5},{7,8},{8,7},{9,10},{10,9},{11,... | collective-permute-start | bytes 61448 | tf_op jit(solution)/shard_map/ppermute | solution.py:468
  7.2 6.6 %collective-permute-start = (bf16[2,40,128]{2,1,0:T(8,128)(2,1)S(1)}, bf16[2,40,128]{2,1,0:T(8,128)(2,1)S(1)}, u32[]{:S(2)}, u32[]{:S(2)}) collective-permute-start(bf16[2,40,128]{2,1,0:T(8,128)(2,1)S(1)} %get-tuple-element.14), channel_id=1, source_target_pairs={{0,1},{1,0},{2,3},{3,2},{4,5},{5,4},{6,7},{7,6},{8,9},{9,8},{10,11... | collective-permute-start | bytes 61448 | tf_op jit(solution)/shard_map/ppermute | solution.py:467
  12.1 0.9 %copy-start.1 = (bf16[191,576]{1,0:T(8,128)(2,1)S(1)}, bf16[191,576]{1,0:T(8,128)(2,1)}, u32[]{:S(2)}) copy-start(bf16[191,576]{1,0:T(8,128)(2,1)} %inverse.1) | copy-start | bytes 660100
  13.0 9.1 %copy-start = (bf16[640,256]{1,0:T(8,128)(2,1)S(1)}, bf16[640,256]{1,0:T(8,128)(2,1)}, u32[]{:S(2)}) copy-start(bf16[640,256]{1,0:T(8,128)(2,1)} %constant.74.matrix) | copy-start | bytes 983044
  13.0 9.1 %copy-start.2 = (f32[2,448]{1,0:T(2,128)S(1)}, f32[2,448]{1,0:T(2,128)}, u32[]{:S(2)}) copy-start(f32[2,448]{1,0:T(2,128)} %constant.51.clone.names) | copy-start | bytes 10756
  13.0 9.1 %copy-start.7 = (s32[2,56]{1,0:T(2,128)S(1)}, s32[2,56]{1,0:T(2,128)}, u32[]{:S(2)}) copy-start(s32[2,56]{1,0:T(2,128)} %constant.50.clone.pairs) | copy-start | bytes 1348
  13.0 9.1 %copy-start.8 = (s32[1,16,1]{1,2,0:T(1,128)S(1)}, s32[1,16,1]{1,2,0:T(1,128)}, u32[]{:S(2)}) copy-start(s32[1,16,1]{1,2,0:T(1,128)} %param.21) | copy-start | bytes 196
  13.0 9.1 %copy-start.9 = (s32[1,16]{1,0:T(1,128)S(1)}, s32[1,16]{1,0:T(1,128)}, u32[]{:S(2)}) copy-start(s32[1,16]{1,0:T(1,128)} %cells.1) | copy-start | bytes 196
  16.7 11.8 %copy-start.3 = (s32[2,16]{1,0:T(2,128)S(1)}, s32[2,16]{1,0:T(2,128)}, u32[]{:S(2)}) copy-start(s32[2,16]{1,0:T(2,128)} %constant.52.clone.pairs) | copy-start | bytes 388
  16.7 11.8 %copy-start.4 = (f32[2,128]{1,0:T(2,128)S(1)}, f32[2,128]{1,0:T(2,128)}, u32[]{:S(2)}) copy-start(f32[2,128]{1,0:T(2,128)} %constant.53.clone.names) | copy-start | bytes 3076
  16.7 11.7 %collective-permute-start.3 = (bf16[256,640]{1,0:T(8,128)(2,1)S(1)}, bf16[256,640]{1,0:T(8,128)(2,1)S(1)}, u32[]{:S(2)}, u32[]{:S(2)}) collective-permute-start(bf16[256,640]{1,0:T(8,128)(2,1)S(1)} %get-tuple-element.18.edge0), channel_id=1, source_target_pairs={{32,0},{64,32},{96,64},{128,96},{160,128},{192,160},{224,192},{256... | collective-permute-start | bytes 983048 | tf_op jit(solution)/shard_map/ppermute | solution.py:489
  18.0 12.2 %collective-permute-start.2 = (bf16[256,640]{1,0:T(8,128)(2,1)S(1)}, bf16[256,640]{1,0:T(8,128)(2,1)S(1)}, u32[]{:S(2)}, u32[]{:S(2)}) collective-permute-start(bf16[256,640]{1,0:T(8,128)(2,1)S(1)} %get-tuple-element.17.edge1), channel_id=1, source_target_pairs={{0,32},{32,64},{64,96},{96,128},{128,160},{160,192},{192,224},{224... | collective-permute-start | bytes 983048 | tf_op jit(solution)/shard_map/ppermute | solution.py:490
  28.5 1.7 %copy-start.5 = (s32[2,8]{1,0:T(2,128)S(1)}, s32[2,8]{1,0:T(2,128)}, u32[]{:S(2)}) copy-start(s32[2,8]{1,0:T(2,128)} %constant.54.clone.pairs) | copy-start | bytes 196
  28.5 1.7 %copy-start.6 = (f32[2,64]{1,0:T(2,128)S(1)}, f32[2,64]{1,0:T(2,128)}, u32[]{:S(2)}) copy-start(f32[2,64]{1,0:T(2,128)} %constant.55.clone.names) | copy-start | bytes 1540

commit v9 on v8

--- a/solution.py
+++ b/solution.py
@@ -74,7 +74,7 @@
         tap_weights(table, date, weights.at[s])
     for s, date in enumerate(dates):
         for part in range(2):
-            tile_a, tile_b = near[part].astype(F32), far[part].astype(F32)
+            tile_a, tile_b = near[part].astype(F32), far[part, 0:ROWS].astype(F32)
             left = pltpu.roll(jnp.where(is_odd, tile_a, tile_b), LANES - HALO - HALO * date, 1)
             right = pltpu.roll(
                 jnp.where(is_odd, tile_b, tile_a), lax.rem(LANES - HALO * date, LANES), 1
@@ -120,7 +120,7 @@
     return jnp.sum(jnp.where(at, row, 0.0), axis=1, keepdims=True)
 
 
-def pack_kernel(odd, own, out0, out1, ends, acc, sems):
+def pack_kernel(odd, own, out0, out1, ends, sems):
     far = own.shape[3] - LANES
     even = odd[0] == 0
     copies = [
@@ -129,22 +129,26 @@
     ]
     for copy in copies:
         copy.start()
-    acc[...] = jnp.zeros_like(acc)
+    lane = iota((ROWS, LANES), 1) // HALO
     for copy in copies:
         copy.wait()
 
-    def one(d, _):
-        for part in range(2):
-            head = pltpu.roll(ends[0, part, d].astype(F32), HALO * d, 1)
-            tail = pltpu.roll(ends[1, part, d].astype(F32), HALO * d + HALO, 1)
-            here = iota(head.shape, 1) // HALO == d
-            for n, tile in enumerate((jnp.where(even, tail, head), jnp.where(even, head, tail))):
-                acc[n, part] = jnp.where(here, tile, acc[n, part])
-        return 0
-
-    lax.fori_loop(0, own.shape[1], one, 0)
-    out0[...] = acc[0].astype(BF16)
-    out1[...] = acc[1].astype(BF16)
+    def one(d, totals):
+        here = lane == d
+        rolled = [
+            pltpu.roll(ends[n, part, d].astype(F32), HALO * d + HALO * n, 1)
+            for part in range(2)
+            for n in range(2)
+        ]
+        return tuple(jnp.where(here, r, t) for r, t in zip(rolled, totals))
+
+    zero = jnp.zeros((ROWS, LANES), F32)
+    totals = lax.fori_loop(0, own.shape[1], one, (zero,) * 4, unroll=4)
+    for part in range(2):
+        head, tail = totals[2 * part], totals[2 * part + 1]
+        out0[part] = jnp.where(even, tail, head).astype(BF16)
+        out1[part, 0:ROWS] = jnp.where(even, head, tail).astype(BF16)
+        out1[part, ROWS:] = jnp.zeros((8, LANES), BF16)
 
 
 def edge_kernel(table, own, near, far, lines, head, tail, lhs, weights, zs):
@@ -455,10 +459,9 @@
         pack_kernel,
         in_specs=[SMEM, pl.BlockSpec(memory_space=pl.ANY)],
         out_specs=[VMEM] * 2,
-        out_shape=[tile] * 2,
+        out_shape=[tile, jax.ShapeDtypeStruct((2, ROWS + 8, LANES), BF16)],
         scratch_shapes=[
             pltpu.VMEM((2,) + slc_stack.shape[:3] + (LANES,), BF16),
-            pltpu.VMEM((2, 2, ROWS, LANES), F32),
             pltpu.SemaphoreType.DMA((2,)),
         ],
         compiler_params=pltpu.CompilerParams(vmem_limit_bytes=53 * 1024 * 1024),
@@ -473,7 +476,6 @@
         [((DATES, groups * PAIR_ROWS), BF16)],
         [pltpu.VMEM((inverse.shape[1], groups * PAIR_ROWS), BF16)],
     )
-    far, weight = lax.optimization_barrier((far, weight))
     scratch = [
         pltpu.VMEM((2, 2 * ROWS * width // LANES, 2 * LANES), BF16),
         pltpu.VMEM((2, 4 * LANES, 2 * LANES), BF16),
@@ -526,6 +528,7 @@
         )
         return result
 
+    later, weight = lax.optimization_barrier((later, weight))
     phase = boundary(
         after_kernel,
         (facts,),

time: 80.2 us -> 79.3 us (0.989)
  local copies, waits for them, and re-layouts: 1.05 us -> 0.24 us
    unnamed x30, local copies, waits for them, and re-layouts: 0.9 us -> 0.09 us
  transfers between devices with their start and end apart: 4 -> 4, of which waited for: 0 -> 1; matrix products, arithmetic and copies ran while one was open for 1% -> 1% of each run, Pallas kernels for 11% -> 11%
where the time goes in v9:
time: 79.3 us; the launch traced here: 79 us
  blocking collectives  47 us (59%)
  Pallas kernels  16.1 us (20%)
  starting transfers between devices  14.7 us (19%)
    all_to_all x1, blocking collectives, local(): lax.all_to_all(routed.reshape(strips, 8, 256), 'col', 0, 0, tiled=True)  32.5 us
    pallas_call x7, Pallas kernels, call(): pl.pallas_call(kernel, in_specs=[SMEM] * len(smem) + [VMEM] * len(vmem),...  14.5 us
    all_to_all x1, blocking collectives, local(): phases = lax.all_to_all(sent, 'date', 0, 0, tiled=True)  14.5 us
    ppermute x1, starting transfers between devices, local(): far = lax.ppermute(tile1, 'col', swaps(strips, 1))  4.94 us
    ppermute x1, starting transfers between devices, local(): near = lax.ppermute(tile0, 'col', swaps(strips, 0))  4.5 us
    ppermute x1, starting transfers between devices, local(): lax.ppermute(edge1, 'date', [(i, i + 1) for i in range(groups - 1)])  4.01 us
  transfers between devices with their start and end apart: 4, of which 1 were waited for; matrix products, arithmetic and copies ran while one was open for 1% of the time, Pallas kernels for 11%

profile of v9, /device:TPU:1, one launch (start us, length us, event | category | flops | bytes accessed | tf_op | source)
XLA Modules:
  0.0 79.0 jit_solution(2250354540196095991)
XLA Ops:
  0.0 1.5 %shard_map.145 = (bf16[2,40,128]{2,1,0:T(8,128)(2,1)S(1)}, bf16[2,48,128]{2,1,0:T(8,128)(2,1)S(1)}) custom-call(s32[1]{0:T(128)} %bitcast.11.odd, bf16[2,12,40,640]{3,2,1,0:T(8,128)(2,1)} %own.1), custom_call_target="tpu_custom_call" | custom-call | tf_op jit(solution)/shard_map/pallas_call | solution.py:458
  1.6 4.9 %collective-permute-start.1 = (bf16[2,48,128]{2,1,0:T(8,128)(2,1)S(1)}, bf16[2,48,128]{2,1,0:T(8,128)(2,1)S(1)}, u32[]{:S(2)}, u32[]{:S(2)}) collective-permute-start(bf16[2,48,128]{2,1,0:T(8,128)(2,1)S(1)} %get-tuple-element.15), channel_id=1, source_target_pairs={{1,2},{2,1},{3,4},{4,3},{5,6},{6,5},{7,8},{8,7},{9,10},{10,9},{11,... | collective-permute-start | bytes 73736 | tf_op jit(solution)/shard_map/ppermute | solution.py:471
  6.5 4.5 %collective-permute-start = (bf16[2,40,128]{2,1,0:T(8,128)(2,1)S(1)}, bf16[2,40,128]{2,1,0:T(8,128)(2,1)S(1)}, u32[]{:S(2)}, u32[]{:S(2)}) collective-permute-start(bf16[2,40,128]{2,1,0:T(8,128)(2,1)S(1)} %get-tuple-element.14), channel_id=1, source_target_pairs={{0,1},{1,0},{2,3},{3,2},{4,5},{5,4},{6,7},{7,6},{8,9},{9,8},{10,11... | collective-permute-start | bytes 61448 | tf_op jit(solution)/shard_map/ppermute | solution.py:470
  11.1 0.1 add_convert_fusion.1
  11.2 0.1 pad.36
  11.3 0.1 fusion.lines
  11.3 0.1 constant_dynamic-slice_fusion.table
  11.4 0.1 reduce_precision.3.own
  11.5 0.0 copy-start
  11.6 0.0 copy-start.7
  11.6 0.3 collective-permute-done.near
  11.9 2.9 %shard_map.146 = (bf16[256,640]{1,0:T(8,128)(2,1)S(1)}, bf16[256,640]{1,0:T(8,128)(2,1)S(1)}) custom-call(f32[24,12]{1,0:T(8,128)S(1)} %constant_dynamic-slice_fusion.table, bf16[2,12,40,640]{3,2,1,0:T(8,128)(2,1)S(1)} %reduce_precision.3.own, bf16[2,40,128]{2,1,0:T(8,128)(2,1)S(1)} %collective-permute-done.near, ...), custom_call_target="tpu_custom_call" | custom-call | tf_op jit(solution)/shard_map/pallas_call | solution.py:410
  14.7 1.3 %collective-permute-start.3 = (bf16[256,640]{1,0:T(8,128)(2,1)S(1)}, bf16[256,640]{1,0:T(8,128)(2,1)S(1)}, u32[]{:S(2)}, u32[]{:S(2)}) collective-permute-start(bf16[256,640]{1,0:T(8,128)(2,1)S(1)} %get-tuple-element.17.edge0), channel_id=1, source_target_pairs={{32,0},{64,32},{96,64},{128,96},{160,128},{192,160},{224,192},{256... | collective-permute-start | bytes 983048 | tf_op jit(solution)/shard_map/ppermute | solution.py:491
  16.0 4.0 %collective-permute-start.2 = (bf16[256,640]{1,0:T(8,128)(2,1)S(1)}, bf16[256,640]{1,0:T(8,128)(2,1)S(1)}, u32[]{:S(2)}, u32[]{:S(2)}) collective-permute-start(bf16[256,640]{1,0:T(8,128)(2,1)S(1)} %get-tuple-element.16.edge1), channel_id=1, source_target_pairs={{0,32},{32,64},{64,96},{96,128},{128,160},{160,192},{192,224},{224... | collective-permute-start | bytes 983048 | tf_op jit(solution)/shard_map/ppermute | solution.py:492
  20.1 0.7 shard_map.148.weight
  20.8 0.0 copy-start.3
  20.8 0.1 add_convert_fusion.facts.table
  20.9 6.3 %shard_map.147 = (f32[48,256]{1,0:T(8,128)S(1)}, f32[96,256]{1,0:T(8,128)S(1)}, f32[12,2,40,640]{3,2,1,0:T(8,128)S(1)}) custom-call(f32[24,12]{1,0:T(8,128)S(1)} %constant_dynamic-slice_fusion.table, s32[2,56]{1,0:T(2,128)S(1)} %copy-done.7, bf16[2,12,40,640]{3,2,1,0:T(8,128)(2,1)S(1)} %reduce_precision.3.own, ...), custom_call_target="tpu_custom_call" | custom-call | tf_op jit(solution)/shard_map/pallas_call | solution.py:410
  27.3 1.7 %shard_map.149.phase = f32[48,256]{1,0:T(8,128)S(1)} custom-call(f32[1,4]{1,0:T(1,128)S(1)} %add_convert_fusion.facts.table, s32[2,16]{1,0:T(2,128)S(1)} %copy-done.3, bf16[256,640]{1,0:T(8,128)(2,1)S(1)} %collective-permute-done.3.got, f32[12,2,40,640]{3,2,1,0:T(8,128)S(1)} %get-tuple-element.18.ys, f32[96,256]{1,0:T(8,128)S(1)} %get-tuple-element.19.power, ...), custom_call_target="tpu_custom_call" | custom-call | tf_op jit(solution)/shard_map/pallas_call | solution.py:410
  29.0 1.3 %shard_map.150 = bf16[16,48,256]{2,1,0:T(8,128)(2,1)S(1)} custom-call(s32[2,8]{1,0:T(2,128)S(1)} %copy-done.5, bf16[256,640]{1,0:T(8,128)(2,1)S(1)} %collective-permute-done.2.got, f32[12,2,40,640]{3,2,1,0:T(8,128)S(1)} %get-tuple-element.18.ys, f32[96,256]{1,0:T(8,128)S(1)} %get-tuple-element.19.power, f32[48,256]{1,0:T(8,128)S(1)} %shard_map.149.phase, ...), custom_call_target="tpu_custom_call" | custom-call | tf_op jit(solution)/shard_map/pallas_call | solution.py:410
  30.3 14.5 %all_to_all.10.got = bf16[16,48,256]{2,1,0:T(8,128)(2,1)S(1)} all-to-all(bf16[16,48,256]{2,1,0:T(8,128)(2,1)S(1)} %shard_map.150), channel_id=1, replica_groups=mesh['date'=16,'col'=32] {'date'}, dimensions={0} | all-to-all | bytes 786432 | tf_op jit(solution)/shard_map/all_to_all | solution.py:548
  44.8 1.0 %shard_map.151 = bf16[256,256]{1,0:T(8,128)(2,1)S(1)} custom-call(f32[1,4]{1,0:T(1,128)S(1)} %add_convert_fusion.facts.table, bf16[16,48,256]{2,1,0:T(8,128)(2,1)S(1)} %all_to_all.10.got, bf16[192,768]{1,0:T(8,128)(2,1)S(1)} %shard_map.148.weight), custom_call_target="tpu_custom_call" | custom-call | tf_op jit(solution)/shard_map/pallas_call | solution.py:410
  45.8 32.5 %all_to_all.11.got = bf16[32,8,256]{2,1,0:T(8,128)(2,1)S(1)} all-to-all(bf16[32,8,256]{2,1,0:T(8,128)(2,1)S(1)} %bitcast.19), channel_id=1, replica_groups=mesh['date'=16,'col'=32] {'col'}, dimensions={0} | all-to-all | bytes 262144 | tf_op jit(solution)/shard_map/all_to_all | solution.py:550
  78.3 0.7 shard_map.152
  (32 shorter events, 0.1 us)
Async XLA Ops:
  0.0 11.4 %copy-start.10 = (bf16[2,12,40,640]{3,2,1,0:T(8,128)(2,1)S(1)}, bf16[2,12,40,640]{3,2,1,0:T(8,128)(2,1)}, u32[]{:S(2)}) copy-start(bf16[2,12,40,640]{3,2,1,0:T(8,128)(2,1)} %own.1) | copy-start | bytes 3686404
  0.0 11.0 %copy-start.12 = (s32[192,2]{0,1:T(2,128)S(1)}, s32[192,2]{0,1:T(2,128)}, u32[]{:S(2)}) copy-start(s32[192,2]{0,1:T(2,128)} %param.16) | copy-start | bytes 4612
  0.0 11.1 %copy-start.14 = (s32[36]{0:T(128)S(1)}, s32[36]{0:T(128)}, u32[]{:S(2)}) copy-start(s32[36]{0:T(128)} %param.18) | copy-start | bytes 436
  0.0 11.2 %copy-start.11 = (f32[192,2,8]{0,2,1:T(8,128)S(1)}, f32[192,2,8]{0,2,1:T(8,128)}, u32[]{:S(2)}) copy-start(f32[192,2,8]{0,2,1:T(8,128)} %param.17) | copy-start | bytes 36868
  0.0 11.2 %copy-start.13 = (f32[191]{0:T(256)S(1)}, f32[191]{0:T(256)}, u32[]{:S(2)}) copy-start(f32[191]{0:T(256)} %param.20) | copy-start | bytes 2296
  1.6 10.3 %collective-permute-start.1 = (bf16[2,48,128]{2,1,0:T(8,128)(2,1)S(1)}, bf16[2,48,128]{2,1,0:T(8,128)(2,1)S(1)}, u32[]{:S(2)}, u32[]{:S(2)}) collective-permute-start(bf16[2,48,128]{2,1,0:T(8,128)(2,1)S(1)} %get-tuple-element.15), channel_id=1, source_target_pairs={{1,2},{2,1},{3,4},{4,3},{5,6},{6,5},{7,8},{8,7},{9,10},{10,9},{11,... | collective-permute-start | bytes 73736 | tf_op jit(solution)/shard_map/ppermute | solution.py:471
  6.5 5.3 %collective-permute-start = (bf16[2,40,128]{2,1,0:T(8,128)(2,1)S(1)}, bf16[2,40,128]{2,1,0:T(8,128)(2,1)S(1)}, u32[]{:S(2)}, u32[]{:S(2)}) collective-permute-start(bf16[2,40,128]{2,1,0:T(8,128)(2,1)S(1)} %get-tuple-element.14), channel_id=1, source_target_pairs={{0,1},{1,0},{2,3},{3,2},{4,5},{5,4},{6,7},{7,6},{8,9},{9,8},{10,11... | collective-permute-start | bytes 61448 | tf_op jit(solution)/shard_map/ppermute | solution.py:470
  11.5 8.5 %copy-start.1 = (bf16[191,576]{1,0:T(8,128)(2,1)S(1)}, bf16[191,576]{1,0:T(8,128)(2,1)}, u32[]{:S(2)}) copy-start(bf16[191,576]{1,0:T(8,128)(2,1)} %inverse.1) | copy-start | bytes 660100
  11.5 9.3 %copy-start = (bf16[640,256]{1,0:T(8,128)(2,1)S(1)}, bf16[640,256]{1,0:T(8,128)(2,1)}, u32[]{:S(2)}) copy-start(bf16[640,256]{1,0:T(8,128)(2,1)} %constant.74.matrix) | copy-start | bytes 983044
  11.6 9.3 %copy-start.2 = (f32[2,448]{1,0:T(2,128)S(1)}, f32[2,448]{1,0:T(2,128)}, u32[]{:S(2)}) copy-start(f32[2,448]{1,0:T(2,128)} %constant.51.clone.names) | copy-start | bytes 10756
  11.6 9.3 %copy-start.7 = (s32[2,56]{1,0:T(2,128)S(1)}, s32[2,56]{1,0:T(2,128)}, u32[]{:S(2)}) copy-start(s32[2,56]{1,0:T(2,128)} %constant.50.clone.pairs) | copy-start | bytes 1348
  11.6 9.3 %copy-start.8 = (s32[1,16,1]{1,2,0:T(1,128)S(1)}, s32[1,16,1]{1,2,0:T(1,128)}, u32[]{:S(2)}) copy-start(s32[1,16,1]{1,2,0:T(1,128)} %param.21) | copy-start | bytes 196
  11.6 9.3 %copy-start.9 = (s32[1,16]{1,0:T(1,128)S(1)}, s32[1,16]{1,0:T(1,128)}, u32[]{:S(2)}) copy-start(s32[1,16]{1,0:T(1,128)} %cells.1) | copy-start | bytes 196
  14.7 12.5 %collective-permute-start.3 = (bf16[256,640]{1,0:T(8,128)(2,1)S(1)}, bf16[256,640]{1,0:T(8,128)(2,1)S(1)}, u32[]{:S(2)}, u32[]{:S(2)}) collective-permute-start(bf16[256,640]{1,0:T(8,128)(2,1)S(1)} %get-tuple-element.17.edge0), channel_id=1, source_target_pairs={{32,0},{64,32},{96,64},{128,96},{160,128},{192,160},{224,192},{256... | collective-permute-start | bytes 983048 | tf_op jit(solution)/shard_map/ppermute | solution.py:491
  16.0 12.9 %collective-permute-start.2 = (bf16[256,640]{1,0:T(8,128)(2,1)S(1)}, bf16[256,640]{1,0:T(8,128)(2,1)S(1)}, u32[]{:S(2)}, u32[]{:S(2)}) collective-permute-start(bf16[256,640]{1,0:T(8,128)(2,1)S(1)} %get-tuple-element.16.edge1), channel_id=1, source_target_pairs={{0,32},{32,64},{64,96},{96,128},{128,160},{160,192},{192,224},{224... | collective-permute-start | bytes 983048 | tf_op jit(solution)/shard_map/ppermute | solution.py:492
  20.8 6.5 %copy-start.3 = (s32[2,16]{1,0:T(2,128)S(1)}, s32[2,16]{1,0:T(2,128)}, u32[]{:S(2)}) copy-start(s32[2,16]{1,0:T(2,128)} %constant.52.clone.pairs) | copy-start | bytes 388
  20.8 6.5 %copy-start.4 = (f32[2,128]{1,0:T(2,128)S(1)}, f32[2,128]{1,0:T(2,128)}, u32[]{:S(2)}) copy-start(f32[2,128]{1,0:T(2,128)} %constant.53.clone.names) | copy-start | bytes 3076
  27.2 1.7 %copy-start.5 = (s32[2,8]{1,0:T(2,128)S(1)}, s32[2,8]{1,0:T(2,128)}, u32[]{:S(2)}) copy-start(s32[2,8]{1,0:T(2,128)} %constant.54.clone.pairs) | copy-start | bytes 196
  27.3 1.7 %copy-start.6 = (f32[2,64]{1,0:T(2,128)S(1)}, f32[2,64]{1,0:T(2,128)}, u32[]{:S(2)}) copy-start(f32[2,64]{1,0:T(2,128)} %constant.55.clone.names) | copy-start | bytes 1540

commit v10 on v9

--- a/solution.py
+++ b/solution.py
@@ -371,30 +371,45 @@
         out[g] = total.astype(BF16)
 
 
-def series_kernel(table, got, weight, out):
+def series_kernel(table, got, weight, out, sums):
     stack = jnp.concatenate([got[g] for g in range(got.shape[0])], axis=0)
     series = jnp.dot(weight[...], stack, preferred_element_type=F32)
     wide = series.shape[1]
-    rows = jnp.where(iota(series.shape, 0) == 191, 1.0, series)
-    rows = jnp.concatenate([rows, jnp.zeros((64, wide), F32)], axis=0).astype(BF16)
+    rows = jnp.where(iota(series.shape, 0) == DATES - 1, 1.0, series).astype(BF16)
+    none = jnp.zeros_like(rows)
     codes = got[0, 40:48, :].astype(F32)
     for g in range(1, got.shape[0]):
         codes = codes + got[g, 40:48, :].astype(F32)
     owner, cell = codes[6:7, :], codes[7:8, :]
-    base = fact(table, 3).astype(F32) * 8.0
-    mine = (cell >= base) & (cell < base + 8)
-    target = jnp.where(mine, owner * 8 + cell - base, -1.0).astype(jnp.int32)
-    select = (iota((out.shape[0], wide), 0) == target).astype(BF16)
-    out[...] = lax.dot_general(
-        select, rows, (((1,), (1,)), ((), ())), preferred_element_type=F32
-    ).astype(BF16)
+    cell = cell - fact(table, 3).astype(F32) * 8.0
+    select = []
+    for base in (0.0, 4.0):
+        mine = (cell >= base) & (cell < base + 4.0)
+        target = jnp.where(mine, owner * 4.0 + cell - base, -1.0).astype(jnp.int32)
+        select.append((iota((sums.shape[0], wide), 0) == target).astype(BF16))
+    sums[...] = lax.dot_general(
+        jnp.concatenate(select, axis=1),
+        jnp.concatenate(
+            [jnp.concatenate([rows, none], axis=0), jnp.concatenate([none, rows], axis=0)], axis=1
+        ),
+        (((1,), (1,)), ((), ())),
+        preferred_element_type=F32,
+    )
+
+    def one(n, _):
+        both = sums[pl.ds(pl.multiple_of(8 * n, 8), 8), :].astype(BF16)
+        out[2 * n], out[2 * n + 1] = both[:4], both[4:]
+        return 0
+
+    lax.fori_loop(0, out.shape[0] // 2, one, 0, unroll=4)
 
 
 def final_kernel(got, lines, out):
     total = got[0].astype(F32)
     for g in range(1, got.shape[0]):
         total = total + got[g].astype(F32)
-    total = total[:, 0:DATES]
+    turned = pltpu.roll(total, DATES, 1)
+    total = jnp.concatenate([total[:, 0:DATES], turned[:, 0:DATES]], axis=0)
     lane = iota(total.shape, 1)
     counts = jnp.sum(jnp.where(lane == DATES - 1, total, 0.0), axis=1, keepdims=True)
     velocity = jnp.sum(total * lines[19:20, :], axis=1, keepdims=True)
@@ -546,8 +561,14 @@
         ((groups, PAIR_ROWS, 256), BF16),
     )
     phases = lax.all_to_all(sent, "date", 0, 0, tiled=True)
-    (routed,) = call(series_kernel, (facts,), (phases, weight), [((8 * strips, 256), BF16)])
-    parts = lax.all_to_all(routed.reshape(strips, 8, 256), "col", 0, 0, tiled=True)
+    (routed,) = call(
+        series_kernel,
+        (facts,),
+        (phases, weight),
+        [((strips, 4, 2 * DATES), BF16)],
+        [pltpu.VMEM((4 * strips, 2 * DATES), F32)],
+    )
+    parts = lax.all_to_all(routed, "col", 0, 0, tiled=True)
     (mean,) = call(final_kernel, (), (parts, table), [((8, DATES), F32)])
     return mean.reshape(1, 8, DATES)
 

time: 79.3 us -> 78.4 us (0.989)
  blocking collectives: 47 us -> 45.9 us
    all_to_all x1, blocking collectives: 32.5 us -> 31.4 us  [local(): parts = lax.all_to_all(routed, 'col', 0, 0, tiled=True)]
where the time goes in v10:
time: 78.4 us; the launch traced here: 78.1 us
  blocking collectives  45.9 us (59%)
  Pallas kernels  16.3 us (21%)
  starting transfers between devices  14.7 us (19%)
    all_to_all x1, blocking collectives, local(): parts = lax.all_to_all(routed, 'col', 0, 0, tiled=True)  31.4 us
    pallas_call x7, Pallas kernels, call(): pl.pallas_call(kernel, in_specs=[SMEM] * len(smem) + [VMEM] * len(vmem),...  14.8 us
    all_to_all x1, blocking collectives, local(): phases = lax.all_to_all(sent, 'date', 0, 0, tiled=True)  14.5 us
    ppermute x1, starting transfers between devices, local(): far = lax.ppermute(tile1, 'col', swaps(strips, 1))  4.94 us
    ppermute x1, starting transfers between devices, local(): near = lax.ppermute(tile0, 'col', swaps(strips, 0))  4.5 us
    ppermute x1, starting transfers between devices, local(): lax.ppermute(edge1, 'date', [(i, i + 1) for i in range(groups - 1)])  4.01 us
  transfers between devices with their start and end apart: 4, of which 1 were waited for; matrix products, arithmetic and copies ran while one was open for 1% of the time, Pallas kernels for 11%

profile of v10, /device:TPU:1, one launch (start us, length us, event | category | flops | bytes accessed | tf_op | source)
XLA Modules:
  0.0 78.1 jit_solution(18341254166086803067)
XLA Ops:
  0.0 1.5 %shard_map.145 = (bf16[2,40,128]{2,1,0:T(8,128)(2,1)S(1)}, bf16[2,48,128]{2,1,0:T(8,128)(2,1)S(1)}) custom-call(s32[1]{0:T(128)} %bitcast.11.odd, bf16[2,12,40,640]{3,2,1,0:T(8,128)(2,1)} %own.1), custom_call_target="tpu_custom_call" | custom-call | tf_op jit(solution)/shard_map/pallas_call | solution.py:473
  1.6 4.9 %collective-permute-start.1 = (bf16[2,48,128]{2,1,0:T(8,128)(2,1)S(1)}, bf16[2,48,128]{2,1,0:T(8,128)(2,1)S(1)}, u32[]{:S(2)}, u32[]{:S(2)}) collective-permute-start(bf16[2,48,128]{2,1,0:T(8,128)(2,1)S(1)} %get-tuple-element.15), channel_id=1, source_target_pairs={{1,2},{2,1},{3,4},{4,3},{5,6},{6,5},{7,8},{8,7},{9,10},{10,9},{11,... | collective-permute-start | bytes 73736 | tf_op jit(solution)/shard_map/ppermute | solution.py:486
  6.5 4.5 %collective-permute-start = (bf16[2,40,128]{2,1,0:T(8,128)(2,1)S(1)}, bf16[2,40,128]{2,1,0:T(8,128)(2,1)S(1)}, u32[]{:S(2)}, u32[]{:S(2)}) collective-permute-start(bf16[2,40,128]{2,1,0:T(8,128)(2,1)S(1)} %get-tuple-element.14), channel_id=1, source_target_pairs={{0,1},{1,0},{2,3},{3,2},{4,5},{5,4},{6,7},{7,6},{8,9},{9,8},{10,11... | collective-permute-start | bytes 61448 | tf_op jit(solution)/shard_map/ppermute | solution.py:485
  11.1 0.1 add_convert_fusion.1
  11.2 0.1 pad.36
  11.3 0.1 fusion.lines
  11.3 0.1 constant_dynamic-slice_fusion.table
  11.4 0.1 reduce_precision.3.own
  11.5 0.0 copy-start
  11.6 0.0 copy-start.7
  11.6 0.3 collective-permute-done.near
  11.9 2.9 %shard_map.146 = (bf16[256,640]{1,0:T(8,128)(2,1)S(1)}, bf16[256,640]{1,0:T(8,128)(2,1)S(1)}) custom-call(f32[24,12]{1,0:T(8,128)S(1)} %constant_dynamic-slice_fusion.table, bf16[2,12,40,640]{3,2,1,0:T(8,128)(2,1)S(1)} %reduce_precision.3.own, bf16[2,40,128]{2,1,0:T(8,128)(2,1)S(1)} %collective-permute-done.near, ...), custom_call_target="tpu_custom_call" | custom-call | tf_op jit(solution)/shard_map/pallas_call | solution.py:425
  14.7 1.3 %collective-permute-start.3 = (bf16[256,640]{1,0:T(8,128)(2,1)S(1)}, bf16[256,640]{1,0:T(8,128)(2,1)S(1)}, u32[]{:S(2)}, u32[]{:S(2)}) collective-permute-start(bf16[256,640]{1,0:T(8,128)(2,1)S(1)} %get-tuple-element.17.edge0), channel_id=1, source_target_pairs={{32,0},{64,32},{96,64},{128,96},{160,128},{192,160},{224,192},{256... | collective-permute-start | bytes 983048 | tf_op jit(solution)/shard_map/ppermute | solution.py:506
  16.0 4.0 %collective-permute-start.2 = (bf16[256,640]{1,0:T(8,128)(2,1)S(1)}, bf16[256,640]{1,0:T(8,128)(2,1)S(1)}, u32[]{:S(2)}, u32[]{:S(2)}) collective-permute-start(bf16[256,640]{1,0:T(8,128)(2,1)S(1)} %get-tuple-element.16.edge1), channel_id=1, source_target_pairs={{0,32},{32,64},{64,96},{96,128},{128,160},{160,192},{192,224},{224... | collective-permute-start | bytes 983048 | tf_op jit(solution)/shard_map/ppermute | solution.py:507
  20.1 0.7 shard_map.148.weight
  20.8 0.0 copy-start.3
  20.8 0.1 add_convert_fusion.facts.table
  20.9 6.3 %shard_map.147 = (f32[48,256]{1,0:T(8,128)S(1)}, f32[96,256]{1,0:T(8,128)S(1)}, f32[12,2,40,640]{3,2,1,0:T(8,128)S(1)}) custom-call(f32[24,12]{1,0:T(8,128)S(1)} %constant_dynamic-slice_fusion.table, s32[2,56]{1,0:T(2,128)S(1)} %copy-done.7, bf16[2,12,40,640]{3,2,1,0:T(8,128)(2,1)S(1)} %reduce_precision.3.own, ...), custom_call_target="tpu_custom_call" | custom-call | tf_op jit(solution)/shard_map/pallas_call | solution.py:425
  27.3 1.7 %shard_map.149.phase = f32[48,256]{1,0:T(8,128)S(1)} custom-call(f32[1,4]{1,0:T(1,128)S(1)} %add_convert_fusion.facts.table, s32[2,16]{1,0:T(2,128)S(1)} %copy-done.3, bf16[256,640]{1,0:T(8,128)(2,1)S(1)} %collective-permute-done.3.got, f32[12,2,40,640]{3,2,1,0:T(8,128)S(1)} %get-tuple-element.18.ys, f32[96,256]{1,0:T(8,128)S(1)} %get-tuple-element.19.power, ...), custom_call_target="tpu_custom_call" | custom-call | tf_op jit(solution)/shard_map/pallas_call | solution.py:425
  29.0 1.3 %shard_map.150 = bf16[16,48,256]{2,1,0:T(8,128)(2,1)S(1)} custom-call(s32[2,8]{1,0:T(2,128)S(1)} %copy-done.5, bf16[256,640]{1,0:T(8,128)(2,1)S(1)} %collective-permute-done.2.got, f32[12,2,40,640]{3,2,1,0:T(8,128)S(1)} %get-tuple-element.18.ys, f32[96,256]{1,0:T(8,128)S(1)} %get-tuple-element.19.power, f32[48,256]{1,0:T(8,128)S(1)} %shard_map.149.phase, ...), custom_call_target="tpu_custom_call" | custom-call | tf_op jit(solution)/shard_map/pallas_call | solution.py:425
  30.3 14.5 %all_to_all.10.got = bf16[16,48,256]{2,1,0:T(8,128)(2,1)S(1)} all-to-all(bf16[16,48,256]{2,1,0:T(8,128)(2,1)S(1)} %shard_map.150), channel_id=1, replica_groups=mesh['date'=16,'col'=32] {'date'}, dimensions={0} | all-to-all | bytes 786432 | tf_op jit(solution)/shard_map/all_to_all | solution.py:563
  44.8 1.2 %shard_map.151 = bf16[32,4,384]{2,1,0:T(4,128)(2,1)S(1)} custom-call(f32[1,4]{1,0:T(1,128)S(1)} %add_convert_fusion.facts.table, bf16[16,48,256]{2,1,0:T(8,128)(2,1)S(1)} %all_to_all.10.got, bf16[192,768]{1,0:T(8,128)(2,1)S(1)} %shard_map.148.weight), custom_call_target="tpu_custom_call" | custom-call | tf_op jit(solution)/shard_map/pallas_call | solution.py:425
  45.9 31.4 %all_to_all.11.got = bf16[32,4,384]{2,1,0:T(4,128)(2,1)S(1)} all-to-all(bf16[32,4,384]{2,1,0:T(4,128)(2,1)S(1)} %shard_map.151), channel_id=1, replica_groups=mesh['date'=16,'col'=32] {'col'}, dimensions={0} | all-to-all | bytes 196608 | tf_op jit(solution)/shard_map/all_to_all | solution.py:571
  77.4 0.8 %shard_map.152 = f32[8,192]{1,0:T(8,128)} custom-call(bf16[32,4,384]{2,1,0:T(4,128)(2,1)S(1)} %all_to_all.11.got, f32[24,192]{1,0:T(8,128)S(1)} %fusion.lines), custom_call_target="tpu_custom_call" | custom-call | tf_op jit(solution)/shard_map/pallas_call | solution.py:425
  (32 shorter events, 0.1 us)
Async XLA Ops:
  0.0 11.4 %copy-start.10 = (bf16[2,12,40,640]{3,2,1,0:T(8,128)(2,1)S(1)}, bf16[2,12,40,640]{3,2,1,0:T(8,128)(2,1)}, u32[]{:S(2)}) copy-start(bf16[2,12,40,640]{3,2,1,0:T(8,128)(2,1)} %own.1) | copy-start | bytes 3686404
  0.0 11.0 %copy-start.12 = (s32[192,2]{0,1:T(2,128)S(1)}, s32[192,2]{0,1:T(2,128)}, u32[]{:S(2)}) copy-start(s32[192,2]{0,1:T(2,128)} %param.16) | copy-start | bytes 4612
  0.0 11.1 %copy-start.14 = (s32[36]{0:T(128)S(1)}, s32[36]{0:T(128)}, u32[]{:S(2)}) copy-start(s32[36]{0:T(128)} %param.18) | copy-start | bytes 436
  0.0 11.2 %copy-start.11 = (f32[192,2,8]{0,2,1:T(8,128)S(1)}, f32[192,2,8]{0,2,1:T(8,128)}, u32[]{:S(2)}) copy-start(f32[192,2,8]{0,2,1:T(8,128)} %param.17) | copy-start | bytes 36868
  0.0 11.2 %copy-start.13 = (f32[191]{0:T(256)S(1)}, f32[191]{0:T(256)}, u32[]{:S(2)}) copy-start(f32[191]{0:T(256)} %param.20) | copy-start | bytes 2296
  1.6 10.3 %collective-permute-start.1 = (bf16[2,48,128]{2,1,0:T(8,128)(2,1)S(1)}, bf16[2,48,128]{2,1,0:T(8,128)(2,1)S(1)}, u32[]{:S(2)}, u32[]{:S(2)}) collective-permute-start(bf16[2,48,128]{2,1,0:T(8,128)(2,1)S(1)} %get-tuple-element.15), channel_id=1, source_target_pairs={{1,2},{2,1},{3,4},{4,3},{5,6},{6,5},{7,8},{8,7},{9,10},{10,9},{11,... | collective-permute-start | bytes 73736 | tf_op jit(solution)/shard_map/ppermute | solution.py:486
  6.5 5.3 %collective-permute-start = (bf16[2,40,128]{2,1,0:T(8,128)(2,1)S(1)}, bf16[2,40,128]{2,1,0:T(8,128)(2,1)S(1)}, u32[]{:S(2)}, u32[]{:S(2)}) collective-permute-start(bf16[2,40,128]{2,1,0:T(8,128)(2,1)S(1)} %get-tuple-element.14), channel_id=1, source_target_pairs={{0,1},{1,0},{2,3},{3,2},{4,5},{5,4},{6,7},{7,6},{8,9},{9,8},{10,11... | collective-permute-start | bytes 61448 | tf_op jit(solution)/shard_map/ppermute | solution.py:485
  11.5 8.5 %copy-start.1 = (bf16[191,576]{1,0:T(8,128)(2,1)S(1)}, bf16[191,576]{1,0:T(8,128)(2,1)}, u32[]{:S(2)}) copy-start(bf16[191,576]{1,0:T(8,128)(2,1)} %inverse.1) | copy-start | bytes 660100
  11.5 9.3 %copy-start = (bf16[640,256]{1,0:T(8,128)(2,1)S(1)}, bf16[640,256]{1,0:T(8,128)(2,1)}, u32[]{:S(2)}) copy-start(bf16[640,256]{1,0:T(8,128)(2,1)} %constant.74.matrix) | copy-start | bytes 983044
  11.6 9.3 %copy-start.2 = (f32[2,448]{1,0:T(2,128)S(1)}, f32[2,448]{1,0:T(2,128)}, u32[]{:S(2)}) copy-start(f32[2,448]{1,0:T(2,128)} %constant.51.clone.names) | copy-start | bytes 10756
  11.6 9.3 %copy-start.7 = (s32[2,56]{1,0:T(2,128)S(1)}, s32[2,56]{1,0:T(2,128)}, u32[]{:S(2)}) copy-start(s32[2,56]{1,0:T(2,128)} %constant.50.clone.pairs) | copy-start | bytes 1348
  11.6 9.3 %copy-start.8 = (s32[1,16,1]{1,2,0:T(1,128)S(1)}, s32[1,16,1]{1,2,0:T(1,128)}, u32[]{:S(2)}) copy-start(s32[1,16,1]{1,2,0:T(1,128)} %param.21) | copy-start | bytes 196
  11.6 9.3 %copy-start.9 = (s32[1,16]{1,0:T(1,128)S(1)}, s32[1,16]{1,0:T(1,128)}, u32[]{:S(2)}) copy-start(s32[1,16]{1,0:T(1,128)} %cells.1) | copy-start | bytes 196
  14.7 12.5 %collective-permute-start.3 = (bf16[256,640]{1,0:T(8,128)(2,1)S(1)}, bf16[256,640]{1,0:T(8,128)(2,1)S(1)}, u32[]{:S(2)}, u32[]{:S(2)}) collective-permute-start(bf16[256,640]{1,0:T(8,128)(2,1)S(1)} %get-tuple-element.17.edge0), channel_id=1, source_target_pairs={{32,0},{64,32},{96,64},{128,96},{160,128},{192,160},{224,192},{256... | collective-permute-start | bytes 983048 | tf_op jit(solution)/shard_map/ppermute | solution.py:506
  16.0 12.9 %collective-permute-start.2 = (bf16[256,640]{1,0:T(8,128)(2,1)S(1)}, bf16[256,640]{1,0:T(8,128)(2,1)S(1)}, u32[]{:S(2)}, u32[]{:S(2)}) collective-permute-start(bf16[256,640]{1,0:T(8,128)(2,1)S(1)} %get-tuple-element.16.edge1), channel_id=1, source_target_pairs={{0,32},{32,64},{64,96},{96,128},{128,160},{160,192},{192,224},{224... | collective-permute-start | bytes 983048 | tf_op jit(solution)/shard_map/ppermute | solution.py:507
  20.8 6.5 %copy-start.3 = (s32[2,16]{1,0:T(2,128)S(1)}, s32[2,16]{1,0:T(2,128)}, u32[]{:S(2)}) copy-start(s32[2,16]{1,0:T(2,128)} %constant.52.clone.pairs) | copy-start | bytes 388
  20.8 6.5 %copy-start.4 = (f32[2,128]{1,0:T(2,128)S(1)}, f32[2,128]{1,0:T(2,128)}, u32[]{:S(2)}) copy-start(f32[2,128]{1,0:T(2,128)} %constant.53.clone.names) | copy-start | bytes 3076
  27.2 1.7 %copy-start.5 = (s32[2,8]{1,0:T(2,128)S(1)}, s32[2,8]{1,0:T(2,128)}, u32[]{:S(2)}) copy-start(s32[2,8]{1,0:T(2,128)} %constant.54.clone.pairs) | copy-start | bytes 196
  27.3 1.7 %copy-start.6 = (f32[2,64]{1,0:T(2,128)S(1)}, f32[2,64]{1,0:T(2,128)}, u32[]{:S(2)}) copy-start(f32[2,64]{1,0:T(2,128)} %constant.55.clone.names) | copy-start | bytes 1540

commit v11 on v10

--- a/solution.py
+++ b/solution.py
@@ -154,7 +154,9 @@
 def edge_kernel(table, own, near, far, lines, head, tail, lhs, weights, zs):
     local = column(partner_row(table, lines), 16, 36 - EXTRA)
     for out in (head, tail):
-        out[240:256, :] = jnp.broadcast_to(local, (16, out.shape[1])).astype(BF16)
+        out[240:248, 0:LANES] = jnp.broadcast_to(local[0:8], (8, LANES)).astype(BF16)
+        rest = (8, out.shape[1] - LANES)
+        out[240:248, LANES:] = jnp.broadcast_to(local[8:9], rest).astype(BF16)
 
     def one(i, _):
         dates = (i, i + 9)
@@ -357,7 +359,10 @@
 
 def before_kernel(pairs, got, ys, power, phase, matrix, names, out, rs, ss, pm, pw):
     boundary_phases(pairs, len(BEFORE), False, got, ys, power, matrix, rs, ss, pm, pw)
-    told = jnp.max(got[240:256, 0:LANES].astype(F32), axis=1, keepdims=True)
+    told = jnp.concatenate(
+        [got[240:248, 0:LANES].astype(F32), got[240:248, LANES : 2 * LANES].astype(F32)], axis=0
+    )
+    told = jnp.max(told, axis=1, keepdims=True)
     spread = (iota((PAIR_ROWS, 16), 0) - 36 == iota((PAIR_ROWS, 16), 1)).astype(BF16)
     moved = jnp.dot(
         spread, jnp.broadcast_to(told, (16, LANES)).astype(BF16), preferred_element_type=F32
@@ -500,7 +505,7 @@
         edge_kernel,
         (mine,),
         (own, near, far, table),
-        [((256, width), BF16)] * 2,
+        [((248, width), BF16)] * 2,
         scratch,
     )
     later = lax.ppermute(edge0, "date", [(i + 1, i) for i in range(groups - 1)])

time: 78.4 us -> 78.4 us (level)
  no operation moved by 1% of the time
where the time goes in v11:
time: 78.4 us; the launch traced here: 78.2 us
  blocking collectives  45.9 us (59%)
  Pallas kernels  16.3 us (21%)
  starting transfers between devices  14.7 us (19%)
    all_to_all x1, blocking collectives, local(): parts = lax.all_to_all(routed, 'col', 0, 0, tiled=True)  31.4 us
    pallas_call x7, Pallas kernels, call(): pl.pallas_call(kernel, in_specs=[SMEM] * len(smem) + [VMEM] * len(vmem),...  14.8 us
    all_to_all x1, blocking collectives, local(): phases = lax.all_to_all(sent, 'date', 0, 0, tiled=True)  14.5 us
    ppermute x1, starting transfers between devices, local(): far = lax.ppermute(tile1, 'col', swaps(strips, 1))  4.94 us
    ppermute x1, starting transfers between devices, local(): near = lax.ppermute(tile0, 'col', swaps(strips, 0))  4.5 us
    ppermute x1, starting transfers between devices, local(): lax.ppermute(edge1, 'date', [(i, i + 1) for i in range(groups - 1)])  4.01 us
  transfers between devices with their start and end apart: 4, of which 1 were waited for; matrix products, arithmetic and copies ran while one was open for 1% of the time, Pallas kernels for 11%

profile of v11, /device:TPU:1, one launch (start us, length us, event | category | flops | bytes accessed | tf_op | source)
XLA Modules:
  0.0 78.2 jit_solution(7211668647317674955)
XLA Ops:
  0.0 1.5 %shard_map.145 = (bf16[2,40,128]{2,1,0:T(8,128)(2,1)S(1)}, bf16[2,48,128]{2,1,0:T(8,128)(2,1)S(1)}) custom-call(s32[1]{0:T(128)} %bitcast.11.odd, bf16[2,12,40,640]{3,2,1,0:T(8,128)(2,1)} %own.1), custom_call_target="tpu_custom_call" | custom-call | tf_op jit(solution)/shard_map/pallas_call | solution.py:478
  1.6 4.9 %collective-permute-start.1 = (bf16[2,48,128]{2,1,0:T(8,128)(2,1)S(1)}, bf16[2,48,128]{2,1,0:T(8,128)(2,1)S(1)}, u32[]{:S(2)}, u32[]{:S(2)}) collective-permute-start(bf16[2,48,128]{2,1,0:T(8,128)(2,1)S(1)} %get-tuple-element.15), channel_id=1, source_target_pairs={{1,2},{2,1},{3,4},{4,3},{5,6},{6,5},{7,8},{8,7},{9,10},{10,9},{11,... | collective-permute-start | bytes 73736 | tf_op jit(solution)/shard_map/ppermute | solution.py:491
  6.5 4.5 %collective-permute-start = (bf16[2,40,128]{2,1,0:T(8,128)(2,1)S(1)}, bf16[2,40,128]{2,1,0:T(8,128)(2,1)S(1)}, u32[]{:S(2)}, u32[]{:S(2)}) collective-permute-start(bf16[2,40,128]{2,1,0:T(8,128)(2,1)S(1)} %get-tuple-element.14), channel_id=1, source_target_pairs={{0,1},{1,0},{2,3},{3,2},{4,5},{5,4},{6,7},{7,6},{8,9},{9,8},{10,11... | collective-permute-start | bytes 61448 | tf_op jit(solution)/shard_map/ppermute | solution.py:490
  11.1 0.1 add_convert_fusion.1
  11.2 0.1 pad.36
  11.3 0.1 fusion.lines
  11.3 0.1 constant_dynamic-slice_fusion.table
  11.4 0.1 reduce_precision.3.own
  11.5 0.0 copy-start
  11.6 0.0 copy-start.7
  11.6 0.3 collective-permute-done.near
  11.9 2.9 %shard_map.146 = (bf16[248,640]{1,0:T(8,128)(2,1)S(1)}, bf16[248,640]{1,0:T(8,128)(2,1)S(1)}) custom-call(f32[24,12]{1,0:T(8,128)S(1)} %constant_dynamic-slice_fusion.table, bf16[2,12,40,640]{3,2,1,0:T(8,128)(2,1)S(1)} %reduce_precision.3.own, bf16[2,40,128]{2,1,0:T(8,128)(2,1)S(1)} %collective-permute-done.near, ...), custom_call_target="tpu_custom_call" | custom-call | tf_op jit(solution)/shard_map/pallas_call | solution.py:430
  14.7 1.3 %collective-permute-start.3 = (bf16[248,640]{1,0:T(8,128)(2,1)S(1)}, bf16[248,640]{1,0:T(8,128)(2,1)S(1)}, u32[]{:S(2)}, u32[]{:S(2)}) collective-permute-start(bf16[248,640]{1,0:T(8,128)(2,1)S(1)} %get-tuple-element.17.edge0), channel_id=1, source_target_pairs={{32,0},{64,32},{96,64},{128,96},{160,128},{192,160},{224,192},{256... | collective-permute-start | bytes 952328 | tf_op jit(solution)/shard_map/ppermute | solution.py:511
  16.0 4.0 %collective-permute-start.2 = (bf16[248,640]{1,0:T(8,128)(2,1)S(1)}, bf16[248,640]{1,0:T(8,128)(2,1)S(1)}, u32[]{:S(2)}, u32[]{:S(2)}) collective-permute-start(bf16[248,640]{1,0:T(8,128)(2,1)S(1)} %get-tuple-element.16.edge1), channel_id=1, source_target_pairs={{0,32},{32,64},{64,96},{96,128},{128,160},{160,192},{192,224},{224... | collective-permute-start | bytes 952328 | tf_op jit(solution)/shard_map/ppermute | solution.py:512
  20.0 0.7 shard_map.148.weight
  20.8 0.0 copy-start.5
  20.8 0.1 add_convert_fusion.facts.table
  20.9 6.3 %shard_map.147 = (f32[48,256]{1,0:T(8,128)S(1)}, f32[96,256]{1,0:T(8,128)S(1)}, f32[12,2,40,640]{3,2,1,0:T(8,128)S(1)}) custom-call(f32[24,12]{1,0:T(8,128)S(1)} %constant_dynamic-slice_fusion.table, s32[2,56]{1,0:T(2,128)S(1)} %copy-done.7, bf16[2,12,40,640]{3,2,1,0:T(8,128)(2,1)S(1)} %reduce_precision.3.own, ...), custom_call_target="tpu_custom_call" | custom-call | tf_op jit(solution)/shard_map/pallas_call | solution.py:430
  27.3 1.7 %shard_map.149.phase = f32[48,256]{1,0:T(8,128)S(1)} custom-call(f32[1,4]{1,0:T(1,128)S(1)} %add_convert_fusion.facts.table, s32[2,16]{1,0:T(2,128)S(1)} %copy-done.5, bf16[248,640]{1,0:T(8,128)(2,1)S(1)} %collective-permute-done.3.got, f32[12,2,40,640]{3,2,1,0:T(8,128)S(1)} %get-tuple-element.18.ys, f32[96,256]{1,0:T(8,128)S(1)} %get-tuple-element.19.power, ...), custom_call_target="tpu_custom_call" | custom-call | tf_op jit(solution)/shard_map/pallas_call | solution.py:430
  29.0 1.3 %shard_map.150 = bf16[16,48,256]{2,1,0:T(8,128)(2,1)S(1)} custom-call(s32[2,8]{1,0:T(2,128)S(1)} %copy-done.3, bf16[248,640]{1,0:T(8,128)(2,1)S(1)} %collective-permute-done.2.got, f32[12,2,40,640]{3,2,1,0:T(8,128)S(1)} %get-tuple-element.18.ys, f32[96,256]{1,0:T(8,128)S(1)} %get-tuple-element.19.power, f32[48,256]{1,0:T(8,128)S(1)} %shard_map.149.phase, ...), custom_call_target="tpu_custom_call" | custom-call | tf_op jit(solution)/shard_map/pallas_call | solution.py:430
  30.3 14.5 %all_to_all.10.got = bf16[16,48,256]{2,1,0:T(8,128)(2,1)S(1)} all-to-all(bf16[16,48,256]{2,1,0:T(8,128)(2,1)S(1)} %shard_map.150), channel_id=1, replica_groups=mesh['date'=16,'col'=32] {'date'}, dimensions={0} | all-to-all | bytes 786432 | tf_op jit(solution)/shard_map/all_to_all | solution.py:568
  44.8 1.2 %shard_map.151 = bf16[32,4,384]{2,1,0:T(4,128)(2,1)S(1)} custom-call(f32[1,4]{1,0:T(1,128)S(1)} %add_convert_fusion.facts.table, bf16[16,48,256]{2,1,0:T(8,128)(2,1)S(1)} %all_to_all.10.got, bf16[192,768]{1,0:T(8,128)(2,1)S(1)} %shard_map.148.weight), custom_call_target="tpu_custom_call" | custom-call | tf_op jit(solution)/shard_map/pallas_call | solution.py:430
  45.9 31.4 %all_to_all.11.got = bf16[32,4,384]{2,1,0:T(4,128)(2,1)S(1)} all-to-all(bf16[32,4,384]{2,1,0:T(4,128)(2,1)S(1)} %shard_map.151), channel_id=1, replica_groups=mesh['date'=16,'col'=32] {'col'}, dimensions={0} | all-to-all | bytes 196608 | tf_op jit(solution)/shard_map/all_to_all | solution.py:576
  77.4 0.8 %shard_map.152 = f32[8,192]{1,0:T(8,128)} custom-call(bf16[32,4,384]{2,1,0:T(4,128)(2,1)S(1)} %all_to_all.11.got, f32[24,192]{1,0:T(8,128)S(1)} %fusion.lines), custom_call_target="tpu_custom_call" | custom-call | tf_op jit(solution)/shard_map/pallas_call | solution.py:430
  (32 shorter events, 0.1 us)
Async XLA Ops:
  0.0 11.4 %copy-start.10 = (bf16[2,12,40,640]{3,2,1,0:T(8,128)(2,1)S(1)}, bf16[2,12,40,640]{3,2,1,0:T(8,128)(2,1)}, u32[]{:S(2)}) copy-start(bf16[2,12,40,640]{3,2,1,0:T(8,128)(2,1)} %own.1) | copy-start | bytes 3686404
  0.0 11.0 %copy-start.12 = (s32[192,2]{0,1:T(2,128)S(1)}, s32[192,2]{0,1:T(2,128)}, u32[]{:S(2)}) copy-start(s32[192,2]{0,1:T(2,128)} %param.16) | copy-start | bytes 4612
  0.0 11.1 %copy-start.14 = (s32[36]{0:T(128)S(1)}, s32[36]{0:T(128)}, u32[]{:S(2)}) copy-start(s32[36]{0:T(128)} %param.18) | copy-start | bytes 436
  0.0 11.2 %copy-start.11 = (f32[192,2,8]{0,2,1:T(8,128)S(1)}, f32[192,2,8]{0,2,1:T(8,128)}, u32[]{:S(2)}) copy-start(f32[192,2,8]{0,2,1:T(8,128)} %param.17) | copy-start | bytes 36868
  0.0 11.2 %copy-start.13 = (f32[191]{0:T(256)S(1)}, f32[191]{0:T(256)}, u32[]{:S(2)}) copy-start(f32[191]{0:T(256)} %param.20) | copy-start | bytes 2296
  1.6 10.3 %collective-permute-start.1 = (bf16[2,48,128]{2,1,0:T(8,128)(2,1)S(1)}, bf16[2,48,128]{2,1,0:T(8,128)(2,1)S(1)}, u32[]{:S(2)}, u32[]{:S(2)}) collective-permute-start(bf16[2,48,128]{2,1,0:T(8,128)(2,1)S(1)} %get-tuple-element.15), channel_id=1, source_target_pairs={{1,2},{2,1},{3,4},{4,3},{5,6},{6,5},{7,8},{8,7},{9,10},{10,9},{11,... | collective-permute-start | bytes 73736 | tf_op jit(solution)/shard_map/ppermute | solution.py:491
  6.5 5.3 %collective-permute-start = (bf16[2,40,128]{2,1,0:T(8,128)(2,1)S(1)}, bf16[2,40,128]{2,1,0:T(8,128)(2,1)S(1)}, u32[]{:S(2)}, u32[]{:S(2)}) collective-permute-start(bf16[2,40,128]{2,1,0:T(8,128)(2,1)S(1)} %get-tuple-element.14), channel_id=1, source_target_pairs={{0,1},{1,0},{2,3},{3,2},{4,5},{5,4},{6,7},{7,6},{8,9},{9,8},{10,11... | collective-permute-start | bytes 61448 | tf_op jit(solution)/shard_map/ppermute | solution.py:490
  11.5 8.5 %copy-start.1 = (bf16[191,576]{1,0:T(8,128)(2,1)S(1)}, bf16[191,576]{1,0:T(8,128)(2,1)}, u32[]{:S(2)}) copy-start(bf16[191,576]{1,0:T(8,128)(2,1)} %inverse.1) | copy-start | bytes 660100
  11.5 9.3 %copy-start = (bf16[640,256]{1,0:T(8,128)(2,1)S(1)}, bf16[640,256]{1,0:T(8,128)(2,1)}, u32[]{:S(2)}) copy-start(bf16[640,256]{1,0:T(8,128)(2,1)} %constant.74.matrix) | copy-start | bytes 983044
  11.6 9.3 %copy-start.2 = (f32[2,448]{1,0:T(2,128)S(1)}, f32[2,448]{1,0:T(2,128)}, u32[]{:S(2)}) copy-start(f32[2,448]{1,0:T(2,128)} %constant.51.clone.names) | copy-start | bytes 10756
  11.6 9.3 %copy-start.7 = (s32[2,56]{1,0:T(2,128)S(1)}, s32[2,56]{1,0:T(2,128)}, u32[]{:S(2)}) copy-start(s32[2,56]{1,0:T(2,128)} %constant.50.clone.pairs) | copy-start | bytes 1348
  11.6 9.3 %copy-start.8 = (s32[1,16,1]{1,2,0:T(1,128)S(1)}, s32[1,16,1]{1,2,0:T(1,128)}, u32[]{:S(2)}) copy-start(s32[1,16,1]{1,2,0:T(1,128)} %param.21) | copy-start | bytes 196
  11.6 9.3 %copy-start.9 = (s32[1,16]{1,0:T(1,128)S(1)}, s32[1,16]{1,0:T(1,128)}, u32[]{:S(2)}) copy-start(s32[1,16]{1,0:T(1,128)} %cells.1) | copy-start | bytes 196
  14.7 12.5 %collective-permute-start.3 = (bf16[248,640]{1,0:T(8,128)(2,1)S(1)}, bf16[248,640]{1,0:T(8,128)(2,1)S(1)}, u32[]{:S(2)}, u32[]{:S(2)}) collective-permute-start(bf16[248,640]{1,0:T(8,128)(2,1)S(1)} %get-tuple-element.17.edge0), channel_id=1, source_target_pairs={{32,0},{64,32},{96,64},{128,96},{160,128},{192,160},{224,192},{256... | collective-permute-start | bytes 952328 | tf_op jit(solution)/shard_map/ppermute | solution.py:511
  16.0 13.0 %collective-permute-start.2 = (bf16[248,640]{1,0:T(8,128)(2,1)S(1)}, bf16[248,640]{1,0:T(8,128)(2,1)S(1)}, u32[]{:S(2)}, u32[]{:S(2)}) collective-permute-start(bf16[248,640]{1,0:T(8,128)(2,1)S(1)} %get-tuple-element.16.edge1), channel_id=1, source_target_pairs={{0,32},{32,64},{64,96},{96,128},{128,160},{160,192},{192,224},{224... | collective-permute-start | bytes 952328 | tf_op jit(solution)/shard_map/ppermute | solution.py:512
  20.8 6.5 %copy-start.5 = (s32[2,16]{1,0:T(2,128)S(1)}, s32[2,16]{1,0:T(2,128)}, u32[]{:S(2)}) copy-start(s32[2,16]{1,0:T(2,128)} %constant.52.clone.pairs) | copy-start | bytes 388
  20.8 6.5 %copy-start.6 = (f32[2,128]{1,0:T(2,128)S(1)}, f32[2,128]{1,0:T(2,128)}, u32[]{:S(2)}) copy-start(f32[2,128]{1,0:T(2,128)} %constant.53.clone.names) | copy-start | bytes 3076
  27.2 1.7 %copy-start.3 = (s32[2,8]{1,0:T(2,128)S(1)}, s32[2,8]{1,0:T(2,128)}, u32[]{:S(2)}) copy-start(s32[2,8]{1,0:T(2,128)} %constant.54.clone.pairs) | copy-start | bytes 196
  27.3 1.7 %copy-start.4 = (f32[2,64]{1,0:T(2,128)S(1)}, f32[2,64]{1,0:T(2,128)}, u32[]{:S(2)}) copy-start(f32[2,64]{1,0:T(2,128)} %constant.55.clone.names) | copy-start | bytes 1540

commit v12 on v10

--- a/solution.py
+++ b/solution.py
@@ -238,7 +238,7 @@
 def inner_kernel(
     table, pairs, own, near, far, edge0, edge1, lines, matrix, names, owners, cells,
     phase_out, power_out, ys,
-    lhs, weights, zs, ps, ss, pm,
+    lhs, weights, zs, ss, pm,
 ):
     width = own.shape[-1]
 
@@ -254,8 +254,10 @@
     unpack_dates(edge0, ys, 0)
     unpack_dates(edge1, ys, 9)
 
+    powers = 8 * len(INNER)
+
     def one_power(d, _):
-        ps[pl.ds(pl.multiple_of(d * 8, 8), 8), :] = power_sum(reader(d))
+        ss[pl.ds(pl.multiple_of(powers + d * 8, 8), 8), :] = power_sum(reader(d))
         return 0
 
     def reader(d):
@@ -268,9 +270,8 @@
         ss[pl.ds(at, 8), :] = cross_sum(reader(pairs[0, c]), reader(pairs[1, c]))
         return 0
 
-    total = ss.shape[0] // 8
-    lax.fori_loop(0, total, one_pair, 0)
-    power_out[...] = window_sum(ps[...], matrix)
+    lax.fori_loop(0, len(INNER), one_pair, 0)
+    ss[powers + 96 :, :] = jnp.zeros_like(ss[powers + 96 :, :])
     block = ss.shape[0] // 2
 
     def one_block(n, _):
@@ -279,7 +280,9 @@
         return 0
 
     lax.fori_loop(0, 2, one_block, 0)
-    phases_of(pairs, total, pm, power_out)
+    power_out[...] = pm[powers : powers + 96, :]
+    total = names.shape[1]
+    phases_of(pairs, total // 8, pm, power_out)
     local = column(partner_row(table, lines), PAIR_ROWS, 0)
     row = iota((PAIR_ROWS, 1), 0)
     have_a = jnp.where(row < 36, row // PER_DATE, -9).astype(F32)
@@ -290,7 +293,7 @@
     codes = jnp.concatenate([owners[...], cells[...]], axis=0).astype(F32).astype(BF16)
     placed = jnp.dot(codes, spread, preferred_element_type=F32)
     lines = iota((PAIR_ROWS, 256), 0)
-    phases = jnp.dot(take, pm[...].astype(BF16), preferred_element_type=F32)
+    phases = jnp.dot(take, pm[:total, :].astype(BF16), preferred_element_type=F32)
     phases = jnp.where(lines == 46, placed[0:1, :], phases)
     phase_out[...] = jnp.where(lines == 47, placed[1:2, :], phases)
 
@@ -522,9 +525,8 @@
         ],
         scratch
         + [
-            pltpu.VMEM((96, width), F32),
-            pltpu.VMEM((inner_rows, width), F32),
-            pltpu.VMEM((inner_rows, 256), F32),
+            pltpu.VMEM((8 * len(INNER) + 104, width), F32),
+            pltpu.VMEM((8 * len(INNER) + 104, 256), F32),
         ],
     )
     def boundary(kernel, smem, vmem, pairs, table_pairs, out):

time: 78.4 us -> 78.1 us (level)
  no operation moved by 1% of the time
where the time goes in v12:
time: 78.1 us; the launch traced here: 77.8 us
  blocking collectives  45.9 us (59%)
  Pallas kernels  16 us (20%)
  starting transfers between devices  14.7 us (19%)
    all_to_all x1, blocking collectives, local(): parts = lax.all_to_all(routed, 'col', 0, 0, tiled=True)  31.4 us
    pallas_call x7, Pallas kernels, call(): pl.pallas_call(kernel, in_specs=[SMEM] * len(smem) + [VMEM] * len(vmem),...  14.5 us
    all_to_all x1, blocking collectives, local(): phases = lax.all_to_all(sent, 'date', 0, 0, tiled=True)  14.5 us
    ppermute x1, starting transfers between devices, local(): far = lax.ppermute(tile1, 'col', swaps(strips, 1))  4.94 us
    ppermute x1, starting transfers between devices, local(): near = lax.ppermute(tile0, 'col', swaps(strips, 0))  4.5 us
    ppermute x1, starting transfers between devices, local(): lax.ppermute(edge1, 'date', [(i, i + 1) for i in range(groups - 1)])  4.01 us
  transfers between devices with their start and end apart: 4, of which 1 were waited for; matrix products, arithmetic and copies ran while one was open for 1% of the time, Pallas kernels for 11%

profile of v12, /device:TPU:1, one launch (start us, length us, event | category | flops | bytes accessed | tf_op | source)
XLA Modules:
  0.0 77.8 jit_solution(5060194688016269137)
XLA Ops:
  0.0 1.5 %shard_map.145 = (bf16[2,40,128]{2,1,0:T(8,128)(2,1)S(1)}, bf16[2,48,128]{2,1,0:T(8,128)(2,1)S(1)}) custom-call(s32[1]{0:T(128)} %bitcast.11.odd, bf16[2,12,40,640]{3,2,1,0:T(8,128)(2,1)} %own.1), custom_call_target="tpu_custom_call" | custom-call | tf_op jit(solution)/shard_map/pallas_call | solution.py:476
  1.6 4.9 %collective-permute-start.1 = (bf16[2,48,128]{2,1,0:T(8,128)(2,1)S(1)}, bf16[2,48,128]{2,1,0:T(8,128)(2,1)S(1)}, u32[]{:S(2)}, u32[]{:S(2)}) collective-permute-start(bf16[2,48,128]{2,1,0:T(8,128)(2,1)S(1)} %get-tuple-element.15), channel_id=1, source_target_pairs={{1,2},{2,1},{3,4},{4,3},{5,6},{6,5},{7,8},{8,7},{9,10},{10,9},{11,... | collective-permute-start | bytes 73736 | tf_op jit(solution)/shard_map/ppermute | solution.py:489
  6.5 4.5 %collective-permute-start = (bf16[2,40,128]{2,1,0:T(8,128)(2,1)S(1)}, bf16[2,40,128]{2,1,0:T(8,128)(2,1)S(1)}, u32[]{:S(2)}, u32[]{:S(2)}) collective-permute-start(bf16[2,40,128]{2,1,0:T(8,128)(2,1)S(1)} %get-tuple-element.14), channel_id=1, source_target_pairs={{0,1},{1,0},{2,3},{3,2},{4,5},{5,4},{6,7},{7,6},{8,9},{9,8},{10,11... | collective-permute-start | bytes 61448 | tf_op jit(solution)/shard_map/ppermute | solution.py:488
  11.1 0.1 add_convert_fusion.1
  11.2 0.1 pad.36
  11.3 0.1 fusion.lines
  11.3 0.1 constant_dynamic-slice_fusion.table
  11.4 0.1 reduce_precision.3.own
  11.5 0.0 copy-start
  11.6 0.0 copy-start.7
  11.6 0.3 collective-permute-done.near
  11.9 2.9 %shard_map.146 = (bf16[256,640]{1,0:T(8,128)(2,1)S(1)}, bf16[256,640]{1,0:T(8,128)(2,1)S(1)}) custom-call(f32[24,12]{1,0:T(8,128)S(1)} %constant_dynamic-slice_fusion.table, bf16[2,12,40,640]{3,2,1,0:T(8,128)(2,1)S(1)} %reduce_precision.3.own, bf16[2,40,128]{2,1,0:T(8,128)(2,1)S(1)} %collective-permute-done.near, ...), custom_call_target="tpu_custom_call" | custom-call | tf_op jit(solution)/shard_map/pallas_call | solution.py:428
  14.7 1.3 %collective-permute-start.3 = (bf16[256,640]{1,0:T(8,128)(2,1)S(1)}, bf16[256,640]{1,0:T(8,128)(2,1)S(1)}, u32[]{:S(2)}, u32[]{:S(2)}) collective-permute-start(bf16[256,640]{1,0:T(8,128)(2,1)S(1)} %get-tuple-element.17.edge0), channel_id=1, source_target_pairs={{32,0},{64,32},{96,64},{128,96},{160,128},{192,160},{224,192},{256... | collective-permute-start | bytes 983048 | tf_op jit(solution)/shard_map/ppermute | solution.py:509
  16.0 4.0 %collective-permute-start.2 = (bf16[256,640]{1,0:T(8,128)(2,1)S(1)}, bf16[256,640]{1,0:T(8,128)(2,1)S(1)}, u32[]{:S(2)}, u32[]{:S(2)}) collective-permute-start(bf16[256,640]{1,0:T(8,128)(2,1)S(1)} %get-tuple-element.16.edge1), channel_id=1, source_target_pairs={{0,32},{32,64},{64,96},{96,128},{128,160},{160,192},{192,224},{224... | collective-permute-start | bytes 983048 | tf_op jit(solution)/shard_map/ppermute | solution.py:510
  20.1 0.7 shard_map.148.weight
  20.8 0.0 copy-start.3
  20.8 0.1 add_convert_fusion.facts.table
  20.9 6.0 %shard_map.147 = (f32[48,256]{1,0:T(8,128)S(1)}, f32[96,256]{1,0:T(8,128)S(1)}, f32[12,2,40,640]{3,2,1,0:T(8,128)S(1)}) custom-call(f32[24,12]{1,0:T(8,128)S(1)} %constant_dynamic-slice_fusion.table, s32[2,56]{1,0:T(2,128)S(1)} %copy-done.7, bf16[2,12,40,640]{3,2,1,0:T(8,128)(2,1)S(1)} %reduce_precision.3.own, ...), custom_call_target="tpu_custom_call" | custom-call | tf_op jit(solution)/shard_map/pallas_call | solution.py:428
  27.0 1.7 %shard_map.149.phase = f32[48,256]{1,0:T(8,128)S(1)} custom-call(f32[1,4]{1,0:T(1,128)S(1)} %add_convert_fusion.facts.table, s32[2,16]{1,0:T(2,128)S(1)} %copy-done.3, bf16[256,640]{1,0:T(8,128)(2,1)S(1)} %collective-permute-done.3.got, f32[12,2,40,640]{3,2,1,0:T(8,128)S(1)} %get-tuple-element.18.ys, f32[96,256]{1,0:T(8,128)S(1)} %get-tuple-element.19.power, ...), custom_call_target="tpu_custom_call" | custom-call | tf_op jit(solution)/shard_map/pallas_call | solution.py:428
  28.7 1.3 %shard_map.150 = bf16[16,48,256]{2,1,0:T(8,128)(2,1)S(1)} custom-call(s32[2,8]{1,0:T(2,128)S(1)} %copy-done.5, bf16[256,640]{1,0:T(8,128)(2,1)S(1)} %collective-permute-done.2.got, f32[12,2,40,640]{3,2,1,0:T(8,128)S(1)} %get-tuple-element.18.ys, f32[96,256]{1,0:T(8,128)S(1)} %get-tuple-element.19.power, f32[48,256]{1,0:T(8,128)S(1)} %shard_map.149.phase, ...), custom_call_target="tpu_custom_call" | custom-call | tf_op jit(solution)/shard_map/pallas_call | solution.py:428
  30.0 14.5 %all_to_all.10.got = bf16[16,48,256]{2,1,0:T(8,128)(2,1)S(1)} all-to-all(bf16[16,48,256]{2,1,0:T(8,128)(2,1)S(1)} %shard_map.150), channel_id=1, replica_groups=mesh['date'=16,'col'=32] {'date'}, dimensions={0} | all-to-all | bytes 786432 | tf_op jit(solution)/shard_map/all_to_all | solution.py:565
  44.5 1.2 %shard_map.151 = bf16[32,4,384]{2,1,0:T(4,128)(2,1)S(1)} custom-call(f32[1,4]{1,0:T(1,128)S(1)} %add_convert_fusion.facts.table, bf16[16,48,256]{2,1,0:T(8,128)(2,1)S(1)} %all_to_all.10.got, bf16[192,768]{1,0:T(8,128)(2,1)S(1)} %shard_map.148.weight), custom_call_target="tpu_custom_call" | custom-call | tf_op jit(solution)/shard_map/pallas_call | solution.py:428
  45.6 31.4 %all_to_all.11.got = bf16[32,4,384]{2,1,0:T(4,128)(2,1)S(1)} all-to-all(bf16[32,4,384]{2,1,0:T(4,128)(2,1)S(1)} %shard_map.151), channel_id=1, replica_groups=mesh['date'=16,'col'=32] {'col'}, dimensions={0} | all-to-all | bytes 196608 | tf_op jit(solution)/shard_map/all_to_all | solution.py:573
  77.1 0.8 %shard_map.152 = f32[8,192]{1,0:T(8,128)} custom-call(bf16[32,4,384]{2,1,0:T(4,128)(2,1)S(1)} %all_to_all.11.got, f32[24,192]{1,0:T(8,128)S(1)} %fusion.lines), custom_call_target="tpu_custom_call" | custom-call | tf_op jit(solution)/shard_map/pallas_call | solution.py:428
  (32 shorter events, 0.1 us)
Async XLA Ops:
  0.0 11.4 %copy-start.10 = (bf16[2,12,40,640]{3,2,1,0:T(8,128)(2,1)S(1)}, bf16[2,12,40,640]{3,2,1,0:T(8,128)(2,1)}, u32[]{:S(2)}) copy-start(bf16[2,12,40,640]{3,2,1,0:T(8,128)(2,1)} %own.1) | copy-start | bytes 3686404
  0.0 11.0 %copy-start.12 = (s32[192,2]{0,1:T(2,128)S(1)}, s32[192,2]{0,1:T(2,128)}, u32[]{:S(2)}) copy-start(s32[192,2]{0,1:T(2,128)} %param.16) | copy-start | bytes 4612
  0.0 11.1 %copy-start.14 = (s32[36]{0:T(128)S(1)}, s32[36]{0:T(128)}, u32[]{:S(2)}) copy-start(s32[36]{0:T(128)} %param.18) | copy-start | bytes 436
  0.0 11.2 %copy-start.11 = (f32[192,2,8]{0,2,1:T(8,128)S(1)}, f32[192,2,8]{0,2,1:T(8,128)}, u32[]{:S(2)}) copy-start(f32[192,2,8]{0,2,1:T(8,128)} %param.17) | copy-start | bytes 36868
  0.0 11.2 %copy-start.13 = (f32[191]{0:T(256)S(1)}, f32[191]{0:T(256)}, u32[]{:S(2)}) copy-start(f32[191]{0:T(256)} %param.20) | copy-start | bytes 2296
  1.6 10.3 %collective-permute-start.1 = (bf16[2,48,128]{2,1,0:T(8,128)(2,1)S(1)}, bf16[2,48,128]{2,1,0:T(8,128)(2,1)S(1)}, u32[]{:S(2)}, u32[]{:S(2)}) collective-permute-start(bf16[2,48,128]{2,1,0:T(8,128)(2,1)S(1)} %get-tuple-element.15), channel_id=1, source_target_pairs={{1,2},{2,1},{3,4},{4,3},{5,6},{6,5},{7,8},{8,7},{9,10},{10,9},{11,... | collective-permute-start | bytes 73736 | tf_op jit(solution)/shard_map/ppermute | solution.py:489
  6.5 5.3 %collective-permute-start = (bf16[2,40,128]{2,1,0:T(8,128)(2,1)S(1)}, bf16[2,40,128]{2,1,0:T(8,128)(2,1)S(1)}, u32[]{:S(2)}, u32[]{:S(2)}) collective-permute-start(bf16[2,40,128]{2,1,0:T(8,128)(2,1)S(1)} %get-tuple-element.14), channel_id=1, source_target_pairs={{0,1},{1,0},{2,3},{3,2},{4,5},{5,4},{6,7},{7,6},{8,9},{9,8},{10,11... | collective-permute-start | bytes 61448 | tf_op jit(solution)/shard_map/ppermute | solution.py:488
  11.5 8.5 %copy-start.1 = (bf16[191,576]{1,0:T(8,128)(2,1)S(1)}, bf16[191,576]{1,0:T(8,128)(2,1)}, u32[]{:S(2)}) copy-start(bf16[191,576]{1,0:T(8,128)(2,1)} %inverse.1) | copy-start | bytes 660100
  11.5 9.3 %copy-start = (bf16[640,256]{1,0:T(8,128)(2,1)S(1)}, bf16[640,256]{1,0:T(8,128)(2,1)}, u32[]{:S(2)}) copy-start(bf16[640,256]{1,0:T(8,128)(2,1)} %constant.74.matrix) | copy-start | bytes 983044
  11.6 9.3 %copy-start.2 = (f32[2,448]{1,0:T(2,128)S(1)}, f32[2,448]{1,0:T(2,128)}, u32[]{:S(2)}) copy-start(f32[2,448]{1,0:T(2,128)} %constant.51.clone.names) | copy-start | bytes 10756
  11.6 9.3 %copy-start.7 = (s32[2,56]{1,0:T(2,128)S(1)}, s32[2,56]{1,0:T(2,128)}, u32[]{:S(2)}) copy-start(s32[2,56]{1,0:T(2,128)} %constant.50.clone.pairs) | copy-start | bytes 1348
  11.6 9.3 %copy-start.8 = (s32[1,16,1]{1,2,0:T(1,128)S(1)}, s32[1,16,1]{1,2,0:T(1,128)}, u32[]{:S(2)}) copy-start(s32[1,16,1]{1,2,0:T(1,128)} %param.21) | copy-start | bytes 196
  11.6 9.3 %copy-start.9 = (s32[1,16]{1,0:T(1,128)S(1)}, s32[1,16]{1,0:T(1,128)}, u32[]{:S(2)}) copy-start(s32[1,16]{1,0:T(1,128)} %cells.1) | copy-start | bytes 196
  14.7 12.2 %collective-permute-start.3 = (bf16[256,640]{1,0:T(8,128)(2,1)S(1)}, bf16[256,640]{1,0:T(8,128)(2,1)S(1)}, u32[]{:S(2)}, u32[]{:S(2)}) collective-permute-start(bf16[256,640]{1,0:T(8,128)(2,1)S(1)} %get-tuple-element.17.edge0), channel_id=1, source_target_pairs={{32,0},{64,32},{96,64},{128,96},{160,128},{192,160},{224,192},{256... | collective-permute-start | bytes 983048 | tf_op jit(solution)/shard_map/ppermute | solution.py:509
  16.0 12.6 %collective-permute-start.2 = (bf16[256,640]{1,0:T(8,128)(2,1)S(1)}, bf16[256,640]{1,0:T(8,128)(2,1)S(1)}, u32[]{:S(2)}, u32[]{:S(2)}) collective-permute-start(bf16[256,640]{1,0:T(8,128)(2,1)S(1)} %get-tuple-element.16.edge1), channel_id=1, source_target_pairs={{0,32},{32,64},{64,96},{96,128},{128,160},{160,192},{192,224},{224... | collective-permute-start | bytes 983048 | tf_op jit(solution)/shard_map/ppermute | solution.py:510
  20.8 6.1 %copy-start.3 = (s32[2,16]{1,0:T(2,128)S(1)}, s32[2,16]{1,0:T(2,128)}, u32[]{:S(2)}) copy-start(s32[2,16]{1,0:T(2,128)} %constant.52.clone.pairs) | copy-start | bytes 388
  20.8 6.1 %copy-start.4 = (f32[2,128]{1,0:T(2,128)S(1)}, f32[2,128]{1,0:T(2,128)}, u32[]{:S(2)}) copy-start(f32[2,128]{1,0:T(2,128)} %constant.53.clone.names) | copy-start | bytes 3076
  26.9 1.7 %copy-start.5 = (s32[2,8]{1,0:T(2,128)S(1)}, s32[2,8]{1,0:T(2,128)}, u32[]{:S(2)}) copy-start(s32[2,8]{1,0:T(2,128)} %constant.54.clone.pairs) | copy-start | bytes 196
  26.9 1.7 %copy-start.6 = (f32[2,64]{1,0:T(2,128)S(1)}, f32[2,64]{1,0:T(2,128)}, u32[]{:S(2)}) copy-start(f32[2,64]{1,0:T(2,128)} %constant.55.clone.names) | copy-start | bytes 1540

commit v13 on v12

--- a/solution.py
+++ b/solution.py
@@ -263,7 +263,7 @@
     def reader(d):
         return lambda part, k: ys[d, part, 8 * k : 8 * k + 8, :]
 
-    lax.fori_loop(0, 12, one_power, 0)
+    lax.fori_loop(0, 12, one_power, 0, unroll=2)
 
     def one_pair(c, _):
         at = pl.multiple_of(c * 8, 8)
@@ -308,7 +308,7 @@
         gather[pl.ds(at, 16), :] = (iota((16, gather.shape[1]), 0) + at == target).astype(BF16)
         return 0
 
-    lax.fori_loop(0, gather.shape[0] // 16, one_rows, 0)
+    lax.fori_loop(0, gather.shape[0] // 16, one_rows, 0, unroll=4)
     weight_out[0:191, :] = jnp.dot(
         inverse[...], gather[...], preferred_element_type=F32
     ).astype(BF16)

time: 78.1 us -> 78 us (level)
  no operation moved by 1% of the time
where the time goes in v13:
time: 78 us; the launch traced here: 77.7 us
  blocking collectives  45.9 us (59%)
  Pallas kernels  15.9 us (20%)
  starting transfers between devices  14.7 us (19%)
    all_to_all x1, blocking collectives, local(): parts = lax.all_to_all(routed, 'col', 0, 0, tiled=True)  31.4 us
    all_to_all x1, blocking collectives, local(): phases = lax.all_to_all(sent, 'date', 0, 0, tiled=True)  14.5 us
    pallas_call x7, Pallas kernels, call(): pl.pallas_call(kernel, in_specs=[SMEM] * len(smem) + [VMEM] * len(vmem),...  14.4 us
    ppermute x1, starting transfers between devices, local(): far = lax.ppermute(tile1, 'col', swaps(strips, 1))  4.94 us
    ppermute x1, starting transfers between devices, local(): near = lax.ppermute(tile0, 'col', swaps(strips, 0))  4.5 us
    ppermute x1, starting transfers between devices, local(): lax.ppermute(edge1, 'date', [(i, i + 1) for i in range(groups - 1)])  4.01 us
  transfers between devices with their start and end apart: 4, of which 1 were waited for; matrix products, arithmetic and copies ran while one was open for 1% of the time, Pallas kernels for 11%

profile of v13, /device:TPU:1, one launch (start us, length us, event | category | flops | bytes accessed | tf_op | source)
XLA Modules:
  0.0 77.7 jit_solution(5810676562905547151)
XLA Ops:
  0.0 1.5 %shard_map.145 = (bf16[2,40,128]{2,1,0:T(8,128)(2,1)S(1)}, bf16[2,48,128]{2,1,0:T(8,128)(2,1)S(1)}) custom-call(s32[1]{0:T(128)} %bitcast.11.odd, bf16[2,12,40,640]{3,2,1,0:T(8,128)(2,1)} %own.1), custom_call_target="tpu_custom_call" | custom-call | tf_op jit(solution)/shard_map/pallas_call | solution.py:476
  1.6 4.9 %collective-permute-start.1 = (bf16[2,48,128]{2,1,0:T(8,128)(2,1)S(1)}, bf16[2,48,128]{2,1,0:T(8,128)(2,1)S(1)}, u32[]{:S(2)}, u32[]{:S(2)}) collective-permute-start(bf16[2,48,128]{2,1,0:T(8,128)(2,1)S(1)} %get-tuple-element.15), channel_id=1, source_target_pairs={{1,2},{2,1},{3,4},{4,3},{5,6},{6,5},{7,8},{8,7},{9,10},{10,9},{11,... | collective-permute-start | bytes 73736 | tf_op jit(solution)/shard_map/ppermute | solution.py:489
  6.5 4.5 %collective-permute-start = (bf16[2,40,128]{2,1,0:T(8,128)(2,1)S(1)}, bf16[2,40,128]{2,1,0:T(8,128)(2,1)S(1)}, u32[]{:S(2)}, u32[]{:S(2)}) collective-permute-start(bf16[2,40,128]{2,1,0:T(8,128)(2,1)S(1)} %get-tuple-element.14), channel_id=1, source_target_pairs={{0,1},{1,0},{2,3},{3,2},{4,5},{5,4},{6,7},{7,6},{8,9},{9,8},{10,11... | collective-permute-start | bytes 61448 | tf_op jit(solution)/shard_map/ppermute | solution.py:488
  11.1 0.1 add_convert_fusion.1
  11.2 0.1 pad.36
  11.3 0.1 fusion.lines
  11.3 0.1 constant_dynamic-slice_fusion.table
  11.4 0.1 reduce_precision.3.own
  11.5 0.0 copy-start
  11.6 0.0 copy-start.2
  11.6 0.0 copy-start.7
  11.6 0.3 collective-permute-done.near
  11.9 2.9 %shard_map.146 = (bf16[256,640]{1,0:T(8,128)(2,1)S(1)}, bf16[256,640]{1,0:T(8,128)(2,1)S(1)}) custom-call(f32[24,12]{1,0:T(8,128)S(1)} %constant_dynamic-slice_fusion.table, bf16[2,12,40,640]{3,2,1,0:T(8,128)(2,1)S(1)} %reduce_precision.3.own, bf16[2,40,128]{2,1,0:T(8,128)(2,1)S(1)} %collective-permute-done.near, ...), custom_call_target="tpu_custom_call" | custom-call | tf_op jit(solution)/shard_map/pallas_call | solution.py:428
  14.7 1.3 %collective-permute-start.3 = (bf16[256,640]{1,0:T(8,128)(2,1)S(1)}, bf16[256,640]{1,0:T(8,128)(2,1)S(1)}, u32[]{:S(2)}, u32[]{:S(2)}) collective-permute-start(bf16[256,640]{1,0:T(8,128)(2,1)S(1)} %get-tuple-element.17.edge0), channel_id=1, source_target_pairs={{32,0},{64,32},{96,64},{128,96},{160,128},{192,160},{224,192},{256... | collective-permute-start | bytes 983048 | tf_op jit(solution)/shard_map/ppermute | solution.py:509
  16.0 4.0 %collective-permute-start.2 = (bf16[256,640]{1,0:T(8,128)(2,1)S(1)}, bf16[256,640]{1,0:T(8,128)(2,1)S(1)}, u32[]{:S(2)}, u32[]{:S(2)}) collective-permute-start(bf16[256,640]{1,0:T(8,128)(2,1)S(1)} %get-tuple-element.16.edge1), channel_id=1, source_target_pairs={{0,32},{32,64},{64,96},{96,128},{128,160},{160,192},{192,224},{224... | collective-permute-start | bytes 983048 | tf_op jit(solution)/shard_map/ppermute | solution.py:510
  20.1 0.6 shard_map.148.weight
  20.7 0.1 add_convert_fusion.facts.table
  20.8 5.9 %shard_map.147 = (f32[48,256]{1,0:T(8,128)S(1)}, f32[96,256]{1,0:T(8,128)S(1)}, f32[12,2,40,640]{3,2,1,0:T(8,128)S(1)}) custom-call(f32[24,12]{1,0:T(8,128)S(1)} %constant_dynamic-slice_fusion.table, s32[2,56]{1,0:T(2,128)S(1)} %copy-done.7, bf16[2,12,40,640]{3,2,1,0:T(8,128)(2,1)S(1)} %reduce_precision.3.own, ...), custom_call_target="tpu_custom_call" | custom-call | tf_op jit(solution)/shard_map/pallas_call | solution.py:428
  26.8 1.7 %shard_map.149.phase = f32[48,256]{1,0:T(8,128)S(1)} custom-call(f32[1,4]{1,0:T(1,128)S(1)} %add_convert_fusion.facts.table, s32[2,16]{1,0:T(2,128)S(1)} %copy-done.3, bf16[256,640]{1,0:T(8,128)(2,1)S(1)} %collective-permute-done.3.got, f32[12,2,40,640]{3,2,1,0:T(8,128)S(1)} %get-tuple-element.18.ys, f32[96,256]{1,0:T(8,128)S(1)} %get-tuple-element.19.power, ...), custom_call_target="tpu_custom_call" | custom-call | tf_op jit(solution)/shard_map/pallas_call | solution.py:428
  28.6 1.3 %shard_map.150 = bf16[16,48,256]{2,1,0:T(8,128)(2,1)S(1)} custom-call(s32[2,8]{1,0:T(2,128)S(1)} %copy-done.5, bf16[256,640]{1,0:T(8,128)(2,1)S(1)} %collective-permute-done.2.got, f32[12,2,40,640]{3,2,1,0:T(8,128)S(1)} %get-tuple-element.18.ys, f32[96,256]{1,0:T(8,128)S(1)} %get-tuple-element.19.power, f32[48,256]{1,0:T(8,128)S(1)} %shard_map.149.phase, ...), custom_call_target="tpu_custom_call" | custom-call | tf_op jit(solution)/shard_map/pallas_call | solution.py:428
  29.9 14.5 %all_to_all.10.got = bf16[16,48,256]{2,1,0:T(8,128)(2,1)S(1)} all-to-all(bf16[16,48,256]{2,1,0:T(8,128)(2,1)S(1)} %shard_map.150), channel_id=1, replica_groups=mesh['date'=16,'col'=32] {'date'}, dimensions={0} | all-to-all | bytes 786432 | tf_op jit(solution)/shard_map/all_to_all | solution.py:565
  44.3 1.2 %shard_map.151 = bf16[32,4,384]{2,1,0:T(4,128)(2,1)S(1)} custom-call(f32[1,4]{1,0:T(1,128)S(1)} %add_convert_fusion.facts.table, bf16[16,48,256]{2,1,0:T(8,128)(2,1)S(1)} %all_to_all.10.got, bf16[192,768]{1,0:T(8,128)(2,1)S(1)} %shard_map.148.weight), custom_call_target="tpu_custom_call" | custom-call | tf_op jit(solution)/shard_map/pallas_call | solution.py:428
  45.5 31.4 %all_to_all.11.got = bf16[32,4,384]{2,1,0:T(4,128)(2,1)S(1)} all-to-all(bf16[32,4,384]{2,1,0:T(4,128)(2,1)S(1)} %shard_map.151), channel_id=1, replica_groups=mesh['date'=16,'col'=32] {'col'}, dimensions={0} | all-to-all | bytes 196608 | tf_op jit(solution)/shard_map/all_to_all | solution.py:573
  76.9 0.8 %shard_map.152 = f32[8,192]{1,0:T(8,128)} custom-call(bf16[32,4,384]{2,1,0:T(4,128)(2,1)S(1)} %all_to_all.11.got, f32[24,192]{1,0:T(8,128)S(1)} %fusion.lines), custom_call_target="tpu_custom_call" | custom-call | tf_op jit(solution)/shard_map/pallas_call | solution.py:428
  (32 shorter events, 0.1 us)
Async XLA Ops:
  0.0 11.4 %copy-start.10 = (bf16[2,12,40,640]{3,2,1,0:T(8,128)(2,1)S(1)}, bf16[2,12,40,640]{3,2,1,0:T(8,128)(2,1)}, u32[]{:S(2)}) copy-start(bf16[2,12,40,640]{3,2,1,0:T(8,128)(2,1)} %own.1) | copy-start | bytes 3686404
  0.0 11.0 %copy-start.12 = (s32[192,2]{0,1:T(2,128)S(1)}, s32[192,2]{0,1:T(2,128)}, u32[]{:S(2)}) copy-start(s32[192,2]{0,1:T(2,128)} %param.16) | copy-start | bytes 4612
  0.0 11.1 %copy-start.14 = (s32[36]{0:T(128)S(1)}, s32[36]{0:T(128)}, u32[]{:S(2)}) copy-start(s32[36]{0:T(128)} %param.18) | copy-start | bytes 436
  0.0 11.2 %copy-start.11 = (f32[192,2,8]{0,2,1:T(8,128)S(1)}, f32[192,2,8]{0,2,1:T(8,128)}, u32[]{:S(2)}) copy-start(f32[192,2,8]{0,2,1:T(8,128)} %param.17) | copy-start | bytes 36868
  0.0 11.2 %copy-start.13 = (f32[191]{0:T(256)S(1)}, f32[191]{0:T(256)}, u32[]{:S(2)}) copy-start(f32[191]{0:T(256)} %param.20) | copy-start | bytes 2296
  1.6 10.3 %collective-permute-start.1 = (bf16[2,48,128]{2,1,0:T(8,128)(2,1)S(1)}, bf16[2,48,128]{2,1,0:T(8,128)(2,1)S(1)}, u32[]{:S(2)}, u32[]{:S(2)}) collective-permute-start(bf16[2,48,128]{2,1,0:T(8,128)(2,1)S(1)} %get-tuple-element.15), channel_id=1, source_target_pairs={{1,2},{2,1},{3,4},{4,3},{5,6},{6,5},{7,8},{8,7},{9,10},{10,9},{11,... | collective-permute-start | bytes 73736 | tf_op jit(solution)/shard_map/ppermute | solution.py:489
  6.5 5.3 %collective-permute-start = (bf16[2,40,128]{2,1,0:T(8,128)(2,1)S(1)}, bf16[2,40,128]{2,1,0:T(8,128)(2,1)S(1)}, u32[]{:S(2)}, u32[]{:S(2)}) collective-permute-start(bf16[2,40,128]{2,1,0:T(8,128)(2,1)S(1)} %get-tuple-element.14), channel_id=1, source_target_pairs={{0,1},{1,0},{2,3},{3,2},{4,5},{5,4},{6,7},{7,6},{8,9},{9,8},{10,11... | collective-permute-start | bytes 61448 | tf_op jit(solution)/shard_map/ppermute | solution.py:488
  11.5 8.5 %copy-start.1 = (bf16[191,576]{1,0:T(8,128)(2,1)S(1)}, bf16[191,576]{1,0:T(8,128)(2,1)}, u32[]{:S(2)}) copy-start(bf16[191,576]{1,0:T(8,128)(2,1)} %inverse.1) | copy-start | bytes 660100
  11.5 9.3 %copy-start = (bf16[640,256]{1,0:T(8,128)(2,1)S(1)}, bf16[640,256]{1,0:T(8,128)(2,1)}, u32[]{:S(2)}) copy-start(bf16[640,256]{1,0:T(8,128)(2,1)} %constant.74.matrix) | copy-start | bytes 983044
  11.6 9.3 %copy-start.2 = (f32[2,448]{1,0:T(2,128)S(1)}, f32[2,448]{1,0:T(2,128)}, u32[]{:S(2)}) copy-start(f32[2,448]{1,0:T(2,128)} %constant.51.clone.names) | copy-start | bytes 10756
  11.6 9.2 %copy-start.7 = (s32[2,56]{1,0:T(2,128)S(1)}, s32[2,56]{1,0:T(2,128)}, u32[]{:S(2)}) copy-start(s32[2,56]{1,0:T(2,128)} %constant.50.clone.pairs) | copy-start | bytes 1348
  11.6 9.2 %copy-start.8 = (s32[1,16,1]{1,2,0:T(1,128)S(1)}, s32[1,16,1]{1,2,0:T(1,128)}, u32[]{:S(2)}) copy-start(s32[1,16,1]{1,2,0:T(1,128)} %param.21) | copy-start | bytes 196
  11.6 9.2 %copy-start.9 = (s32[1,16]{1,0:T(1,128)S(1)}, s32[1,16]{1,0:T(1,128)}, u32[]{:S(2)}) copy-start(s32[1,16]{1,0:T(1,128)} %cells.1) | copy-start | bytes 196
  14.7 12.1 %collective-permute-start.3 = (bf16[256,640]{1,0:T(8,128)(2,1)S(1)}, bf16[256,640]{1,0:T(8,128)(2,1)S(1)}, u32[]{:S(2)}, u32[]{:S(2)}) collective-permute-start(bf16[256,640]{1,0:T(8,128)(2,1)S(1)} %get-tuple-element.17.edge0), channel_id=1, source_target_pairs={{32,0},{64,32},{96,64},{128,96},{160,128},{192,160},{224,192},{256... | collective-permute-start | bytes 983048 | tf_op jit(solution)/shard_map/ppermute | solution.py:509
  16.0 12.5 %collective-permute-start.2 = (bf16[256,640]{1,0:T(8,128)(2,1)S(1)}, bf16[256,640]{1,0:T(8,128)(2,1)S(1)}, u32[]{:S(2)}, u32[]{:S(2)}) collective-permute-start(bf16[256,640]{1,0:T(8,128)(2,1)S(1)} %get-tuple-element.16.edge1), channel_id=1, source_target_pairs={{0,32},{32,64},{64,96},{96,128},{128,160},{160,192},{192,224},{224... | collective-permute-start | bytes 983048 | tf_op jit(solution)/shard_map/ppermute | solution.py:510
  20.7 6.1 %copy-start.3 = (s32[2,16]{1,0:T(2,128)S(1)}, s32[2,16]{1,0:T(2,128)}, u32[]{:S(2)}) copy-start(s32[2,16]{1,0:T(2,128)} %constant.52.clone.pairs) | copy-start | bytes 388
  20.7 6.1 %copy-start.4 = (f32[2,128]{1,0:T(2,128)S(1)}, f32[2,128]{1,0:T(2,128)}, u32[]{:S(2)}) copy-start(f32[2,128]{1,0:T(2,128)} %constant.53.clone.names) | copy-start | bytes 3076
  26.8 1.7 %copy-start.5 = (s32[2,8]{1,0:T(2,128)S(1)}, s32[2,8]{1,0:T(2,128)}, u32[]{:S(2)}) copy-start(s32[2,8]{1,0:T(2,128)} %constant.54.clone.pairs) | copy-start | bytes 196
  26.8 1.7 %copy-start.6 = (f32[2,64]{1,0:T(2,128)S(1)}, f32[2,64]{1,0:T(2,128)}, u32[]{:S(2)}) copy-start(f32[2,64]{1,0:T(2,128)} %constant.55.clone.names) | copy-start | bytes 1540

commit v14 on v13

--- a/solution.py
+++ b/solution.py
@@ -298,17 +298,7 @@
     phase_out[...] = jnp.where(lines == 47, placed[1:2, :], phases)
 
 
-def weights_kernel(inverse, weight_out, gather):
-    spots = iota((1, weight_out.shape[1]), 1)
-    group, k = spots // PAIR_ROWS, spots % PAIR_ROWS
-    target = jnp.where(k < 36, 36 * group + k, jnp.where(k < 45, 36 * group + k - 45, -1))
-
-    def one_rows(n, _):
-        at = pl.multiple_of(n * 16, 16)
-        gather[pl.ds(at, 16), :] = (iota((16, gather.shape[1]), 0) + at == target).astype(BF16)
-        return 0
-
-    lax.fori_loop(0, gather.shape[0] // 16, one_rows, 0, unroll=4)
+def weights_kernel(inverse, gather, weight_out):
     weight_out[0:191, :] = jnp.dot(
         inverse[...], gather[...], preferred_element_type=F32
     ).astype(BF16)
@@ -487,12 +477,15 @@
     own = lax.reduce_precision(slc_stack, 8, 7)
     near = lax.ppermute(tile0, "col", swaps(strips, 0))
     far = lax.ppermute(tile1, "col", swaps(strips, 1))
+    spots = np.arange(groups * PAIR_ROWS)
+    of, k = spots // PAIR_ROWS, spots % PAIR_ROWS
+    target = np.where(k < 36, 36 * of + k, np.where(k < 36 + EXTRA, 36 * of + k - 45, -1))
+    gather = np.arange(inverse.shape[1])[:, None] == target[None, :]
     (weight,) = call(
         weights_kernel,
         (),
-        (inverse,),
+        (inverse, jnp.asarray(gather.astype(np.float32)).astype(BF16)),
         [((DATES, groups * PAIR_ROWS), BF16)],
-        [pltpu.VMEM((inverse.shape[1], groups * PAIR_ROWS), BF16)],
     )
     scratch = [
         pltpu.VMEM((2, 2 * ROWS * width // LANES, 2 * LANES), BF16),

time: 78 us -> 77.8 us (level)
  transfers between devices with their start and end apart: 4 -> 4, of which waited for: 1 -> 1; matrix products, arithmetic and copies ran while one was open for 1% -> 1% of each run, Pallas kernels for 11% -> 10%
where the time goes in v14:
time: 77.8 us; the launch traced here: 77.5 us
  blocking collectives  45.9 us (59%)
  Pallas kernels  15.7 us (20%)
  starting transfers between devices  14.7 us (19%)
    all_to_all x1, blocking collectives, local(): parts = lax.all_to_all(routed, 'col', 0, 0, tiled=True)  31.4 us
    all_to_all x1, blocking collectives, local(): phases = lax.all_to_all(sent, 'date', 0, 0, tiled=True)  14.5 us
    pallas_call x7, Pallas kernels, call(): pl.pallas_call(kernel, in_specs=[SMEM] * len(smem) + [VMEM] * len(vmem),...  14.1 us
    ppermute x1, starting transfers between devices, local(): far = lax.ppermute(tile1, 'col', swaps(strips, 1))  4.94 us
    ppermute x1, starting transfers between devices, local(): near = lax.ppermute(tile0, 'col', swaps(strips, 0))  4.5 us
    ppermute x1, starting transfers between devices, local(): lax.ppermute(edge1, 'date', [(i, i + 1) for i in range(groups - 1)])  4.01 us
  transfers between devices with their start and end apart: 4, of which 1 were waited for; matrix products, arithmetic and copies ran while one was open for 1% of the time, Pallas kernels for 10%

profile of v14, /device:TPU:1, one launch (start us, length us, event | category | flops | bytes accessed | tf_op | source)
XLA Modules:
  0.0 77.5 jit_solution(16880006147115652024)
XLA Ops:
  0.0 1.5 %shard_map.154 = (bf16[2,40,128]{2,1,0:T(8,128)(2,1)S(1)}, bf16[2,48,128]{2,1,0:T(8,128)(2,1)S(1)}) custom-call(s32[1]{0:T(128)} %bitcast.11.odd, bf16[2,12,40,640]{3,2,1,0:T(8,128)(2,1)} %own.1), custom_call_target="tpu_custom_call" | custom-call | tf_op jit(solution)/shard_map/pallas_call | solution.py:466
  1.6 4.9 %collective-permute-start.1 = (bf16[2,48,128]{2,1,0:T(8,128)(2,1)S(1)}, bf16[2,48,128]{2,1,0:T(8,128)(2,1)S(1)}, u32[]{:S(2)}, u32[]{:S(2)}) collective-permute-start(bf16[2,48,128]{2,1,0:T(8,128)(2,1)S(1)} %get-tuple-element.15), channel_id=1, source_target_pairs={{1,2},{2,1},{3,4},{4,3},{5,6},{6,5},{7,8},{8,7},{9,10},{10,9},{11,... | collective-permute-start | bytes 73736 | tf_op jit(solution)/shard_map/ppermute | solution.py:479
  6.5 4.5 %collective-permute-start = (bf16[2,40,128]{2,1,0:T(8,128)(2,1)S(1)}, bf16[2,40,128]{2,1,0:T(8,128)(2,1)S(1)}, u32[]{:S(2)}, u32[]{:S(2)}) collective-permute-start(bf16[2,40,128]{2,1,0:T(8,128)(2,1)S(1)} %get-tuple-element.14), channel_id=1, source_target_pairs={{0,1},{1,0},{2,3},{3,2},{4,5},{5,4},{6,7},{7,6},{8,9},{9,8},{10,11... | collective-permute-start | bytes 61448 | tf_op jit(solution)/shard_map/ppermute | solution.py:478
  11.1 0.1 add_convert_fusion.1
  11.2 0.1 pad.36
  11.3 0.1 fusion.lines
  11.3 0.1 constant_dynamic-slice_fusion.table
  11.4 0.1 reduce_precision.3.own
  11.5 0.0 copy-start.1
  11.5 0.0 copy-start
  11.6 0.0 copy-start.3
  11.6 0.3 collective-permute-done.near
  11.9 2.9 %shard_map.155 = (bf16[256,640]{1,0:T(8,128)(2,1)S(1)}, bf16[256,640]{1,0:T(8,128)(2,1)S(1)}) custom-call(f32[24,12]{1,0:T(8,128)S(1)} %constant_dynamic-slice_fusion.table, bf16[2,12,40,640]{3,2,1,0:T(8,128)(2,1)S(1)} %reduce_precision.3.own, bf16[2,40,128]{2,1,0:T(8,128)(2,1)S(1)} %collective-permute-done.near, ...), custom_call_target="tpu_custom_call" | custom-call | tf_op jit(solution)/shard_map/pallas_call | solution.py:418
  14.7 1.3 %collective-permute-start.3 = (bf16[256,640]{1,0:T(8,128)(2,1)S(1)}, bf16[256,640]{1,0:T(8,128)(2,1)S(1)}, u32[]{:S(2)}, u32[]{:S(2)}) collective-permute-start(bf16[256,640]{1,0:T(8,128)(2,1)S(1)} %get-tuple-element.17.edge0), channel_id=1, source_target_pairs={{32,0},{64,32},{96,64},{128,96},{160,128},{192,160},{224,192},{256... | collective-permute-start | bytes 983048 | tf_op jit(solution)/shard_map/ppermute | solution.py:502
  16.0 4.0 %collective-permute-start.2 = (bf16[256,640]{1,0:T(8,128)(2,1)S(1)}, bf16[256,640]{1,0:T(8,128)(2,1)S(1)}, u32[]{:S(2)}, u32[]{:S(2)}) collective-permute-start(bf16[256,640]{1,0:T(8,128)(2,1)S(1)} %get-tuple-element.16.edge1), channel_id=1, source_target_pairs={{0,32},{32,64},{64,96},{96,128},{128,160},{160,192},{192,224},{224... | collective-permute-start | bytes 983048 | tf_op jit(solution)/shard_map/ppermute | solution.py:503
  20.1 0.4 shard_map.157.weight
  20.5 0.1 add_convert_fusion.facts.table
  20.6 5.9 %shard_map.156 = (f32[48,256]{1,0:T(8,128)S(1)}, f32[96,256]{1,0:T(8,128)S(1)}, f32[12,2,40,640]{3,2,1,0:T(8,128)S(1)}) custom-call(f32[24,12]{1,0:T(8,128)S(1)} %constant_dynamic-slice_fusion.table, s32[2,56]{1,0:T(2,128)S(1)} %copy-done.8, bf16[2,12,40,640]{3,2,1,0:T(8,128)(2,1)S(1)} %reduce_precision.3.own, ...), custom_call_target="tpu_custom_call" | custom-call | tf_op jit(solution)/shard_map/pallas_call | solution.py:418
  26.6 1.7 %shard_map.158.phase = f32[48,256]{1,0:T(8,128)S(1)} custom-call(f32[1,4]{1,0:T(1,128)S(1)} %add_convert_fusion.facts.table, s32[2,16]{1,0:T(2,128)S(1)} %copy-done.4, bf16[256,640]{1,0:T(8,128)(2,1)S(1)} %collective-permute-done.3.got, f32[12,2,40,640]{3,2,1,0:T(8,128)S(1)} %get-tuple-element.18.ys, f32[96,256]{1,0:T(8,128)S(1)} %get-tuple-element.19.power, ...), custom_call_target="tpu_custom_call" | custom-call | tf_op jit(solution)/shard_map/pallas_call | solution.py:418
  28.4 1.3 %shard_map.159 = bf16[16,48,256]{2,1,0:T(8,128)(2,1)S(1)} custom-call(s32[2,8]{1,0:T(2,128)S(1)} %copy-done.6, bf16[256,640]{1,0:T(8,128)(2,1)S(1)} %collective-permute-done.2.got, f32[12,2,40,640]{3,2,1,0:T(8,128)S(1)} %get-tuple-element.18.ys, f32[96,256]{1,0:T(8,128)S(1)} %get-tuple-element.19.power, f32[48,256]{1,0:T(8,128)S(1)} %shard_map.158.phase, ...), custom_call_target="tpu_custom_call" | custom-call | tf_op jit(solution)/shard_map/pallas_call | solution.py:418
  29.6 14.5 %all_to_all.10.got = bf16[16,48,256]{2,1,0:T(8,128)(2,1)S(1)} all-to-all(bf16[16,48,256]{2,1,0:T(8,128)(2,1)S(1)} %shard_map.159), channel_id=1, replica_groups=mesh['date'=16,'col'=32] {'date'}, dimensions={0} | all-to-all | bytes 786432 | tf_op jit(solution)/shard_map/all_to_all | solution.py:558
  44.1 1.2 %shard_map.160 = bf16[32,4,384]{2,1,0:T(4,128)(2,1)S(1)} custom-call(f32[1,4]{1,0:T(1,128)S(1)} %add_convert_fusion.facts.table, bf16[16,48,256]{2,1,0:T(8,128)(2,1)S(1)} %all_to_all.10.got, bf16[192,768]{1,0:T(8,128)(2,1)S(1)} %shard_map.157.weight), custom_call_target="tpu_custom_call" | custom-call | tf_op jit(solution)/shard_map/pallas_call | solution.py:418
  45.3 31.4 %all_to_all.11.got = bf16[32,4,384]{2,1,0:T(4,128)(2,1)S(1)} all-to-all(bf16[32,4,384]{2,1,0:T(4,128)(2,1)S(1)} %shard_map.160), channel_id=1, replica_groups=mesh['date'=16,'col'=32] {'col'}, dimensions={0} | all-to-all | bytes 196608 | tf_op jit(solution)/shard_map/all_to_all | solution.py:566
  76.7 0.8 %shard_map.161 = f32[8,192]{1,0:T(8,128)} custom-call(bf16[32,4,384]{2,1,0:T(4,128)(2,1)S(1)} %all_to_all.11.got, f32[24,192]{1,0:T(8,128)S(1)} %fusion.lines), custom_call_target="tpu_custom_call" | custom-call | tf_op jit(solution)/shard_map/pallas_call | solution.py:418
  (34 shorter events, 0.1 us)
Async XLA Ops:
  0.0 11.4 %copy-start.11 = (bf16[2,12,40,640]{3,2,1,0:T(8,128)(2,1)S(1)}, bf16[2,12,40,640]{3,2,1,0:T(8,128)(2,1)}, u32[]{:S(2)}) copy-start(bf16[2,12,40,640]{3,2,1,0:T(8,128)(2,1)} %own.1) | copy-start | bytes 3686404
  0.0 11.0 %copy-start.13 = (s32[192,2]{0,1:T(2,128)S(1)}, s32[192,2]{0,1:T(2,128)}, u32[]{:S(2)}) copy-start(s32[192,2]{0,1:T(2,128)} %param.17) | copy-start | bytes 4612
  0.0 11.1 %copy-start.15 = (s32[36]{0:T(128)S(1)}, s32[36]{0:T(128)}, u32[]{:S(2)}) copy-start(s32[36]{0:T(128)} %param.19) | copy-start | bytes 436
  0.0 11.2 %copy-start.12 = (f32[192,2,8]{0,2,1:T(8,128)S(1)}, f32[192,2,8]{0,2,1:T(8,128)}, u32[]{:S(2)}) copy-start(f32[192,2,8]{0,2,1:T(8,128)} %param.18) | copy-start | bytes 36868
  0.0 11.2 %copy-start.14 = (f32[191]{0:T(256)S(1)}, f32[191]{0:T(256)}, u32[]{:S(2)}) copy-start(f32[191]{0:T(256)} %param.21) | copy-start | bytes 2296
  1.6 10.3 %collective-permute-start.1 = (bf16[2,48,128]{2,1,0:T(8,128)(2,1)S(1)}, bf16[2,48,128]{2,1,0:T(8,128)(2,1)S(1)}, u32[]{:S(2)}, u32[]{:S(2)}) collective-permute-start(bf16[2,48,128]{2,1,0:T(8,128)(2,1)S(1)} %get-tuple-element.15), channel_id=1, source_target_pairs={{1,2},{2,1},{3,4},{4,3},{5,6},{6,5},{7,8},{8,7},{9,10},{10,9},{11,... | collective-permute-start | bytes 73736 | tf_op jit(solution)/shard_map/ppermute | solution.py:479
  6.5 5.3 %collective-permute-start = (bf16[2,40,128]{2,1,0:T(8,128)(2,1)S(1)}, bf16[2,40,128]{2,1,0:T(8,128)(2,1)S(1)}, u32[]{:S(2)}, u32[]{:S(2)}) collective-permute-start(bf16[2,40,128]{2,1,0:T(8,128)(2,1)S(1)} %get-tuple-element.14), channel_id=1, source_target_pairs={{0,1},{1,0},{2,3},{3,2},{4,5},{5,4},{6,7},{7,6},{8,9},{9,8},{10,11... | collective-permute-start | bytes 61448 | tf_op jit(solution)/shard_map/ppermute | solution.py:478
  11.4 8.6 %copy-start.2 = (bf16[191,576]{1,0:T(8,128)(2,1)S(1)}, bf16[191,576]{1,0:T(8,128)(2,1)}, u32[]{:S(2)}) copy-start(bf16[191,576]{1,0:T(8,128)(2,1)} %inverse.1) | copy-start | bytes 660100
  11.5 8.5 %copy-start.1 = (bf16[576,768]{1,0:T(8,128)(2,1)S(1)}, bf16[576,768]{1,0:T(8,128)(2,1)}, u32[]{:S(2)}) copy-start(bf16[576,768]{1,0:T(8,128)(2,1)} %constant.78.gather) | copy-start | bytes 2654212
  11.5 9.0 %copy-start = (bf16[640,256]{1,0:T(8,128)(2,1)S(1)}, bf16[640,256]{1,0:T(8,128)(2,1)}, u32[]{:S(2)}) copy-start(bf16[640,256]{1,0:T(8,128)(2,1)} %constant.77.matrix) | copy-start | bytes 983044
  11.6 9.0 %copy-start.3 = (f32[2,448]{1,0:T(2,128)S(1)}, f32[2,448]{1,0:T(2,128)}, u32[]{:S(2)}) copy-start(f32[2,448]{1,0:T(2,128)} %constant.54.clone.names) | copy-start | bytes 10756
  11.6 9.0 %copy-start.8 = (s32[2,56]{1,0:T(2,128)S(1)}, s32[2,56]{1,0:T(2,128)}, u32[]{:S(2)}) copy-start(s32[2,56]{1,0:T(2,128)} %constant.53.clone.pairs) | copy-start | bytes 1348
  11.6 9.0 %copy-start.9 = (s32[1,16,1]{1,2,0:T(1,128)S(1)}, s32[1,16,1]{1,2,0:T(1,128)}, u32[]{:S(2)}) copy-start(s32[1,16,1]{1,2,0:T(1,128)} %param.22) | copy-start | bytes 196
  11.6 9.0 %copy-start.10 = (s32[1,16]{1,0:T(1,128)S(1)}, s32[1,16]{1,0:T(1,128)}, u32[]{:S(2)}) copy-start(s32[1,16]{1,0:T(1,128)} %cells.1) | copy-start | bytes 196
  14.7 11.8 %collective-permute-start.3 = (bf16[256,640]{1,0:T(8,128)(2,1)S(1)}, bf16[256,640]{1,0:T(8,128)(2,1)S(1)}, u32[]{:S(2)}, u32[]{:S(2)}) collective-permute-start(bf16[256,640]{1,0:T(8,128)(2,1)S(1)} %get-tuple-element.17.edge0), channel_id=1, source_target_pairs={{32,0},{64,32},{96,64},{128,96},{160,128},{192,160},{224,192},{256... | collective-permute-start | bytes 983048 | tf_op jit(solution)/shard_map/ppermute | solution.py:502
  16.0 12.3 %collective-permute-start.2 = (bf16[256,640]{1,0:T(8,128)(2,1)S(1)}, bf16[256,640]{1,0:T(8,128)(2,1)S(1)}, u32[]{:S(2)}, u32[]{:S(2)}) collective-permute-start(bf16[256,640]{1,0:T(8,128)(2,1)S(1)} %get-tuple-element.16.edge1), channel_id=1, source_target_pairs={{0,32},{32,64},{64,96},{96,128},{128,160},{160,192},{192,224},{224... | collective-permute-start | bytes 983048 | tf_op jit(solution)/shard_map/ppermute | solution.py:503
  20.5 6.1 %copy-start.4 = (s32[2,16]{1,0:T(2,128)S(1)}, s32[2,16]{1,0:T(2,128)}, u32[]{:S(2)}) copy-start(s32[2,16]{1,0:T(2,128)} %constant.55.clone.pairs) | copy-start | bytes 388
  20.5 6.1 %copy-start.5 = (f32[2,128]{1,0:T(2,128)S(1)}, f32[2,128]{1,0:T(2,128)}, u32[]{:S(2)}) copy-start(f32[2,128]{1,0:T(2,128)} %constant.56.clone.names) | copy-start | bytes 3076
  26.6 1.7 %copy-start.6 = (s32[2,8]{1,0:T(2,128)S(1)}, s32[2,8]{1,0:T(2,128)}, u32[]{:S(2)}) copy-start(s32[2,8]{1,0:T(2,128)} %constant.57.clone.pairs) | copy-start | bytes 196
  26.6 1.7 %copy-start.7 = (f32[2,64]{1,0:T(2,128)S(1)}, f32[2,64]{1,0:T(2,128)}, u32[]{:S(2)}) copy-start(f32[2,64]{1,0:T(2,128)} %constant.58.clone.names) | copy-start | bytes 1540
